TPU v7x, 32 devices: a whole 2x2x4 slice. The times are simulated.
32 devices in a mesh: cells: 16 (over z, y, core), lanes: 2 (over x).
Axes of the slice: x: 2, y: 2, z: 4, core: 2. Of those that a mesh axis runs over, the one named last changes fastest.
Arguments:
- centres: float32 [3, 16384], P(None, 'cells'), may hold values from 0 to 4
- seg_lines: float32 [3, 16384], P(None, 'cells'), may hold values from -3 to 3
- burgers: float32 [3, 16384], P(None, 'cells'), may hold values from -6 to 6
- neighbour_blocks: int32 [128, 16], P('cells', 'lanes'), may hold values from 0 to 39
- seg_nodes: int32 [2, 16384], P(None, 'cells'), may hold values from 0 to 1023
- node_owner: int32 [2, 16384], P(None, 'cells'), may hold values from 0 to 1
- mobility: float32 [16384], P('cells'), may hold values from 0.5 to 4
- cand_target: int32 [512], P('cells'), may hold values from 0 to 7
- cand_source: int32 [512], P('cells'), may hold values from 0 to 39
Outputs:
- node_velocity: float32 [3, 16384], P(None, 'cells')
- nearness: float32 [16384], P('cells')
All inputs are finite; a program needn't handle non-finite values.
Results may differ from a plain program's by a relative error of at most 0.0003.
Values sent between devices are 32-bit elements; how exact they have to be, the bound alone decides.
No kernel may reach another device: no remote copies, remote signals or barrier semaphores. Data moves between devices by JAX's collectives and lax.ppermute only.
A program may use at most 64 MiB of HBM per device.

v0:
```python
import jax
import jax.numpy as jnp
from jax import lax
from jax.sharding import PartitionSpec as P

BLK = 128
REACH = 2


FORCE_SCALE = 0.02
CORE_SQUARE = 0.25
TIME_STEP = 4.0
HIGH = lax.Precision.HIGHEST


def passed_along(block, axis, distance):
    devices = range(lax.axis_size(axis))
    route = [((i - distance) % len(devices), i) for i in devices]
    return lax.ppermute(block, axis, route)


def cross_product(first, second):
    return jnp.stack(
        [
            first[1] * second[2] - first[2] * second[1],
            first[2] * second[0] - first[0] * second[2],
            first[0] * second[1] - first[1] * second[0],
        ]
    )


def tile_forces(own_blocks, source_blocks):
    target_centre = own_blocks[0:3]
    target_line = own_blocks[3:6]
    source_centre = source_blocks[0:3]
    source_line = source_blocks[3:6]
    source_burgers = source_blocks[6:9]
    along = jnp.einsum("ckj,cki->kij", source_burgers, target_line, precision=HIGH)
    separation = target_centre[:, :, :, None] - source_centre[:, :, None, :]
    square = jnp.sum(separation * separation, axis=0) + CORE_SQUARE
    inverse = lax.rsqrt(square)
    weight = along * inverse * inverse * inverse
    summed_line = jnp.einsum("kij,ckj->cki", weight, source_line, precision=HIGH)
    summed_moment = jnp.einsum(
        "kij,ckj->cki", weight, cross_product(source_line, source_centre), precision=HIGH
    )
    return FORCE_SCALE * (cross_product(summed_line, target_centre) - summed_moment)


def block_forces(own_blocks, window_blocks, block_lists):

    def add_entry(summed, column):
        chosen = jnp.take(window_blocks, column, axis=1)
        return (summed + tile_forces(own_blocks, chosen), None)

    initial = jnp.zeros((3,) + own_blocks.shape[1:], jnp.float32)
    summed, unused = lax.scan(add_entry, initial, jnp.transpose(block_lists))
    return summed


def swept_tiles(own_blocks, window_blocks, targets, sources):
    target_side = jnp.take(own_blocks, targets, axis=1)
    source_side = jnp.take(window_blocks, sources, axis=1)
    separation = target_side[0:3, :, :, None] - source_side[0:3, :, None, :]
    motion = TIME_STEP * (target_side[3:6, :, :, None] - source_side[3:6, :, None, :])
    approach = jnp.sum(separation * motion, axis=0)
    motion_square = jnp.sum(motion * motion, axis=0)
    fraction = jnp.clip(-approach / (motion_square + CORE_SQUARE), 0.0, 1.0)
    closest = separation + fraction[None] * motion
    distance = jnp.sum(closest * closest, axis=0)
    summed = jnp.sum(jnp.exp(-distance), axis=2)
    selector = (
        targets[:, None] == jnp.arange(own_blocks.shape[1], dtype=jnp.int32)[None, :]
    ).astype(jnp.float32)
    return jnp.einsum("nk,nb->kb", selector, summed, precision=HIGH)


def deposit(deposits, node_ids, keep_mask, node_count):
    masked = deposits * keep_mask.astype(jnp.float32)[None, :]
    return jnp.transpose(
        jax.ops.segment_sum(jnp.transpose(masked), node_ids, num_segments=node_count)
    )


def end_velocity(velocity, next_velocity, node_ids, owner_map):
    return jnp.where(
        owner_map[None, :] == 0,
        jnp.take(velocity, node_ids, axis=1),
        jnp.take(next_velocity, node_ids, axis=1),
    )


def local(
    centres,
    seg_lines,
    burgers,
    neighbour_blocks,
    seg_nodes,
    node_owner,
    mobility,
    cand_target,
    cand_source,
):
    seg_count = centres.shape[1]
    block_count = seg_count // BLK
    offsets = [shift_size for shift_size in range(-REACH, REACH + 1) if shift_size != 0]
    own_fields = jnp.concatenate([centres, seg_lines, burgers], 0)
    fetched = [passed_along(own_fields, "cells", -offset) for offset in offsets]
    window = jnp.concatenate(fetched[:REACH] + [own_fields] + fetched[REACH:], 1)
    own_blocks = own_fields.reshape(9, block_count, BLK)
    window_blocks = window.reshape(9, -1, BLK)
    partial_value = block_forces(own_blocks, window_blocks, neighbour_blocks).reshape(3, seg_count)
    forces = lax.psum(partial_value, "lanes")
    lengths = jnp.sqrt(jnp.sum(seg_lines * seg_lines, axis=0))
    deposits = jnp.concatenate([0.5 * forces, 0.5 * lengths[None, :]], 0)
    node_count = mobility.shape[0]
    own_part = deposit(deposits, seg_nodes[0], node_owner[0] == 0, node_count) + deposit(
        deposits, seg_nodes[1], node_owner[1] == 0, node_count
    )
    next_part = deposit(deposits, seg_nodes[0], node_owner[0] == 1, node_count) + deposit(
        deposits, seg_nodes[1], node_owner[1] == 1, node_count
    )
    received = passed_along(next_part, "cells", 1)
    totals = own_part + received
    velocity = mobility[None, :] * totals[0:3] / (1.0 + totals[3:4])
    next_velocity = passed_along(velocity, "cells", -1)
    seg_velocity = 0.5 * (
        end_velocity(velocity, next_velocity, seg_nodes[0], node_owner[0])
        + end_velocity(velocity, next_velocity, seg_nodes[1], node_owner[1])
    )
    moved = [passed_along(seg_velocity, "cells", -offset) for offset in offsets]
    window_velocity = jnp.concatenate(moved[:REACH] + [seg_velocity] + moved[REACH:], 1)
    window_motion = jnp.concatenate([window[0:3], window_velocity], 0).reshape(6, -1, BLK)
    own_motion = jnp.concatenate([centres, seg_velocity], 0).reshape(6, block_count, BLK)
    tile_count = cand_target.shape[0] // lax.axis_size("lanes")
    beginning = lax.axis_index("lanes") * tile_count
    local_near = swept_tiles(
        own_motion,
        window_motion,
        lax.dynamic_slice_in_dim(cand_target, beginning, tile_count),
        lax.dynamic_slice_in_dim(cand_source, beginning, tile_count),
    )
    nearness = lax.psum(local_near, "lanes")
    return (velocity, nearness.reshape(seg_count))


def solution(mesh):
    in_specs = (
        P(None, "cells"),
        P(None, "cells"),
        P(None, "cells"),
        P("cells", "lanes"),
        P(None, "cells"),
        P(None, "cells"),
        P("cells"),
        P("cells"),
        P("cells"),
    )
    out_specs = (P(None, "cells"), P("cells"))
    return jax.shard_map(local, mesh=mesh, in_specs=in_specs, out_specs=out_specs, check_vma=False)
```

profile of v0, /device:TPU:29, one launch (start us, length us, event | category | flops | bytes accessed | tf_op | source)
XLA Modules:
  0.0 150.9 jit_solution(16045853036463992818)
XLA Ops:
  0.6 0.8 pad_maximum_fusion
  1.7 1.0 collective-permute-start.2
  2.6 3.8 %collective-permute-start.1 = (f32[9,1024]{1,0:T(8,128)S(1)}, f32[9,1024]{1,0:T(8,128)S(1)}, u32[]{:S(2)}, u32[]{:S(2)}) collective-permute-start(f32[9,1024]{1,0:T(8,128)S(1)} %pad_maximum_fusion), channel_id=1, source_target_pairs={{30,0},{0,2},{2,4},{4,6},{6,8},{8,10},{10,12},{12,14},{14,16},{16,... | collective-permute-start | bytes 110600 | tf_op jit(solution)/shard_map/ppermute | solution.py:19
  6.5 0.9 collective-permute-start
  7.4 0.7 multiply_reduce_fusion.1
  8.1 0.8 fusion.38
  8.9 0.8 compare_reduce_fusion
  9.8 0.7 compare_and_fusion.4
  10.5 0.8 copy.95
  11.4 0.8 constant_dynamic-update-slice_fusion.2
  12.3 28.7 %while.11 = (s32[]{:T(128)}, f32[3,8,128]{2,0,1:T(4,128)S(1)}, s32[8,8]{1,0:T(8,128)S(1)}, f32[9,40,128]{2,0,1:T(8,128)S(1)}, f32[9,8,128]{2,0,1:T(8,128)S(1)}, /*index=5*/s32[]{:T(128)}, s32[]{:T(128)}) while((s32[]{:T(128)}, f32[3,8,128]{2,0,1:T(4,128)S(1)}, s32[8,8]{1,0:T(8,128)S(1)}, f32[9,40,128]{2,0,1:T(8,128)S(1)}, ...), condition=%wide.region_2.3_spmd.clone, body=%wide.region_0.2_spmd.clone.sunk | while | flops 15781963 | bytes 4129047 | solution.py:57
  12.4 0.6 gather_fusion
  13.8 1.0 fusion.58
  16.0 0.6 gather_fusion
  17.4 1.0 fusion.58
  19.6 0.6 gather_fusion
  21.0 1.0 fusion.58
  23.2 0.6 gather_fusion
  24.6 1.0 fusion.58
  26.8 0.6 gather_fusion
  28.2 1.0 fusion.58
  30.4 0.6 gather_fusion
  31.7 1.0 fusion.58
  34.0 0.6 gather_fusion
  35.3 1.0 fusion.58
  37.5 0.6 gather_fusion
  38.9 1.0 fusion.58
  41.3 16.7 %psum.14 = f32[3,1024]{0,1:T(8,128)S(1)} all-reduce(f32[3,1024]{0,1:T(8,128)S(1)} %bitcast.96), channel_id=1, replica_groups=mesh['cells'=16,'lanes'=2] {'lanes'}, use_global_device_ids=true, to_apply=%region_3.4 | all-reduce | flops 3072 | bytes 24576 | tf_op jit(solution)/shard_map/psum | solution.py:113
  58.7 6.2 %scatter_custom_fusion.2 = f32[1024,4]{1,0:T(8,128)S(1)} fusion(s32[1024]{0:T(1024)S(1)} %bitcast.103, f32[1024,4]{1,0:T(8,128)S(1)} %copy.102, f32[]{:T(128)} %constant.45.clone.1), kind=kCustom, calls=%fused_computation.68 | custom fusion | flops 4096 | bytes 16388 | tf_op jit(solution)/shard_map/scatter-add | solution.py:81
  64.9 6.1 %scatter_custom_fusion.3 = f32[1024,4]{1,0:T(8,128)S(1)} fusion(s32[1024]{0:T(1024)S(1)} %bitcast.107, f32[1024,4]{1,0:T(8,128)S(1)} %copy.103, f32[]{:T(128)} %constant.45.clone.1), kind=kCustom, calls=%fused_computation.66 | custom fusion | flops 4096 | bytes 16388 | tf_op jit(solution)/shard_map/scatter-add | solution.py:81
  71.1 3.5 %collective-permute-start.4 = (f32[4,1024]{0,1:T(8,128)S(1)}, f32[4,1024]{0,1:T(8,128)S(1)}, u32[]{:S(2)}, u32[]{:S(2)}) collective-permute-start(f32[4,1024]{0,1:T(8,128)S(1)} %add_bitcast_fusion), channel_id=1, source_target_pairs={{30,0},{0,2},{2,4},{4,6},{6,8},{8,10},{10,12},{12,14},{14,16},{16,... | collective-permute-start | bytes 49160 | tf_op jit(solution)/shard_map/ppermute | solution.py:19
  74.9 6.3 %scatter_custom_fusion.1 = f32[1024,4]{1,0:T(8,128)S(1)} fusion(s32[1024]{0:T(1024)S(1)} %bitcast.108, f32[1024,4]{1,0:T(8,128)S(1)} %copy.101, f32[]{:T(128)} %constant.45.clone.1), kind=kCustom, calls=%fused_computation.70 | custom fusion | flops 4096 | bytes 16388 | tf_op jit(solution)/shard_map/scatter-add | solution.py:81
  81.5 6.2 %scatter_custom_fusion = f32[1024,4]{1,0:T(8,128)S(1)} fusion(s32[1024]{0:T(1024)S(1)} %bitcast.104, f32[1024,4]{1,0:T(8,128)S(1)} %copy.100, f32[]{:T(128)} %constant.45.clone.1), kind=kCustom, calls=%fused_computation.72 | custom fusion | flops 4096 | bytes 16388 | tf_op jit(solution)/shard_map/scatter-add | solution.py:81
  88.8 0.8 copy.114
  89.6 2.8 %gather_fusion.5 = f32[1024,3]{1,0:T(8,128)S(1)} fusion(f32[3,1024]{0,1:T(8,128)S(1)} %fusion.22, s32[1024]{0:T(1024)S(1)} %get-tuple-element.123), kind=kCustom, calls=%fused_computation.3.clone | custom fusion | bytes 28672 | tf_op jit(solution)/shard_map/jit(_take)/gather | solution.py:88
  92.4 2.8 %gather_fusion.3 = f32[1024,3]{1,0:T(8,128)S(1)} fusion(f32[3,1024]{0,1:T(8,128)S(1)} %fusion.22, s32[1024]{0:T(1024)S(1)} %get-tuple-element.122), kind=kCustom, calls=%fused_computation.1.clone | custom fusion | bytes 28672 | tf_op jit(solution)/shard_map/jit(_take)/gather | solution.py:88
  95.2 4.8 %collective-permute-done.5 = f32[3,1024]{0,1:T(8,128)S(1)} collective-permute-done((f32[3,1024]{0,1:T(8,128)S(1)}, f32[3,1024]{0,1:T(8,128)S(1)}, u32[]{:S(2)}, u32[]{:S(2)}) %collective-permute-start.5) | collective-permute-done | bytes 12320 | tf_op jit(solution)/shard_map/ppermute | solution.py:19
  100.0 2.8 %gather_fusion.6 = f32[1024,3]{1,0:T(8,128)S(1)} fusion(f32[3,1024]{0,1:T(8,128)S(1)} %collective-permute-done.5, s32[1024]{0:T(1024)S(1)} %get-tuple-element.123), kind=kCustom, calls=%fused_computation.4.clone | custom fusion | bytes 28672 | tf_op jit(solution)/shard_map/jit(_take)/gather | solution.py:89
  102.8 2.8 %gather_fusion.4 = f32[1024,3]{1,0:T(8,128)S(1)} fusion(f32[3,1024]{0,1:T(8,128)S(1)} %collective-permute-done.5, s32[1024]{0:T(1024)S(1)} %get-tuple-element.122), kind=kCustom, calls=%fused_computation.2.clone | custom fusion | bytes 28672 | tf_op jit(solution)/shard_map/jit(_take)/gather | solution.py:89
  105.7 0.9 fusion.24
  106.9 4.4 %collective-permute-start.7 = (f32[3,1024]{0,1:T(8,128)S(1)}, f32[3,1024]{0,1:T(8,128)S(1)}, u32[]{:S(2)}, u32[]{:S(2)}) collective-permute-start(f32[3,1024]{0,1:T(8,128)S(1)} %fusion.24), channel_id=1, source_target_pairs={{30,0},{0,2},{2,4},{4,6},{6,8},{8,10},{10,12},{12,14},{14,16},{16,... | collective-permute-start | bytes 36872 | tf_op jit(solution)/shard_map/ppermute | solution.py:19
  111.3 1.4 collective-permute-start.6
  112.7 0.6 gather_fusion.1
  113.4 26.5 %collective-permute-done.6 = f32[3,1024]{0,1:T(8,128)S(1)} collective-permute-done((f32[3,1024]{0,1:T(8,128)S(1)}, f32[3,1024]{0,1:T(8,128)S(1)}, u32[]{:S(2)}, u32[]{:S(2)}) %collective-permute-start.6) | collective-permute-done | bytes 12320 | tf_op jit(solution)/shard_map/ppermute | solution.py:19
  140.9 0.6 gather_fusion.2
  141.6 2.1 %fusion.18 = (f32[16,128,128]{2,1,0:T(8,128)S(1)}, f32[16,128,128]{2,1,0:T(8,128)S(1)}) fusion(f32[3,16,128]{2,1,0:T(8,128)S(1)} %copy.113, f32[3,16,128]{2,1,0:T(8,128)S(1)} %copy.112, f32[3,16,128]{2,1,0:T(8,128)S(1)} %copy.111, f32[3,16,128]{2,1,0:T(8,128)S(1)} %copy.105), kind=kLoop, calls=%fused_computation.49 | loop fusion | flops 4980736 | bytes 2195456 | tf_op jit(solution)/shard_map/reduce_sum | solution.py:66
  143.9 2.0 %fusion.20 = f32[16,128,128]{2,1,0:T(8,128)S(1)} fusion(f32[16,128,128]{2,1,0:T(8,128)S(1)} %clamp_multiply_fusion, f32[3,16,128]{2,1,0:T(8,128)S(1)} %copy.113, f32[3,16,128]{2,1,0:T(8,128)S(1)} %copy.112, f32[3,16,128]{2,1,0:T(8,128)S(1)} %copy.111, f32[3,16,128]{2,1,0:T(8,128)S(1)} %copy.105), kind=kLoop, calls=%fused_computation.51 | loop fusion | flops 4456448 | bytes 2195456 | tf_op jit(solution)/shard_map/reduce_sum | solution.py:70
  146.6 4.3 %psum.15 = f32[1024]{0:T(1024)} all-reduce(f32[1024]{0:T(1024)S(1)} %convolution_bitcast_fusion.3), channel_id=1, replica_groups=mesh['cells'=16,'lanes'=2] {'lanes'}, use_global_device_ids=true, to_apply=%region_13.15 | all-reduce | flops 1024 | bytes 8192 | tf_op jit(solution)/shard_map/psum | solution.py:143
  (185 shorter events, 20.5 us)
Async XLA Ops:
  1.4 10.8 %collective-permute-start.3 = (f32[9,1024]{1,0:T(8,128)S(1)}, f32[9,1024]{1,0:T(8,128)S(1)}, u32[]{:S(2)}, u32[]{:S(2)}) collective-permute-start(f32[9,1024]{1,0:T(8,128)S(1)} %pad_maximum_fusion), channel_id=1, source_target_pairs={{4,0},{6,2},{8,4},{10,6},{12,8},{14,10},{16,12},{18,14},{20,16},{2... | collective-permute-start | bytes 110600 | tf_op jit(solution)/shard_map/ppermute | solution.py:19
  1.7 10.5 %collective-permute-start.2 = (f32[9,1024]{1,0:T(8,128)S(1)}, f32[9,1024]{1,0:T(8,128)S(1)}, u32[]{:S(2)}, u32[]{:S(2)}) collective-permute-start(f32[9,1024]{1,0:T(8,128)S(1)} %pad_maximum_fusion), channel_id=1, source_target_pairs={{2,0},{4,2},{6,4},{8,6},{10,8},{12,10},{14,12},{16,14},{18,16},{20... | collective-permute-start | bytes 110600 | tf_op jit(solution)/shard_map/ppermute | solution.py:19
  2.6 8.7 %collective-permute-start.1 = (f32[9,1024]{1,0:T(8,128)S(1)}, f32[9,1024]{1,0:T(8,128)S(1)}, u32[]{:S(2)}, u32[]{:S(2)}) collective-permute-start(f32[9,1024]{1,0:T(8,128)S(1)} %pad_maximum_fusion), channel_id=1, source_target_pairs={{30,0},{0,2},{2,4},{4,6},{6,8},{8,10},{10,12},{12,14},{14,16},{16,... | collective-permute-start | bytes 110600 | tf_op jit(solution)/shard_map/ppermute | solution.py:19
  6.5 4.8 %collective-permute-start = (f32[9,1024]{1,0:T(8,128)S(1)}, f32[9,1024]{1,0:T(8,128)S(1)}, u32[]{:S(2)}, u32[]{:S(2)}) collective-permute-start(f32[9,1024]{1,0:T(8,128)S(1)} %pad_maximum_fusion), channel_id=1, source_target_pairs={{28,0},{30,2},{0,4},{2,6},{4,8},{6,10},{8,12},{10,14},{12,16},{14,... | collective-permute-start | bytes 110600 | tf_op jit(solution)/shard_map/ppermute | solution.py:19
  64.9 9.7 %copy-start.2 = (s32[32]{0:T(128)S(1)}, s32[32]{0:T(128)}, u32[]{:S(2)}) copy-start(s32[32]{0:T(128)} %param.21) | copy-start | bytes 388
  71.1 16.5 %collective-permute-start.4 = (f32[4,1024]{0,1:T(8,128)S(1)}, f32[4,1024]{0,1:T(8,128)S(1)}, u32[]{:S(2)}, u32[]{:S(2)}) collective-permute-start(f32[4,1024]{0,1:T(8,128)S(1)} %add_bitcast_fusion), channel_id=1, source_target_pairs={{30,0},{0,2},{2,4},{4,6},{6,8},{8,10},{10,12},{12,14},{14,16},{16,... | collective-permute-start | bytes 49160 | tf_op jit(solution)/shard_map/ppermute | solution.py:19
  87.6 0.7 copy-start.1
  88.7 11.4 %collective-permute-start.5 = (f32[3,1024]{0,1:T(8,128)S(1)}, f32[3,1024]{0,1:T(8,128)S(1)}, u32[]{:S(2)}, u32[]{:S(2)}) collective-permute-start(f32[3,1024]{0,1:T(8,128)S(1)} %fusion.22), channel_id=1, source_target_pairs={{2,0},{4,2},{6,4},{8,6},{10,8},{12,10},{14,12},{16,14},{18,16},{20... | collective-permute-start | bytes 36872 | tf_op jit(solution)/shard_map/ppermute | solution.py:19
  105.6 7.1 %copy-start = (f32[3,1024]{1,0:T(4,128)S(1)}, f32[3,1024]{1,0:T(4,128)}, u32[]{:S(2)}) copy-start(f32[3,1024]{1,0:T(4,128)} %param.13) | copy-start | bytes 36868
  106.8 33.8 %collective-permute-start.9 = (f32[3,1024]{0,1:T(8,128)S(1)}, f32[3,1024]{0,1:T(8,128)S(1)}, u32[]{:S(2)}, u32[]{:S(2)}) collective-permute-start(f32[3,1024]{0,1:T(8,128)S(1)} %fusion.24), channel_id=1, source_target_pairs={{4,0},{6,2},{8,4},{10,6},{12,8},{14,10},{16,12},{18,14},{20,16},{2... | collective-permute-start | bytes 36872 | tf_op jit(solution)/shard_map/ppermute | solution.py:19
  106.8 33.6 %collective-permute-start.8 = (f32[3,1024]{0,1:T(8,128)S(1)}, f32[3,1024]{0,1:T(8,128)S(1)}, u32[]{:S(2)}, u32[]{:S(2)}) collective-permute-start(f32[3,1024]{0,1:T(8,128)S(1)} %fusion.24), channel_id=1, source_target_pairs={{2,0},{4,2},{6,4},{8,6},{10,8},{12,10},{14,12},{16,14},{18,16},{20... | collective-permute-start | bytes 36872 | tf_op jit(solution)/shard_map/ppermute | solution.py:19
  106.9 33.3 %collective-permute-start.7 = (f32[3,1024]{0,1:T(8,128)S(1)}, f32[3,1024]{0,1:T(8,128)S(1)}, u32[]{:S(2)}, u32[]{:S(2)}) collective-permute-start(f32[3,1024]{0,1:T(8,128)S(1)} %fusion.24), channel_id=1, source_target_pairs={{30,0},{0,2},{2,4},{4,6},{6,8},{8,10},{10,12},{12,14},{14,16},{16,... | collective-permute-start | bytes 36872 | tf_op jit(solution)/shard_map/ppermute | solution.py:19
  111.3 28.6 %collective-permute-start.6 = (f32[3,1024]{0,1:T(8,128)S(1)}, f32[3,1024]{0,1:T(8,128)S(1)}, u32[]{:S(2)}, u32[]{:S(2)}) collective-permute-start(f32[3,1024]{0,1:T(8,128)S(1)} %fusion.24), channel_id=1, source_target_pairs={{28,0},{30,2},{0,4},{2,6},{4,8},{6,10},{8,12},{10,14},{12,16},{14,... | collective-permute-start | bytes 36872 | tf_op jit(solution)/shard_map/ppermute | solution.py:19
where the time goes:
time: 152 us; the launch traced here: 151 us
  other arithmetic  40.5 us (27%)
  waiting for transfers between devices  31.4 us (21%)
  local copies, waits for them, and re-layouts  23.6 us (16%)
  blocking collectives  21.1 us (14%)
  matrix products  17 us (11%)
  starting transfers between devices  15.4 us (10%)
    ppermute x10, waiting for transfers between devices, passed_along(): return lax.ppermute(block, axis, route)  31.4 us
    scatter-add x4, other arithmetic, deposit(): jax.ops.segment_sum(jnp.transpose(masked), node_ids, num_segments=node_co...  24.8 us
    psum x1, blocking collectives, local(): forces = lax.psum(partial_value, 'lanes')  16.7 us
    ppermute x10, starting transfers between devices, passed_along(): return lax.ppermute(block, axis, route)  15.4 us
    dot_general x8, matrix products, tile_forces(): jnp.einsum('ckj,cki->kij', source_burgers, target_line, precision=HIGH)  8.18 us
    gather x2, local copies, waits for them, and re-layouts, end_velocity(): jnp.take(next_velocity, node_ids, axis=1)  5.62 us
    gather x2, local copies, waits for them, and re-layouts, end_velocity(): jnp.take(velocity, node_ids, axis=1)  5.62 us
    gather x8, local copies, waits for them, and re-layouts, add_entry(): chosen = jnp.take(window_blocks, column, axis=1)  4.44 us
  transfers between devices with their start and end apart: 10, of which 2 were waited for; matrix products, arithmetic and copies ran while one was open for 17% of the time, Pallas kernels for 0%

commit v1 on v0

v1 whole, which is shorter than its diff:
```python
import functools

import jax
import jax.numpy as jnp
from jax import lax
from jax.experimental import pallas as pl
from jax.experimental.pallas import tpu as pltpu
from jax.sharding import PartitionSpec as P

BLK = 128
REACH = 2
FORCE_SCALE = 0.02
CORE_SQUARE = 0.25
TIME_STEP = 4.0
MIDDLE = 2.0

F32 = jnp.float32
BF16 = jnp.bfloat16
VM = pl.BlockSpec(memory_space=pltpu.VMEM)
SM = pl.BlockSpec(memory_space=pltpu.SMEM)


def shifted(block, cell_step, lane_step):
    cells, lanes = lax.axis_size("cells"), lax.axis_size("lanes")
    route = []
    for c in range(cells):
        for l in range(lanes):
            source = ((c + cell_step) % cells) * lanes + (l + lane_step) % lanes
            route.append((source, c * lanes + l))
    return lax.ppermute(block, ("cells", "lanes"), route)


def split3(x):
    high = x.astype(BF16).astype(F32)
    rest = x - high
    mid = rest.astype(BF16).astype(F32)
    return high, mid, rest - mid


def cross_rows(a, b):
    return jnp.concatenate(
        [
            a[1:2] * b[2:3] - a[2:3] * b[1:2],
            a[2:3] * b[0:1] - a[0:1] * b[2:3],
            a[0:1] * b[1:2] - a[1:2] * b[0:1],
        ],
        0,
    )


def contract_lanes(a, b):
    return lax.dot_general(a, b, (((1,), (1,)), ((), ())), preferred_element_type=F32)


def end_address(pack, end, high_count):
    node = pack[9 + end : 10 + end].astype(jnp.int32)
    owner = pack[11 + end : 12 + end].astype(jnp.int32)
    return owner * high_count + node // BLK, node % BLK


def low_onehot(low):
    rows = lax.broadcasted_iota(jnp.int32, (BLK, low.shape[1]), 0)
    return (rows == low).astype(F32).astype(BF16)


def force_kernel(lanes, high_count, lists, *refs):
    packs = refs[: 2 * REACH + 1]
    own_out, next_out, rhs_s, src_s, lhs_s, force_s = refs[2 * REACH + 1 :]
    seg = packs[0].shape[1]
    blocks = seg // BLK
    one = jnp.ones((1, seg), F32)

    for d, ref in enumerate(packs):
        centre = ref[0:3] - MIDDLE
        line = ref[3:6]
        burgers = ref[6:9]
        square = jnp.sum(centre * centre, axis=0, keepdims=True)
        near = jnp.concatenate([-2.0 * centre, square, one, jnp.zeros((3, seg), F32)], 0)
        along = jnp.concatenate([jnp.zeros((5, seg), F32), burgers], 0)
        sums = jnp.concatenate(
            [line, cross_rows(line, centre), jnp.zeros((2, seg), F32)], 0
        )
        nh, nm, nl = split3(near)
        ah, am, al = split3(along)
        sh, sm, sl = split3(sums)
        near6 = jnp.concatenate([nh, nm, nh, nl, nh, nm], 0).astype(BF16)
        along6 = jnp.concatenate([ah, am, ah, al, ah, am], 0).astype(BF16)
        sums3 = jnp.concatenate([sh, sm, sl, jnp.zeros((8, seg), F32)], 0).astype(BF16)
        for k in range(blocks):
            cut = slice(k * BLK, (k + 1) * BLK)
            rhs_s[d * blocks + k, :, 0:BLK] = near6[:, cut]
            rhs_s[d * blocks + k, :, BLK : 2 * BLK] = along6[:, cut]
            src_s[d * blocks + k] = sums3[:, cut]
        if d == REACH:
            target = jnp.concatenate([centre, one, square + CORE_SQUARE, line], 0)
            th, tm, tl = split3(target)
            target6 = jnp.concatenate([th, th, tm, th, tl, tm], 0)
            for k in range(blocks):
                lhs_s[k] = target6[:, k * BLK : (k + 1) * BLK].T.astype(BF16)

    own = packs[REACH]

    def one_target(t, carry):
        lhs = lhs_s[t]
        total = jnp.zeros((32, BLK), F32)
        for e in range(lists.shape[1]):
            w = lists[t, e]
            both = jnp.dot(lhs, rhs_s[w], preferred_element_type=F32)
            inverse = lax.rsqrt(both[:, :BLK])
            weight = both[:, BLK:] * inverse * (inverse * inverse)
            high = weight.astype(BF16)
            low = (weight - high.astype(F32)).astype(BF16)
            src = src_s[w]
            total = total + contract_lanes(src, high) + contract_lanes(src, low)
        whole = total[0:8] + (total[8:16] + total[16:24])
        force_s[t] = whole
        return carry

    lax.fori_loop(0, blocks, one_target, 0)

    whole = jnp.concatenate([force_s[t] for t in range(blocks)], 1)
    centre = own[0:3] - MIDDLE
    line = own[3:6]
    force = (0.5 * FORCE_SCALE) * (cross_rows(whole[0:3], centre) - whole[3:6])
    length = jnp.sqrt(jnp.sum(line * line, axis=0, keepdims=True)) * (0.5 / lanes)
    parts = split3(jnp.concatenate([force, length], 0))
    rows16 = lax.broadcasted_iota(jnp.int32, (2 * high_count, seg), 0)
    pack = own[...]
    out = None
    for end in range(2):
        high, low = end_address(pack, end, high_count)
        mask = rows16 == high
        lhs = jnp.concatenate(
            [
                jnp.where(mask, part[k : k + 1], 0.0)
                for part in parts
                for k in range(4)
            ],
            0,
        ).astype(BF16)
        term = contract_lanes(lhs, low_onehot(low))
        out = term if out is None else out + term
    n = 8 * high_count
    out = out[0:n] + (out[n : 2 * n] + out[2 * n : 3 * n])
    for k in range(4):
        first = 2 * high_count * k
        own_out[k] = out[first : first + high_count]
        next_out[k] = out[first + high_count : first + 2 * high_count]


def near_kernel(high_count, targets, sources, *refs):
    packs = refs[: 2 * REACH + 1]
    velocities = refs[2 * REACH + 1 : 4 * REACH + 3]
    near_out, vel_out, tgt_s, src_s, acc_s = refs[4 * REACH + 3 :]
    seg = packs[0].shape[1]
    blocks = seg // BLK
    rows8 = lax.broadcasted_iota(jnp.int32, (high_count, seg), 0)

    for k in range(high_count):
        for x in range(3):
            vel_out[x : x + 1, k * BLK : (k + 1) * BLK] = velocities[REACH][x, k : k + 1, :]

    for d, ref in enumerate(packs):
        pack = ref[...]
        table = jnp.concatenate(
            [velocities[d][x] for x in range(3)] + [velocities[d + 1][x] for x in range(3)], 0
        )
        lhs = jnp.concatenate(split3(table), 0).astype(BF16)
        n = 6 * high_count
        picked = [None] * 3
        for end in range(2):
            high, low = end_address(pack, end, high_count)
            got = jnp.dot(lhs, low_onehot(low), preferred_element_type=F32)
            got = got[0:n] + (got[n : 2 * n] + got[2 * n : 3 * n])
            for owner in range(2):
                mask = rows8 + owner * high_count == high
                for x in range(3):
                    first = (3 * owner + x) * high_count
                    term = jnp.where(mask, got[first : first + high_count], 0.0)
                    picked[x] = term if picked[x] is None else picked[x] + term
        motion = jnp.concatenate(
            [jnp.sum(p, axis=0, keepdims=True) * (0.5 * TIME_STEP) for p in picked], 0
        )
        fields = jnp.concatenate([pack[0:3], motion, jnp.zeros((2, seg), F32)], 0)
        for k in range(blocks):
            src_s[d * blocks + k] = fields[:, k * BLK : (k + 1) * BLK]

    for t in range(blocks):
        columns = src_s[REACH * blocks + t].T
        for x in range(6):
            tgt_s[t, x] = jnp.broadcast_to(columns[:, x : x + 1], (BLK, BLK))
    acc_s[...] = jnp.zeros_like(acc_s)

    def one_pair(k, carry):
        t = targets[k]
        src = src_s[sources[k]]
        r = [tgt_s[t, x] - src[x : x + 1] for x in range(3)]
        v = [tgt_s[t, 3 + x] - src[3 + x : 4 + x] for x in range(3)]
        dot = r[0] * v[0] + r[1] * v[1] + r[2] * v[2]
        vv = v[0] * v[0] + v[1] * v[1] + v[2] * v[2] + CORE_SQUARE
        s = jnp.clip(-dot / vv, 0.0, 1.0)
        m = [r[x] + s * v[x] for x in range(3)]
        acc_s[t] += jnp.exp(-(m[0] * m[0] + m[1] * m[1] + m[2] * m[2]))
        return carry

    lax.fori_loop(0, targets.shape[0], one_pair, 0)

    ones = jnp.ones((8, BLK), BF16)
    for t in range(blocks):
        h, m, l = split3(acc_s[t])
        total = (
            contract_lanes(ones, h.astype(BF16))
            + contract_lanes(ones, m.astype(BF16))
            + contract_lanes(ones, l.astype(BF16))
        )
        near_out[t : t + 1] = total[0:1]


def local(
    centres, seg_lines, burgers, neighbour_blocks, seg_nodes, node_owner, mobility, cand_target, cand_source
):
    seg = centres.shape[1]
    blocks = seg // BLK
    high_count = mobility.shape[0] // BLK
    lanes = lax.axis_size("lanes")
    window = (2 * REACH + 1) * blocks
    own = jnp.concatenate(
        [centres, seg_lines, burgers, seg_nodes.astype(F32), node_owner.astype(F32)], 0
    )
    packs = [own if o == 0 else shifted(own, o, 0) for o in range(-REACH, REACH + 1)]
    part = jax.ShapeDtypeStruct((4, high_count, BLK), F32)
    own_part, next_part = pl.pallas_call(
        functools.partial(force_kernel, lanes, high_count),
        out_shape=(part, part),
        in_specs=[SM] + [VM] * len(packs),
        out_specs=(VM, VM),
        scratch_shapes=[
            pltpu.VMEM((window, 48, 2 * BLK), BF16),
            pltpu.VMEM((window, 32, BLK), BF16),
            pltpu.VMEM((blocks, BLK, 48), BF16),
            pltpu.VMEM((blocks, 8, BLK), F32),
        ],
        name="forces",
    )(neighbour_blocks, *packs)
    totals = own_part
    for lane in range(1, lanes):
        totals = totals + shifted(own_part, 0, lane)
    for lane in range(lanes):
        totals = totals + shifted(next_part, -1, lane)
    velocity = mobility.reshape(1, high_count, BLK) * totals[0:3] / (1.0 + totals[3:4])
    velocities = [
        velocity if o == 0 else shifted(velocity, o, 0) for o in range(-REACH, REACH + 2)
    ]
    near, vel = pl.pallas_call(
        functools.partial(near_kernel, high_count),
        out_shape=(
            jax.ShapeDtypeStruct((blocks, BLK), F32),
            jax.ShapeDtypeStruct((3, high_count * BLK), F32),
        ),
        in_specs=[SM, SM] + [VM] * (len(packs) + len(velocities)),
        out_specs=(VM, VM),
        scratch_shapes=[
            pltpu.VMEM((blocks, 6, BLK, BLK), F32),
            pltpu.VMEM((window, 8, BLK), F32),
            pltpu.VMEM((blocks, BLK, BLK), F32),
        ],
        name="nearness",
    )(cand_target, cand_source, *packs, *velocities)
    return vel, near.reshape(seg)


def solution(mesh):
    in_specs = (
        P(None, "cells"),
        P(None, "cells"),
        P(None, "cells"),
        P("cells", "lanes"),
        P(None, "cells"),
        P(None, "cells"),
        P("cells"),
        P("cells"),
        P("cells"),
    )
    out_specs = (P(None, "cells"), P("cells"))
    return jax.shard_map(local, mesh=mesh, in_specs=in_specs, out_specs=out_specs, check_vma=False)
```

time: 152 us -> 57.2 us (0.38)
  the two profiles are of different devices: /device:TPU:29 before, /device:TPU:0 now
where the time goes in v1:
time: 57.2 us; the launch traced here: 56.6 us
  Pallas kernels  21.4 us (37%)
  waiting for transfers between devices  18.2 us (32%)
  starting transfers between devices  11.3 us (20%)
  local copies, waits for them, and re-layouts  2.82 us (5%)
  other arithmetic  2.15 us (4%)
  between operations  0.75 us (1%)
    ppermute x12, waiting for transfers between devices, shifted(): return lax.ppermute(block, ('cells', 'lanes'), route)  18.2 us
    pallas_call x1, Pallas kernels, local(): pl.pallas_call(functools.partial(force_kernel, lanes, high_count), out_sh...  14.1 us
    ppermute x12, starting transfers between devices, shifted(): return lax.ppermute(block, ('cells', 'lanes'), route)  11.3 us
    pallas_call x1, Pallas kernels, local(): pl.pallas_call(functools.partial(near_kernel, high_count), out_shape=(jax...  7.27 us
    unnamed x28, local copies, waits for them, and re-layouts  1.92 us
  transfers between devices with their start and end apart: 12, of which 10 were waited for; matrix products, arithmetic and copies ran while one was open for 0% of the time, Pallas kernels for 0%

profile of v1, /device:TPU:0, one launch (start us, length us, event | category | flops | bytes accessed | tf_op | source)
XLA Modules:
  0.0 56.6 jit_solution(17141904342527184839)
XLA Ops:
  0.6 0.0 copy-start.7
  0.6 0.0 copy-start.6
  0.6 0.7 %convert_element_type.6 = f32[2,1024]{1,0:T(2,128)S(1)} convert(s32[2,1024]{1,0:T(2,128)} %param.13) | non-fusion elementwise | flops 2048 | bytes 16384 | tf_op jit(solution)/shard_map/convert_element_type | solution.py:228
  1.4 0.7 %convert_element_type.7 = f32[2,1024]{1,0:T(2,128)S(1)} convert(s32[2,1024]{1,0:T(2,128)} %param.14) | non-fusion elementwise | flops 2048 | bytes 16384 | tf_op jit(solution)/shard_map/convert_element_type | solution.py:228
  2.1 0.0 copy-done.7
  2.1 0.0 copy-done.6
  2.1 0.9 %concatenate.3.refs_2_ = f32[13,1024]{1,0:T(8,128)S(1)} concatenate(f32[3,1024]{1,0:T(4,128)S(1)} %copy-done.6, f32[3,1024]{1,0:T(4,128)S(1)} %copy-done.7, f32[3,1024]{1,0:T(4,128)} %param.11, f32[2,1024]{1,0:T(2,128)S(1)} %convert_element_type.6, f32[2,1024]{1,0:T(2,128)S(1)} %convert_element_type.7), dimensions={0} | concatenate | bytes 106496 | tf_op jit(solution)/shard_map/concatenate | solution.py:227
  3.0 6.1 %collective-permute-start.3 = (f32[13,1024]{1,0:T(8,128)S(1)}, f32[13,1024]{1,0:T(8,128)S(1)}, u32[]{:S(2)}, u32[]{:S(2)}) collective-permute-start(f32[13,1024]{1,0:T(8,128)S(1)} %concatenate.3.refs_2_), channel_id=1, source_target_pairs={{4,0},{5,1},{6,2},{7,3},{8,4},{9,5},{10,6},{11,7},{12,8},{13,9},{1... | collective-permute-start | bytes 159752 | tf_op jit(solution)/shard_map/ppermute | solution.py:30
  9.1 0.0 collective-permute-start.2
  9.1 0.5 collective-permute-start.1
  9.6 0.7 %collective-permute-start = (f32[13,1024]{1,0:T(8,128)S(1)}, f32[13,1024]{1,0:T(8,128)S(1)}, u32[]{:S(2)}, u32[]{:S(2)}) collective-permute-start(f32[13,1024]{1,0:T(8,128)S(1)} %concatenate.3.refs_2_), channel_id=1, source_target_pairs={{28,0},{29,1},{30,2},{31,3},{0,4},{1,5},{2,6},{3,7},{4,8},{5,9},{6... | collective-permute-start | bytes 159752 | tf_op jit(solution)/shard_map/ppermute | solution.py:30
  10.2 0.7 %collective-permute-done.3.refs_4_ = f32[13,1024]{1,0:T(8,128)S(1)} collective-permute-done((f32[13,1024]{1,0:T(8,128)S(1)}, f32[13,1024]{1,0:T(8,128)S(1)}, u32[]{:S(2)}, u32[]{:S(2)}) %collective-permute-start.3) | collective-permute-done | bytes 53280 | tf_op jit(solution)/shard_map/ppermute | solution.py:30
  11.0 0.6 %collective-permute-done.2.refs_3_ = f32[13,1024]{1,0:T(8,128)S(1)} collective-permute-done((f32[13,1024]{1,0:T(8,128)S(1)}, f32[13,1024]{1,0:T(8,128)S(1)}, u32[]{:S(2)}, u32[]{:S(2)}) %collective-permute-start.2) | collective-permute-done | bytes 53280 | tf_op jit(solution)/shard_map/ppermute | solution.py:30
  11.6 3.9 %collective-permute-done.1.refs_1_ = f32[13,1024]{1,0:T(8,128)S(1)} collective-permute-done((f32[13,1024]{1,0:T(8,128)S(1)}, f32[13,1024]{1,0:T(8,128)S(1)}, u32[]{:S(2)}, u32[]{:S(2)}) %collective-permute-start.1) | collective-permute-done | bytes 53280 | tf_op jit(solution)/shard_map/ppermute | solution.py:30
  15.5 1.6 %collective-permute-done.refs_0_ = f32[13,1024]{1,0:T(8,128)S(1)} collective-permute-done((f32[13,1024]{1,0:T(8,128)S(1)}, f32[13,1024]{1,0:T(8,128)S(1)}, u32[]{:S(2)}, u32[]{:S(2)}) %collective-permute-start) | collective-permute-done | bytes 53280 | tf_op jit(solution)/shard_map/ppermute | solution.py:30
  17.1 0.0 copy-done
  17.1 0.0 copy-done.1
  17.1 0.0 copy-done.2
  17.1 0.0 copy-done.3
  17.1 0.0 copy-start.4
  17.1 0.6 %copy-done.4 = f32[13,1024]{1,0:T(8,128)} copy-done((f32[13,1024]{1,0:T(8,128)}, f32[13,1024]{1,0:T(8,128)S(1)}, u32[]{:S(2)}) %copy-start.4) | copy-done | bytes 53272
  17.7 14.1 %forces.1 = (f32[4,8,128]{2,1,0:T(8,128)}, f32[4,8,128]{2,1,0:T(8,128)}) custom-call(s32[8,8]{1,0:T(8,128)} %lists.1, f32[13,1024]{1,0:T(8,128)} %copy-done.4, f32[13,1024]{1,0:T(8,128)} %copy-done.3, f32[13,1024]{1,0:T(8,128)} %copy-done, f32[13,1024]{1,0:T(8,128)} %copy-done.2, f32[13,1024]{1,0:T(8,128)} %copy-done.1), custom_call_target="tpu_custom_call" | custom-call | tf_op jit(solution)/shard_map/forces/pallas_call | solution.py:232
  31.8 1.5 %collective-permute-start.4 = (f32[4,8,128]{2,1,0:T(8,128)}, f32[4,8,128]{2,1,0:T(8,128)S(1)}, u32[]{:S(2)}, u32[]{:S(2)}) collective-permute-start(f32[4,8,128]{2,1,0:T(8,128)} %get-tuple-element.6), channel_id=1, source_target_pairs={{1,0},{0,1},{3,2},{2,3},{5,4},{4,5},{7,6},{6,7},{9,8},{8,9},{11,10... | collective-permute-start | bytes 49160 | tf_op jit(solution)/shard_map/ppermute | solution.py:30
  33.3 0.0 collective-permute-start.6
  33.3 0.0 collective-permute-start.5
  33.3 2.5 %collective-permute-done.4 = f32[4,8,128]{2,1,0:T(8,128)S(1)} collective-permute-done((f32[4,8,128]{2,1,0:T(8,128)}, f32[4,8,128]{2,1,0:T(8,128)S(1)}, u32[]{:S(2)}, u32[]{:S(2)}) %collective-permute-start.4) | collective-permute-done | bytes 16416 | tf_op jit(solution)/shard_map/ppermute | solution.py:30
  35.8 4.5 %collective-permute-done.6 = f32[4,8,128]{2,1,0:T(8,128)S(1)} collective-permute-done((f32[4,8,128]{2,1,0:T(8,128)}, f32[4,8,128]{2,1,0:T(8,128)S(1)}, u32[]{:S(2)}, u32[]{:S(2)}) %collective-permute-start.6) | collective-permute-done | bytes 16416 | tf_op jit(solution)/shard_map/ppermute | solution.py:30
  40.3 0.0 collective-permute-done.5
  40.3 0.7 %add_add_fusion = f32[4,8,128]{2,1,0:T(8,128)S(1)} fusion(f32[4,8,128]{2,1,0:T(8,128)S(1)} %collective-permute-done.6, f32[4,8,128]{2,1,0:T(8,128)S(1)} %collective-permute-done.5, f32[4,8,128]{2,1,0:T(8,128)} %get-tuple-element.6, f32[4,8,128]{2,1,0:T(8,128)S(1)} %collective-permute-done.4), kind=kLoop, calls=%fused_computation | loop fusion | flops 12288 | bytes 81920 | tf_op jit(solution)/shard_map/add | solution.py:249
  41.0 0.7 %copy-done.13 = f32[1024]{0:T(1024)S(1)} copy-done((f32[1024]{0:T(1024)S(1)}, f32[1024]{0:T(1024)}, u32[]{:S(2)}) %copy-start.13) | copy-done | bytes 4120
  41.7 0.0 collective-permute-start.11
  41.7 0.1 collective-permute-start.10
  41.8 0.1 collective-permute-start.9
  41.8 0.5 collective-permute-start.8
  42.3 2.0 %collective-permute-start.7 = (f32[3,8,128]{2,1,0:T(8,128)S(1)}, f32[3,8,128]{2,1,0:T(8,128)S(1)}, u32[]{:S(2)}, u32[]{:S(2)}) collective-permute-start(f32[3,8,128]{2,1,0:T(8,128)S(1)} %fusion.refs_7_), channel_id=1, source_target_pairs={{28,0},{29,1},{30,2},{31,3},{0,4},{1,5},{2,6},{3,7},{4,8},{5,9},{6... | collective-permute-start | bytes 36872 | tf_op jit(solution)/shard_map/ppermute | solution.py:30
  44.3 0.5 collective-permute-done.11.refs_10_
  44.8 0.6 %collective-permute-done.10.refs_9_ = f32[3,8,128]{2,1,0:T(8,128)S(1)} collective-permute-done((f32[3,8,128]{2,1,0:T(8,128)S(1)}, f32[3,8,128]{2,1,0:T(8,128)S(1)}, u32[]{:S(2)}, u32[]{:S(2)}) %collective-permute-start.10) | collective-permute-done | bytes 12320 | tf_op jit(solution)/shard_map/ppermute | solution.py:30
  45.5 0.0 collective-permute-done.9.refs_8_
  45.5 2.2 %collective-permute-done.8.refs_6_ = f32[3,8,128]{2,1,0:T(8,128)S(1)} collective-permute-done((f32[3,8,128]{2,1,0:T(8,128)S(1)}, f32[3,8,128]{2,1,0:T(8,128)S(1)}, u32[]{:S(2)}, u32[]{:S(2)}) %collective-permute-start.8) | collective-permute-done | bytes 12320 | tf_op jit(solution)/shard_map/ppermute | solution.py:30
  47.7 1.0 %collective-permute-done.7.refs_5_ = f32[3,8,128]{2,1,0:T(8,128)S(1)} collective-permute-done((f32[3,8,128]{2,1,0:T(8,128)S(1)}, f32[3,8,128]{2,1,0:T(8,128)S(1)}, u32[]{:S(2)}, u32[]{:S(2)}) %collective-permute-start.7) | collective-permute-done | bytes 12320 | tf_op jit(solution)/shard_map/ppermute | solution.py:30
  48.7 0.0 copy-done.5
  48.7 0.0 copy-done.8
  48.7 0.0 copy-done.9
  48.7 0.0 copy-done.10
  48.7 0.0 copy-done.11
  48.8 0.0 copy-start.12
  48.8 0.6 %copy-done.12 = f32[3,8,128]{2,1,0:T(8,128)} copy-done((f32[3,8,128]{2,1,0:T(8,128)}, f32[3,8,128]{2,1,0:T(8,128)S(1)}, u32[]{:S(2)}) %copy-start.12) | copy-done | bytes 12312
  49.4 7.3 %nearness.1 = (f32[8,128]{1,0:T(8,128)}, f32[3,1024]{1,0:T(4,128)}) custom-call(s32[32]{0:T(128)} %targets.1, s32[32]{0:T(128)} %sources.1, f32[13,1024]{1,0:T(8,128)} %copy-done.4, f32[13,1024]{1,0:T(8,128)} %copy-done.3, f32[13,1024]{1,0:T(8,128)} %copy-done, f32[13,1024]{1,0:T(8,128)} %copy-done.2, f32[13,1024]{1,0:T(8,128)} %copy-done.1, ...), custom_call_target="tpu_custom_call" | custom-call | tf_op jit(solution)/shard_map/nearness/pallas_call | solution.py:254
  (12 shorter events, 0.0 us)
Async XLA Ops:
  0.6 1.4 %copy-start.7 = (f32[3,1024]{1,0:T(4,128)S(1)}, f32[3,1024]{1,0:T(4,128)}, u32[]{:S(2)}) copy-start(f32[3,1024]{1,0:T(4,128)} %param.10) | copy-start | bytes 36868
  0.6 1.4 %copy-start.6 = (f32[3,1024]{1,0:T(4,128)S(1)}, f32[3,1024]{1,0:T(4,128)}, u32[]{:S(2)}) copy-start(f32[3,1024]{1,0:T(4,128)} %param.9) | copy-start | bytes 36868
  3.0 14.1 %copy-start = (f32[13,1024]{1,0:T(8,128)}, f32[13,1024]{1,0:T(8,128)S(1)}, u32[]{:S(2)}) copy-start(f32[13,1024]{1,0:T(8,128)S(1)} %concatenate.3.refs_2_) | copy-start | bytes 159748
  3.0 8.0 %collective-permute-start.3 = (f32[13,1024]{1,0:T(8,128)S(1)}, f32[13,1024]{1,0:T(8,128)S(1)}, u32[]{:S(2)}, u32[]{:S(2)}) collective-permute-start(f32[13,1024]{1,0:T(8,128)S(1)} %concatenate.3.refs_2_), channel_id=1, source_target_pairs={{4,0},{5,1},{6,2},{7,3},{8,4},{9,5},{10,6},{11,7},{12,8},{13,9},{1... | collective-permute-start | bytes 159752 | tf_op jit(solution)/shard_map/ppermute | solution.py:30
  9.1 2.5 %collective-permute-start.2 = (f32[13,1024]{1,0:T(8,128)S(1)}, f32[13,1024]{1,0:T(8,128)S(1)}, u32[]{:S(2)}, u32[]{:S(2)}) collective-permute-start(f32[13,1024]{1,0:T(8,128)S(1)} %concatenate.3.refs_2_), channel_id=1, source_target_pairs={{2,0},{3,1},{4,2},{5,3},{6,4},{7,5},{8,6},{9,7},{10,8},{11,9},{12,... | collective-permute-start | bytes 159752 | tf_op jit(solution)/shard_map/ppermute | solution.py:30
  9.1 6.4 %collective-permute-start.1 = (f32[13,1024]{1,0:T(8,128)S(1)}, f32[13,1024]{1,0:T(8,128)S(1)}, u32[]{:S(2)}, u32[]{:S(2)}) collective-permute-start(f32[13,1024]{1,0:T(8,128)S(1)} %concatenate.3.refs_2_), channel_id=1, source_target_pairs={{30,0},{31,1},{0,2},{1,3},{2,4},{3,5},{4,6},{5,7},{6,8},{7,9},{8,1... | collective-permute-start | bytes 159752 | tf_op jit(solution)/shard_map/ppermute | solution.py:30
  9.6 7.5 %collective-permute-start = (f32[13,1024]{1,0:T(8,128)S(1)}, f32[13,1024]{1,0:T(8,128)S(1)}, u32[]{:S(2)}, u32[]{:S(2)}) collective-permute-start(f32[13,1024]{1,0:T(8,128)S(1)} %concatenate.3.refs_2_), channel_id=1, source_target_pairs={{28,0},{29,1},{30,2},{31,3},{0,4},{1,5},{2,6},{3,7},{4,8},{5,9},{6... | collective-permute-start | bytes 159752 | tf_op jit(solution)/shard_map/ppermute | solution.py:30
  11.0 6.1 %copy-start.1 = (f32[13,1024]{1,0:T(8,128)}, f32[13,1024]{1,0:T(8,128)S(1)}, u32[]{:S(2)}) copy-start(f32[13,1024]{1,0:T(8,128)S(1)} %collective-permute-done.3.refs_4_) | copy-start | bytes 159748
  11.6 5.5 %copy-start.2 = (f32[13,1024]{1,0:T(8,128)}, f32[13,1024]{1,0:T(8,128)S(1)}, u32[]{:S(2)}) copy-start(f32[13,1024]{1,0:T(8,128)S(1)} %collective-permute-done.2.refs_3_) | copy-start | bytes 159748
  15.5 1.6 %copy-start.3 = (f32[13,1024]{1,0:T(8,128)}, f32[13,1024]{1,0:T(8,128)S(1)}, u32[]{:S(2)}) copy-start(f32[13,1024]{1,0:T(8,128)S(1)} %collective-permute-done.1.refs_1_) | copy-start | bytes 159748
  17.1 0.6 %copy-start.4 = (f32[13,1024]{1,0:T(8,128)}, f32[13,1024]{1,0:T(8,128)S(1)}, u32[]{:S(2)}) copy-start(f32[13,1024]{1,0:T(8,128)S(1)} %collective-permute-done.refs_0_) | copy-start | bytes 159748
  31.8 3.9 %collective-permute-start.4 = (f32[4,8,128]{2,1,0:T(8,128)}, f32[4,8,128]{2,1,0:T(8,128)S(1)}, u32[]{:S(2)}, u32[]{:S(2)}) collective-permute-start(f32[4,8,128]{2,1,0:T(8,128)} %get-tuple-element.6), channel_id=1, source_target_pairs={{1,0},{0,1},{3,2},{2,3},{5,4},{4,5},{7,6},{6,7},{9,8},{8,9},{11,10... | collective-permute-start | bytes 49160 | tf_op jit(solution)/shard_map/ppermute | solution.py:30
  33.3 7.0 %collective-permute-start.6 = (f32[4,8,128]{2,1,0:T(8,128)}, f32[4,8,128]{2,1,0:T(8,128)S(1)}, u32[]{:S(2)}, u32[]{:S(2)}) collective-permute-start(f32[4,8,128]{2,1,0:T(8,128)} %get-tuple-element.7), channel_id=1, source_target_pairs={{31,0},{30,1},{1,2},{0,3},{3,4},{2,5},{5,6},{4,7},{7,8},{6,9},{9,1... | collective-permute-start | bytes 49160 | tf_op jit(solution)/shard_map/ppermute | solution.py:30
  33.3 7.0 %collective-permute-start.5 = (f32[4,8,128]{2,1,0:T(8,128)}, f32[4,8,128]{2,1,0:T(8,128)S(1)}, u32[]{:S(2)}, u32[]{:S(2)}) collective-permute-start(f32[4,8,128]{2,1,0:T(8,128)} %get-tuple-element.7), channel_id=1, source_target_pairs={{30,0},{31,1},{0,2},{1,3},{2,4},{3,5},{4,6},{5,7},{6,8},{7,9},{8,1... | collective-permute-start | bytes 49160 | tf_op jit(solution)/shard_map/ppermute | solution.py:30
  41.0 0.7 %copy-start.13 = (f32[1024]{0:T(1024)S(1)}, f32[1024]{0:T(1024)}, u32[]{:S(2)}) copy-start(f32[1024]{0:T(1024)} %param.15) | copy-start | bytes 12292
  41.7 7.0 %copy-start.5 = (f32[3,8,128]{2,1,0:T(8,128)}, f32[3,8,128]{2,1,0:T(8,128)S(1)}, u32[]{:S(2)}) copy-start(f32[3,8,128]{2,1,0:T(8,128)S(1)} %fusion.refs_7_) | copy-start | bytes 36868
  41.7 3.1 %collective-permute-start.11 = (f32[3,8,128]{2,1,0:T(8,128)S(1)}, f32[3,8,128]{2,1,0:T(8,128)S(1)}, u32[]{:S(2)}, u32[]{:S(2)}) collective-permute-start(f32[3,8,128]{2,1,0:T(8,128)S(1)} %fusion.refs_7_), channel_id=1, source_target_pairs={{6,0},{7,1},{8,2},{9,3},{10,4},{11,5},{12,6},{13,7},{14,8},{15,9},... | collective-permute-start | bytes 36872 | tf_op jit(solution)/shard_map/ppermute | solution.py:30
  41.7 3.7 %collective-permute-start.10 = (f32[3,8,128]{2,1,0:T(8,128)S(1)}, f32[3,8,128]{2,1,0:T(8,128)S(1)}, u32[]{:S(2)}, u32[]{:S(2)}) collective-permute-start(f32[3,8,128]{2,1,0:T(8,128)S(1)} %fusion.refs_7_), channel_id=1, source_target_pairs={{4,0},{5,1},{6,2},{7,3},{8,4},{9,5},{10,6},{11,7},{12,8},{13,9},{1... | collective-permute-start | bytes 36872 | tf_op jit(solution)/shard_map/ppermute | solution.py:30
  41.8 3.7 %collective-permute-start.9 = (f32[3,8,128]{2,1,0:T(8,128)S(1)}, f32[3,8,128]{2,1,0:T(8,128)S(1)}, u32[]{:S(2)}, u32[]{:S(2)}) collective-permute-start(f32[3,8,128]{2,1,0:T(8,128)S(1)} %fusion.refs_7_), channel_id=1, source_target_pairs={{2,0},{3,1},{4,2},{5,3},{6,4},{7,5},{8,6},{9,7},{10,8},{11,9},{12,... | collective-permute-start | bytes 36872 | tf_op jit(solution)/shard_map/ppermute | solution.py:30
  41.8 5.9 %collective-permute-start.8 = (f32[3,8,128]{2,1,0:T(8,128)S(1)}, f32[3,8,128]{2,1,0:T(8,128)S(1)}, u32[]{:S(2)}, u32[]{:S(2)}) collective-permute-start(f32[3,8,128]{2,1,0:T(8,128)S(1)} %fusion.refs_7_), channel_id=1, source_target_pairs={{30,0},{31,1},{0,2},{1,3},{2,4},{3,5},{4,6},{5,7},{6,8},{7,9},{8,1... | collective-permute-start | bytes 36872 | tf_op jit(solution)/shard_map/ppermute | solution.py:30
  42.3 6.4 %collective-permute-start.7 = (f32[3,8,128]{2,1,0:T(8,128)S(1)}, f32[3,8,128]{2,1,0:T(8,128)S(1)}, u32[]{:S(2)}, u32[]{:S(2)}) collective-permute-start(f32[3,8,128]{2,1,0:T(8,128)S(1)} %fusion.refs_7_), channel_id=1, source_target_pairs={{28,0},{29,1},{30,2},{31,3},{0,4},{1,5},{2,6},{3,7},{4,8},{5,9},{6... | collective-permute-start | bytes 36872 | tf_op jit(solution)/shard_map/ppermute | solution.py:30
  44.8 3.9 %copy-start.8 = (f32[3,8,128]{2,1,0:T(8,128)}, f32[3,8,128]{2,1,0:T(8,128)S(1)}, u32[]{:S(2)}) copy-start(f32[3,8,128]{2,1,0:T(8,128)S(1)} %collective-permute-done.11.refs_10_) | copy-start | bytes 36868
  45.5 3.3 %copy-start.9 = (f32[3,8,128]{2,1,0:T(8,128)}, f32[3,8,128]{2,1,0:T(8,128)S(1)}, u32[]{:S(2)}) copy-start(f32[3,8,128]{2,1,0:T(8,128)S(1)} %collective-permute-done.10.refs_9_) | copy-start | bytes 36868
  45.5 3.3 %copy-start.10 = (f32[3,8,128]{2,1,0:T(8,128)}, f32[3,8,128]{2,1,0:T(8,128)S(1)}, u32[]{:S(2)}) copy-start(f32[3,8,128]{2,1,0:T(8,128)S(1)} %collective-permute-done.9.refs_8_) | copy-start | bytes 36868
  47.7 1.0 %copy-start.11 = (f32[3,8,128]{2,1,0:T(8,128)}, f32[3,8,128]{2,1,0:T(8,128)S(1)}, u32[]{:S(2)}) copy-start(f32[3,8,128]{2,1,0:T(8,128)S(1)} %collective-permute-done.8.refs_6_) | copy-start | bytes 36868
  48.8 0.6 %copy-start.12 = (f32[3,8,128]{2,1,0:T(8,128)}, f32[3,8,128]{2,1,0:T(8,128)S(1)}, u32[]{:S(2)}) copy-start(f32[3,8,128]{2,1,0:T(8,128)S(1)} %collective-permute-done.7.refs_5_) | copy-start | bytes 36868

commit v2 on v1

--- a/solution.py
+++ b/solution.py
@@ -18,6 +18,10 @@
 BF16 = jnp.bfloat16
 VM = pl.BlockSpec(memory_space=pltpu.VMEM)
 SM = pl.BlockSpec(memory_space=pltpu.SMEM)
+
+
+def params(mib):
+    return pltpu.CompilerParams(vmem_limit_bytes=mib << 20)
 
 
 def shifted(block, cell_step, lane_step):
@@ -102,18 +106,21 @@
 
     def one_target(t, carry):
         lhs = lhs_s[t]
-        total = jnp.zeros((32, BLK), F32)
+        highs, lows, srcs = [], [], []
         for e in range(lists.shape[1]):
             w = lists[t, e]
             both = jnp.dot(lhs, rhs_s[w], preferred_element_type=F32)
             inverse = lax.rsqrt(both[:, :BLK])
             weight = both[:, BLK:] * inverse * (inverse * inverse)
             high = weight.astype(BF16)
-            low = (weight - high.astype(F32)).astype(BF16)
-            src = src_s[w]
-            total = total + contract_lanes(src, high) + contract_lanes(src, low)
-        whole = total[0:8] + (total[8:16] + total[16:24])
-        force_s[t] = whole
+            highs.append(high)
+            lows.append((weight - high.astype(F32)).astype(BF16))
+            srcs.append(src_s[w])
+        src = jnp.concatenate(srcs, 1)
+        total = contract_lanes(jnp.concatenate(highs, 1), src)
+        total = total + contract_lanes(jnp.concatenate(lows, 1), src)
+        total = total.T
+        force_s[t] = total[0:8] + (total[8:16] + total[16:24])
         return carry
 
     lax.fori_loop(0, blocks, one_target, 0)
@@ -181,39 +188,65 @@
         motion = jnp.concatenate(
             [jnp.sum(p, axis=0, keepdims=True) * (0.5 * TIME_STEP) for p in picked], 0
         )
-        fields = jnp.concatenate([pack[0:3], motion, jnp.zeros((2, seg), F32)], 0)
-        for k in range(blocks):
-            src_s[d * blocks + k] = fields[:, k * BLK : (k + 1) * BLK]
-
-    for t in range(blocks):
-        columns = src_s[REACH * blocks + t].T
-        for x in range(6):
-            tgt_s[t, x] = jnp.broadcast_to(columns[:, x : x + 1], (BLK, BLK))
+        centre = pack[0:3] - MIDDLE
+        cc = jnp.sum(centre * centre, axis=0, keepdims=True)
+        vv = jnp.sum(motion * motion, axis=0, keepdims=True)
+        cv = jnp.sum(centre * motion, axis=0, keepdims=True)
+        one = jnp.ones((1, seg), F32)
+
+        def zero(n):
+            return jnp.zeros((n, seg), F32)
+
+        columns = [
+            [-2.0 * centre, cc, one, zero(11)],
+            [-motion, cv, zero(1), -centre, zero(1), one, zero(6)],
+            [zero(3), vv, zero(1), -2.0 * motion, one, zero(7)],
+        ]
+        for n, rows in enumerate(columns):
+            h, m, l = split3(jnp.concatenate(rows, 0))
+            six = jnp.concatenate([h, m, h, l, h, m], 0).astype(BF16)
+            for k in range(blocks):
+                src_s[d * blocks + k, :, n * BLK : (n + 1) * BLK] = six[:, k * BLK : (k + 1) * BLK]
+        if d == REACH:
+            h, m, l = split3(jnp.concatenate([centre, one, cc, motion, vv, cv, zero(6)], 0))
+            six = jnp.concatenate([h, h, m, h, l, m], 0)
+            for k in range(blocks):
+                tgt_s[k] = six[:, k * BLK : (k + 1) * BLK].T.astype(BF16)
+
     acc_s[...] = jnp.zeros_like(acc_s)
-
-    def one_pair(k, carry):
-        t = targets[k]
-        src = src_s[sources[k]]
-        r = [tgt_s[t, x] - src[x : x + 1] for x in range(3)]
-        v = [tgt_s[t, 3 + x] - src[3 + x : 4 + x] for x in range(3)]
-        dot = r[0] * v[0] + r[1] * v[1] + r[2] * v[2]
-        vv = v[0] * v[0] + v[1] * v[1] + v[2] * v[2] + CORE_SQUARE
-        s = jnp.clip(-dot / vv, 0.0, 1.0)
-        m = [r[x] + s * v[x] for x in range(3)]
-        acc_s[t] += jnp.exp(-(m[0] * m[0] + m[1] * m[1] + m[2] * m[2]))
+    count = targets.shape[0]
+    group = max(g for g in (1, 2, 4) if count % g == 0)
+
+    def some_pairs(step, carry):
+        for u in range(group):
+            k = step * group + u
+            t = targets[k]
+            three = jnp.dot(tgt_s[t], src_s[sources[k]], preferred_element_type=F32)
+            rr = three[:, 0:BLK]
+            rv = three[:, BLK : 2 * BLK]
+            vv = jnp.maximum(three[:, 2 * BLK : 3 * BLK], 0.0)
+            s = jnp.clip(-rv / (vv + CORE_SQUARE), 0.0, 1.0)
+            acc_s[t] += jnp.exp(-(rr + s * (2.0 * rv + s * vv)))
         return carry
 
-    lax.fori_loop(0, targets.shape[0], one_pair, 0)
+    lax.fori_loop(0, count // group, some_pairs, 0)
 
     ones = jnp.ones((8, BLK), BF16)
     for t in range(blocks):
-        h, m, l = split3(acc_s[t])
-        total = (
-            contract_lanes(ones, h.astype(BF16))
-            + contract_lanes(ones, m.astype(BF16))
-            + contract_lanes(ones, l.astype(BF16))
-        )
-        near_out[t : t + 1] = total[0:1]
+        total = acc_s[t]
+        high = total.astype(BF16)
+        low = (total - high.astype(F32)).astype(BF16)
+        near_out[t : t + 1] = (contract_lanes(ones, high) + contract_lanes(ones, low))[0:1]
+
+
+def velocity_kernel(mobility, *refs):
+    out = refs[-1]
+    total = refs[0][...]
+    for ref in refs[1:-1]:
+        total = total + ref[...]
+    scale = mobility[...] / (1.0 + total[3])
+    for x in range(3):
+        out[x] = total[x] * scale
 
 
 def local(
@@ -224,9 +257,14 @@
     high_count = mobility.shape[0] // BLK
     lanes = lax.axis_size("lanes")
     window = (2 * REACH + 1) * blocks
-    own = jnp.concatenate(
-        [centres, seg_lines, burgers, seg_nodes.astype(F32), node_owner.astype(F32)], 0
-    )
+    pieces = [centres, seg_lines, burgers, seg_nodes.astype(F32), node_owner.astype(F32)]
+    rows = sum(piece.shape[0] for piece in pieces)
+    own, first = 0.0, 0
+    for piece in pieces:
+        last = first + piece.shape[0]
+        own = own + jnp.pad(piece, ((first, rows - last), (0, 0)))
+        first = last
+    rate = mobility.reshape(high_count, BLK)
     packs = [own if o == 0 else shifted(own, o, 0) for o in range(-REACH, REACH + 1)]
     part = jax.ShapeDtypeStruct((4, high_count, BLK), F32)
     own_part, next_part = pl.pallas_call(
@@ -240,14 +278,20 @@
             pltpu.VMEM((blocks, BLK, 48), BF16),
             pltpu.VMEM((blocks, 8, BLK), F32),
         ],
+        compiler_params=params(16),
         name="forces",
     )(neighbour_blocks, *packs)
-    totals = own_part
-    for lane in range(1, lanes):
-        totals = totals + shifted(own_part, 0, lane)
-    for lane in range(lanes):
-        totals = totals + shifted(next_part, -1, lane)
-    velocity = mobility.reshape(1, high_count, BLK) * totals[0:3] / (1.0 + totals[3:4])
+    terms = [own_part]
+    terms += [shifted(own_part, 0, lane) for lane in range(1, lanes)]
+    terms += [shifted(next_part, -1, lane) for lane in range(lanes)]
+    velocity = pl.pallas_call(
+        velocity_kernel,
+        out_shape=jax.ShapeDtypeStruct((3, high_count, BLK), F32),
+        in_specs=[VM] * (1 + len(terms)),
+        out_specs=VM,
+        compiler_params=params(4),
+        name="velocity",
+    )(rate, *terms)
     velocities = [
         velocity if o == 0 else shifted(velocity, o, 0) for o in range(-REACH, REACH + 2)
     ]
@@ -260,10 +304,11 @@
         in_specs=[SM, SM] + [VM] * (len(packs) + len(velocities)),
         out_specs=(VM, VM),
         scratch_shapes=[
-            pltpu.VMEM((blocks, 6, BLK, BLK), F32),
-            pltpu.VMEM((window, 8, BLK), F32),
+            pltpu.VMEM((blocks, BLK, 96), BF16),
+            pltpu.VMEM((window, 96, 3 * BLK), BF16),
             pltpu.VMEM((blocks, BLK, BLK), F32),
         ],
+        compiler_params=params(16),
         name="nearness",
     )(cand_target, cand_source, *packs, *velocities)
     return vel, near.reshape(seg)

time: 57.2 us -> 45.4 us (0.79)
  Pallas kernels: 21.4 us -> 12.7 us
  local copies, waits for them, and re-layouts: 2.82 us -> 0.03 us
    pallas_call x1, Pallas kernels: 14.1 us -> 6.8 us  [local(): pl.pallas_call(functools.partial(force_kernel, lanes, high_count), out_sh...]
    unnamed x28 -> x12, local copies, waits for them, and re-layouts: 1.92 us -> 0.03 us
    pallas_call x1, Pallas kernels: 7.27 us -> 5.84 us  [local(): pl.pallas_call(functools.partial(near_kernel, high_count), out_shape=(jax...]
    concatenate x1 -> x0, local copies, waits for them, and re-layouts: 0.89 us -> none  [local(): jnp.concatenate([centres, seg_lines, burgers, seg_nodes.astype(F32), node...]
where the time goes in v2:
time: 45.4 us; the launch traced here: 45 us
  waiting for transfers between devices  18 us (40%)
  Pallas kernels  12.7 us (28%)
  starting transfers between devices  11.5 us (25%)
  other arithmetic  2.17 us (5%)
  between operations  0.73 us (2%)
    ppermute x12, waiting for transfers between devices, shifted(): return lax.ppermute(block, ('cells', 'lanes'), route)  18 us
    ppermute x12, starting transfers between devices, shifted(): return lax.ppermute(block, ('cells', 'lanes'), route)  11.5 us
    pallas_call x1, Pallas kernels, local(): pl.pallas_call(functools.partial(force_kernel, lanes, high_count), out_sh...  6.8 us
    pallas_call x1, Pallas kernels, local(): pl.pallas_call(functools.partial(near_kernel, high_count), out_shape=(jax...  5.84 us
  transfers between devices with their start and end apart: 12, of which 10 were waited for; matrix products, arithmetic and copies ran while one was open for 0% of the time, Pallas kernels for 0%

profile of v2, /device:TPU:0, one launch (start us, length us, event | category | flops | bytes accessed | tf_op | source)
XLA Modules:
  0.0 45.0 jit_solution(7971363151667824192)
XLA Ops:
  0.6 0.0 copy-start.4
  0.6 0.0 copy-start.5
  0.7 0.7 %convert_element_type.16 = f32[2,1024]{1,0:T(2,128)S(1)} convert(s32[2,1024]{1,0:T(2,128)} %param.13) | non-fusion elementwise | flops 2048 | bytes 16384 | tf_op jit(solution)/shard_map/convert_element_type | solution.py:260
  1.4 0.7 %convert_element_type.17 = f32[2,1024]{1,0:T(2,128)S(1)} convert(s32[2,1024]{1,0:T(2,128)} %param.14) | non-fusion elementwise | flops 2048 | bytes 16384 | tf_op jit(solution)/shard_map/convert_element_type | solution.py:260
  2.1 0.0 copy-done.4
  2.1 0.0 copy-done.5
  2.1 0.0 copy-start.1
  2.1 0.8 %pad_add_fusion.refs_2_ = f32[13,1024]{1,0:T(8,128)S(1)} fusion(f32[2,1024]{1,0:T(2,128)S(1)} %convert_element_type.17, f32[2,1024]{1,0:T(2,128)S(1)} %convert_element_type.16, f32[3,1024]{1,0:T(4,128)S(1)} %copy-done.4, f32[3,1024]{1,0:T(4,128)S(1)} %copy-done.5, f32[3,1024]{1,0:T(4,128)} %param.9), kind=kLoop, calls=%fused_computation | loop fusion | flops 53248 | bytes 106496 | tf_op jit(solution)/shard_map/add | solution.py:265
  2.8 6.1 %collective-permute-start.3 = (f32[13,1024]{1,0:T(8,128)S(1)}, f32[13,1024]{1,0:T(8,128)S(1)}, u32[]{:S(2)}, u32[]{:S(2)}) collective-permute-start(f32[13,1024]{1,0:T(8,128)S(1)} %pad_add_fusion.refs_2_), channel_id=1, source_target_pairs={{4,0},{5,1},{6,2},{7,3},{8,4},{9,5},{10,6},{11,7},{12,8},{13,9},{1... | collective-permute-start | bytes 159752 | tf_op jit(solution)/shard_map/ppermute | solution.py:34
  8.9 0.0 collective-permute-start.2
  8.9 0.5 %collective-permute-start.1 = (f32[13,1024]{1,0:T(8,128)S(1)}, f32[13,1024]{1,0:T(8,128)S(1)}, u32[]{:S(2)}, u32[]{:S(2)}) collective-permute-start(f32[13,1024]{1,0:T(8,128)S(1)} %pad_add_fusion.refs_2_), channel_id=1, source_target_pairs={{30,0},{31,1},{0,2},{1,3},{2,4},{3,5},{4,6},{5,7},{6,8},{7,9},{8,1... | collective-permute-start | bytes 159752 | tf_op jit(solution)/shard_map/ppermute | solution.py:34
  9.4 0.7 %collective-permute-start = (f32[13,1024]{1,0:T(8,128)S(1)}, f32[13,1024]{1,0:T(8,128)S(1)}, u32[]{:S(2)}, u32[]{:S(2)}) collective-permute-start(f32[13,1024]{1,0:T(8,128)S(1)} %pad_add_fusion.refs_2_), channel_id=1, source_target_pairs={{28,0},{29,1},{30,2},{31,3},{0,4},{1,5},{2,6},{3,7},{4,8},{5,9},{6... | collective-permute-start | bytes 159752 | tf_op jit(solution)/shard_map/ppermute | solution.py:34
  10.1 0.7 %collective-permute-done.3.refs_4_ = f32[13,1024]{1,0:T(8,128)S(1)} collective-permute-done((f32[13,1024]{1,0:T(8,128)S(1)}, f32[13,1024]{1,0:T(8,128)S(1)}, u32[]{:S(2)}, u32[]{:S(2)}) %collective-permute-start.3) | collective-permute-done | bytes 53280 | tf_op jit(solution)/shard_map/ppermute | solution.py:34
  10.8 0.6 %collective-permute-done.2.refs_3_ = f32[13,1024]{1,0:T(8,128)S(1)} collective-permute-done((f32[13,1024]{1,0:T(8,128)S(1)}, f32[13,1024]{1,0:T(8,128)S(1)}, u32[]{:S(2)}, u32[]{:S(2)}) %collective-permute-start.2) | collective-permute-done | bytes 53280 | tf_op jit(solution)/shard_map/ppermute | solution.py:34
  11.4 3.9 %collective-permute-done.1.refs_1_ = f32[13,1024]{1,0:T(8,128)S(1)} collective-permute-done((f32[13,1024]{1,0:T(8,128)S(1)}, f32[13,1024]{1,0:T(8,128)S(1)}, u32[]{:S(2)}, u32[]{:S(2)}) %collective-permute-start.1) | collective-permute-done | bytes 53280 | tf_op jit(solution)/shard_map/ppermute | solution.py:34
  15.3 1.6 %collective-permute-done.refs_0_ = f32[13,1024]{1,0:T(8,128)S(1)} collective-permute-done((f32[13,1024]{1,0:T(8,128)S(1)}, f32[13,1024]{1,0:T(8,128)S(1)}, u32[]{:S(2)}, u32[]{:S(2)}) %collective-permute-start) | collective-permute-done | bytes 53280 | tf_op jit(solution)/shard_map/ppermute | solution.py:34
  16.9 0.0 copy-done.1
  16.9 6.8 %forces.1 = (f32[4,8,128]{2,1,0:T(8,128)S(1)}, f32[4,8,128]{2,1,0:T(8,128)S(1)}) custom-call(s32[8,8]{1,0:T(8,128)S(1)} %copy-done.1, f32[13,1024]{1,0:T(8,128)S(1)} %collective-permute-done.refs_0_, f32[13,1024]{1,0:T(8,128)S(1)} %collective-permute-done.1.refs_1_, f32[13,1024]{1,0:T(8,128)S(1)} %pad_add_fusion.refs_2_, ...), custom_call_target="tpu_custom_call" | custom-call | tf_op jit(solution)/shard_map/forces/pallas_call | solution.py:270
  23.7 0.0 copy-start
  23.7 1.6 %collective-permute-start.4 = (f32[4,8,128]{2,1,0:T(8,128)S(1)}, f32[4,8,128]{2,1,0:T(8,128)S(1)}, u32[]{:S(2)}, u32[]{:S(2)}) collective-permute-start(f32[4,8,128]{2,1,0:T(8,128)S(1)} %get-tuple-element.6.refs_0_), channel_id=1, source_target_pairs={{1,0},{0,1},{3,2},{2,3},{5,4},{4,5},{7,6},{6,7},{9,8},{8,9},{11,10... | collective-permute-start | bytes 49160 | tf_op jit(solution)/shard_map/ppermute | solution.py:34
  25.3 0.0 collective-permute-start.6
  25.3 0.0 collective-permute-start.5
  25.3 2.2 %collective-permute-done.4.refs_1_ = f32[4,8,128]{2,1,0:T(8,128)S(1)} collective-permute-done((f32[4,8,128]{2,1,0:T(8,128)S(1)}, f32[4,8,128]{2,1,0:T(8,128)S(1)}, u32[]{:S(2)}, u32[]{:S(2)}) %collective-permute-start.4) | collective-permute-done | bytes 16416 | tf_op jit(solution)/shard_map/ppermute | solution.py:34
  27.6 4.5 %collective-permute-done.6.refs_3_ = f32[4,8,128]{2,1,0:T(8,128)S(1)} collective-permute-done((f32[4,8,128]{2,1,0:T(8,128)S(1)}, f32[4,8,128]{2,1,0:T(8,128)S(1)}, u32[]{:S(2)}, u32[]{:S(2)}) %collective-permute-start.6) | collective-permute-done | bytes 16416 | tf_op jit(solution)/shard_map/ppermute | solution.py:34
  32.1 0.0 collective-permute-done.5.refs_2_
  32.1 0.0 copy-done
  32.1 0.0 copy-start.2
  32.1 0.0 copy-start.3
  32.1 0.1 collective-permute-start.11
  32.2 0.1 collective-permute-start.10
  32.2 0.1 collective-permute-start.9
  32.3 0.5 %collective-permute-start.8 = (f32[3,8,128]{2,1,0:T(8,128)S(1)}, f32[3,8,128]{2,1,0:T(8,128)S(1)}, u32[]{:S(2)}, u32[]{:S(2)}) collective-permute-start(f32[3,8,128]{2,1,0:T(8,128)S(1)} %velocity.1.refs_7_), channel_id=1, source_target_pairs={{30,0},{31,1},{0,2},{1,3},{2,4},{3,5},{4,6},{5,7},{6,8},{7,9},{8,1... | collective-permute-start | bytes 36872 | tf_op jit(solution)/shard_map/ppermute | solution.py:34
  32.8 2.0 %collective-permute-start.7 = (f32[3,8,128]{2,1,0:T(8,128)S(1)}, f32[3,8,128]{2,1,0:T(8,128)S(1)}, u32[]{:S(2)}, u32[]{:S(2)}) collective-permute-start(f32[3,8,128]{2,1,0:T(8,128)S(1)} %velocity.1.refs_7_), channel_id=1, source_target_pairs={{28,0},{29,1},{30,2},{31,3},{0,4},{1,5},{2,6},{3,7},{4,8},{5,9},{6... | collective-permute-start | bytes 36872 | tf_op jit(solution)/shard_map/ppermute | solution.py:34
  34.8 0.5 %collective-permute-done.11.refs_10_ = f32[3,8,128]{2,1,0:T(8,128)S(1)} collective-permute-done((f32[3,8,128]{2,1,0:T(8,128)S(1)}, f32[3,8,128]{2,1,0:T(8,128)S(1)}, u32[]{:S(2)}, u32[]{:S(2)}) %collective-permute-start.11) | collective-permute-done | bytes 12320 | tf_op jit(solution)/shard_map/ppermute | solution.py:34
  35.3 0.6 %collective-permute-done.10.refs_9_ = f32[3,8,128]{2,1,0:T(8,128)S(1)} collective-permute-done((f32[3,8,128]{2,1,0:T(8,128)S(1)}, f32[3,8,128]{2,1,0:T(8,128)S(1)}, u32[]{:S(2)}, u32[]{:S(2)}) %collective-permute-start.10) | collective-permute-done | bytes 12320 | tf_op jit(solution)/shard_map/ppermute | solution.py:34
  35.9 0.0 collective-permute-done.9.refs_8_
  35.9 2.2 %collective-permute-done.8.refs_6_ = f32[3,8,128]{2,1,0:T(8,128)S(1)} collective-permute-done((f32[3,8,128]{2,1,0:T(8,128)S(1)}, f32[3,8,128]{2,1,0:T(8,128)S(1)}, u32[]{:S(2)}, u32[]{:S(2)}) %collective-permute-start.8) | collective-permute-done | bytes 12320 | tf_op jit(solution)/shard_map/ppermute | solution.py:34
  38.2 1.0 %collective-permute-done.7.refs_5_ = f32[3,8,128]{2,1,0:T(8,128)S(1)} collective-permute-done((f32[3,8,128]{2,1,0:T(8,128)S(1)}, f32[3,8,128]{2,1,0:T(8,128)S(1)}, u32[]{:S(2)}, u32[]{:S(2)}) %collective-permute-start.7) | collective-permute-done | bytes 12320 | tf_op jit(solution)/shard_map/ppermute | solution.py:34
  39.2 0.0 copy-done.2
  39.2 0.0 copy-done.3
  39.2 5.8 %nearness.1 = (f32[8,128]{1,0:T(8,128)}, f32[3,1024]{1,0:T(4,128)}) custom-call(s32[32]{0:T(128)S(1)} %copy-done.2, s32[32]{0:T(128)S(1)} %copy-done.3, f32[13,1024]{1,0:T(8,128)S(1)} %collective-permute-done.refs_0_, f32[13,1024]{1,0:T(8,128)S(1)} %collective-permute-done.1.refs_1_, f32[13,1024]{1,0:T(8,128)S(1)} %pad_add_fusion.refs_2_, ...), custom_call_target="tpu_custom_call" | custom-call | tf_op jit(solution)/shard_map/nearness/pallas_call | solution.py:298
  (1 shorter events, 0.0 us)
Async XLA Ops:
  0.6 1.4 %copy-start.4 = (f32[3,1024]{1,0:T(4,128)S(1)}, f32[3,1024]{1,0:T(4,128)}, u32[]{:S(2)}) copy-start(f32[3,1024]{1,0:T(4,128)} %param.11) | copy-start | bytes 36868
  0.6 1.4 %copy-start.5 = (f32[3,1024]{1,0:T(4,128)S(1)}, f32[3,1024]{1,0:T(4,128)}, u32[]{:S(2)}) copy-start(f32[3,1024]{1,0:T(4,128)} %param.10) | copy-start | bytes 36868
  2.1 14.9 %copy-start.1 = (s32[8,8]{1,0:T(8,128)S(1)}, s32[8,8]{1,0:T(8,128)}, u32[]{:S(2)}) copy-start(s32[8,8]{1,0:T(8,128)} %lists.1) | copy-start | bytes 772
  2.8 8.0 %collective-permute-start.3 = (f32[13,1024]{1,0:T(8,128)S(1)}, f32[13,1024]{1,0:T(8,128)S(1)}, u32[]{:S(2)}, u32[]{:S(2)}) collective-permute-start(f32[13,1024]{1,0:T(8,128)S(1)} %pad_add_fusion.refs_2_), channel_id=1, source_target_pairs={{4,0},{5,1},{6,2},{7,3},{8,4},{9,5},{10,6},{11,7},{12,8},{13,9},{1... | collective-permute-start | bytes 159752 | tf_op jit(solution)/shard_map/ppermute | solution.py:34
  8.9 2.5 %collective-permute-start.2 = (f32[13,1024]{1,0:T(8,128)S(1)}, f32[13,1024]{1,0:T(8,128)S(1)}, u32[]{:S(2)}, u32[]{:S(2)}) collective-permute-start(f32[13,1024]{1,0:T(8,128)S(1)} %pad_add_fusion.refs_2_), channel_id=1, source_target_pairs={{2,0},{3,1},{4,2},{5,3},{6,4},{7,5},{8,6},{9,7},{10,8},{11,9},{12,... | collective-permute-start | bytes 159752 | tf_op jit(solution)/shard_map/ppermute | solution.py:34
  8.9 6.4 %collective-permute-start.1 = (f32[13,1024]{1,0:T(8,128)S(1)}, f32[13,1024]{1,0:T(8,128)S(1)}, u32[]{:S(2)}, u32[]{:S(2)}) collective-permute-start(f32[13,1024]{1,0:T(8,128)S(1)} %pad_add_fusion.refs_2_), channel_id=1, source_target_pairs={{30,0},{31,1},{0,2},{1,3},{2,4},{3,5},{4,6},{5,7},{6,8},{7,9},{8,1... | collective-permute-start | bytes 159752 | tf_op jit(solution)/shard_map/ppermute | solution.py:34
  9.4 7.5 %collective-permute-start = (f32[13,1024]{1,0:T(8,128)S(1)}, f32[13,1024]{1,0:T(8,128)S(1)}, u32[]{:S(2)}, u32[]{:S(2)}) collective-permute-start(f32[13,1024]{1,0:T(8,128)S(1)} %pad_add_fusion.refs_2_), channel_id=1, source_target_pairs={{28,0},{29,1},{30,2},{31,3},{0,4},{1,5},{2,6},{3,7},{4,8},{5,9},{6... | collective-permute-start | bytes 159752 | tf_op jit(solution)/shard_map/ppermute | solution.py:34
  23.7 8.3 %copy-start = (f32[1024]{0:T(1024)S(1)}, f32[1024]{0:T(1024)}, u32[]{:S(2)}) copy-start(f32[1024]{0:T(1024)} %param.15) | copy-start | bytes 12292
  23.7 3.8 %collective-permute-start.4 = (f32[4,8,128]{2,1,0:T(8,128)S(1)}, f32[4,8,128]{2,1,0:T(8,128)S(1)}, u32[]{:S(2)}, u32[]{:S(2)}) collective-permute-start(f32[4,8,128]{2,1,0:T(8,128)S(1)} %get-tuple-element.6.refs_0_), channel_id=1, source_target_pairs={{1,0},{0,1},{3,2},{2,3},{5,4},{4,5},{7,6},{6,7},{9,8},{8,9},{11,10... | collective-permute-start | bytes 49160 | tf_op jit(solution)/shard_map/ppermute | solution.py:34
  25.3 6.8 %collective-permute-start.6 = (f32[4,8,128]{2,1,0:T(8,128)S(1)}, f32[4,8,128]{2,1,0:T(8,128)S(1)}, u32[]{:S(2)}, u32[]{:S(2)}) collective-permute-start(f32[4,8,128]{2,1,0:T(8,128)S(1)} %get-tuple-element.7), channel_id=1, source_target_pairs={{31,0},{30,1},{1,2},{0,3},{3,4},{2,5},{5,6},{4,7},{7,8},{6,9},{9,1... | collective-permute-start | bytes 49160 | tf_op jit(solution)/shard_map/ppermute | solution.py:34
  25.3 6.8 %collective-permute-start.5 = (f32[4,8,128]{2,1,0:T(8,128)S(1)}, f32[4,8,128]{2,1,0:T(8,128)S(1)}, u32[]{:S(2)}, u32[]{:S(2)}) collective-permute-start(f32[4,8,128]{2,1,0:T(8,128)S(1)} %get-tuple-element.7), channel_id=1, source_target_pairs={{30,0},{31,1},{0,2},{1,3},{2,4},{3,5},{4,6},{5,7},{6,8},{7,9},{8,1... | collective-permute-start | bytes 49160 | tf_op jit(solution)/shard_map/ppermute | solution.py:34
  32.1 7.1 %copy-start.2 = (s32[32]{0:T(128)S(1)}, s32[32]{0:T(128)}, u32[]{:S(2)}) copy-start(s32[32]{0:T(128)} %targets.1) | copy-start | bytes 388
  32.1 7.1 %copy-start.3 = (s32[32]{0:T(128)S(1)}, s32[32]{0:T(128)}, u32[]{:S(2)}) copy-start(s32[32]{0:T(128)} %sources.1) | copy-start | bytes 388
  32.1 3.2 %collective-permute-start.11 = (f32[3,8,128]{2,1,0:T(8,128)S(1)}, f32[3,8,128]{2,1,0:T(8,128)S(1)}, u32[]{:S(2)}, u32[]{:S(2)}) collective-permute-start(f32[3,8,128]{2,1,0:T(8,128)S(1)} %velocity.1.refs_7_), channel_id=1, source_target_pairs={{6,0},{7,1},{8,2},{9,3},{10,4},{11,5},{12,6},{13,7},{14,8},{15,9},... | collective-permute-start | bytes 36872 | tf_op jit(solution)/shard_map/ppermute | solution.py:34
  32.2 3.7 %collective-permute-start.10 = (f32[3,8,128]{2,1,0:T(8,128)S(1)}, f32[3,8,128]{2,1,0:T(8,128)S(1)}, u32[]{:S(2)}, u32[]{:S(2)}) collective-permute-start(f32[3,8,128]{2,1,0:T(8,128)S(1)} %velocity.1.refs_7_), channel_id=1, source_target_pairs={{4,0},{5,1},{6,2},{7,3},{8,4},{9,5},{10,6},{11,7},{12,8},{13,9},{1... | collective-permute-start | bytes 36872 | tf_op jit(solution)/shard_map/ppermute | solution.py:34
  32.2 3.7 %collective-permute-start.9 = (f32[3,8,128]{2,1,0:T(8,128)S(1)}, f32[3,8,128]{2,1,0:T(8,128)S(1)}, u32[]{:S(2)}, u32[]{:S(2)}) collective-permute-start(f32[3,8,128]{2,1,0:T(8,128)S(1)} %velocity.1.refs_7_), channel_id=1, source_target_pairs={{2,0},{3,1},{4,2},{5,3},{6,4},{7,5},{8,6},{9,7},{10,8},{11,9},{12,... | collective-permute-start | bytes 36872 | tf_op jit(solution)/shard_map/ppermute | solution.py:34
  32.3 5.9 %collective-permute-start.8 = (f32[3,8,128]{2,1,0:T(8,128)S(1)}, f32[3,8,128]{2,1,0:T(8,128)S(1)}, u32[]{:S(2)}, u32[]{:S(2)}) collective-permute-start(f32[3,8,128]{2,1,0:T(8,128)S(1)} %velocity.1.refs_7_), channel_id=1, source_target_pairs={{30,0},{31,1},{0,2},{1,3},{2,4},{3,5},{4,6},{5,7},{6,8},{7,9},{8,1... | collective-permute-start | bytes 36872 | tf_op jit(solution)/shard_map/ppermute | solution.py:34
  32.8 6.4 %collective-permute-start.7 = (f32[3,8,128]{2,1,0:T(8,128)S(1)}, f32[3,8,128]{2,1,0:T(8,128)S(1)}, u32[]{:S(2)}, u32[]{:S(2)}) collective-permute-start(f32[3,8,128]{2,1,0:T(8,128)S(1)} %velocity.1.refs_7_), channel_id=1, source_target_pairs={{28,0},{29,1},{30,2},{31,3},{0,4},{1,5},{2,6},{3,7},{4,8},{5,9},{6... | collective-permute-start | bytes 36872 | tf_op jit(solution)/shard_map/ppermute | solution.py:34

commit v3 on v2

v3 whole, which is shorter than its diff:
```python
import functools
import math

import jax
import jax.numpy as jnp
from jax import lax
from jax.experimental import pallas as pl
from jax.experimental.pallas import tpu as pltpu
from jax.sharding import PartitionSpec as P

BLK = 128
REACH = 2
FORCE_SCALE = 0.02
CORE_SQUARE = 0.25
TIME_STEP = 4.0
MIDDLE = 2.0

F32 = jnp.float32
BF16 = jnp.bfloat16
VM = pl.BlockSpec(memory_space=pltpu.VMEM)
SM = pl.BlockSpec(memory_space=pltpu.SMEM)


def params(mib):
    return pltpu.CompilerParams(vmem_limit_bytes=mib << 20)


def shifted(block, cell_step, lane_step):
    cells, lanes = lax.axis_size("cells"), lax.axis_size("lanes")
    route = []
    for c in range(cells):
        for l in range(lanes):
            source = ((c + cell_step) % cells) * lanes + (l + lane_step) % lanes
            route.append((source, c * lanes + l))
    return lax.ppermute(block, ("cells", "lanes"), route)


def split3(x):
    high = x.astype(BF16).astype(F32)
    rest = x - high
    mid = rest.astype(BF16).astype(F32)
    return high, mid, rest - mid


def cross_rows(a, b):
    return jnp.concatenate(
        [
            a[1:2] * b[2:3] - a[2:3] * b[1:2],
            a[2:3] * b[0:1] - a[0:1] * b[2:3],
            a[0:1] * b[1:2] - a[1:2] * b[0:1],
        ],
        0,
    )


def contract_lanes(a, b):
    return lax.dot_general(a, b, (((1,), (1,)), ((), ())), preferred_element_type=F32)


def end_address(pack, end, high_count):
    node = pack[16 + end : 17 + end].astype(jnp.int32)
    owner = pack[18 + end : 19 + end].astype(jnp.int32)
    return owner * high_count + node // BLK, node % BLK


def six_left(x):
    h, m, l = split3(x)
    return jnp.concatenate([h, h, m, h, l, m], 0)


def six_right(x):
    h, m, l = split3(x)
    return jnp.concatenate([h, m, h, l, h, m], 0)


def pack_kernel(fields, out):
    seg = fields.shape[1]
    centre = fields[0:3] - MIDDLE
    line = fields[3:6]
    out[0:3] = -2.0 * centre
    out[3:4] = jnp.sum(centre * centre, axis=0, keepdims=True)
    out[4:5] = jnp.ones((1, seg), F32)
    out[5:8] = fields[6:9]
    out[8:11] = line
    out[11:14] = cross_rows(line, centre)
    out[14:16] = jnp.zeros((2, seg), F32)
    out[16:20] = fields[9:13]
    out[20:24] = jnp.zeros((4, seg), F32)


def low_onehot(low):
    rows = lax.broadcasted_iota(jnp.int32, (BLK, low.shape[1]), 0)
    return (rows == low).astype(F32).astype(BF16)


def early_kernel(high_count, own, *refs):
    count = (len(refs) - 2) // 2
    for source, out in zip(refs[:count], refs[count : 2 * count]):
        out[...] = source[...]
    lhs_out, onehots = refs[2 * count :]
    pack = own[...]
    target = jnp.concatenate(
        [-0.5 * pack[0:3], pack[4:5], pack[3:4] + CORE_SQUARE, pack[8:11]], 0
    )
    six = six_left(target)
    for k in range(own.shape[1] // BLK):
        lhs_out[k] = six[:, k * BLK : (k + 1) * BLK].T.astype(BF16)
    for end in range(2):
        onehots[end] = low_onehot(end_address(pack, end, high_count)[1])


def force_kernel(lanes, high_count, lists, lhs_s, onehots, *refs):
    packs = refs[: 2 * REACH + 1]
    own_out, next_out, rhs_s, src_s, force_s = refs[2 * REACH + 1 :]
    seg = packs[0].shape[1]
    blocks = seg // BLK
    rows = lax.broadcasted_iota(jnp.int32, (8, seg), 0)

    for d, ref in enumerate(packs):
        source = ref[0:8]
        h, m, l = split3(source)
        near = [jnp.where(rows < 5, x, 0.0) for x in (h, m, l)]
        along = [jnp.where(rows < 5, 0.0, x) for x in (h, m, l)]
        near6, along6 = [
            jnp.concatenate([x[0], x[1], x[0], x[2], x[0], x[1]], 0).astype(BF16)
            for x in (near, along)
        ]
        sums = split3(ref[8:16])
        sums3 = jnp.concatenate([*sums, jnp.zeros((8, seg), F32)], 0).astype(BF16)
        for k in range(blocks):
            cut = slice(k * BLK, (k + 1) * BLK)
            rhs_s[d * blocks + k, :, 0:BLK] = near6[:, cut]
            rhs_s[d * blocks + k, :, BLK : 2 * BLK] = along6[:, cut]
            src_s[d * blocks + k] = sums3[:, cut]
    own = packs[REACH]

    def one_target(t, carry):
        lhs = lhs_s[t]
        highs, lows, srcs = [], [], []
        for e in range(lists.shape[1]):
            w = lists[t, e]
            both = jnp.dot(lhs, rhs_s[w], preferred_element_type=F32)
            inverse = lax.rsqrt(both[:, :BLK])
            weight = both[:, BLK:] * inverse * (inverse * inverse)
            high = weight.astype(BF16)
            highs.append(high)
            lows.append((weight - high.astype(F32)).astype(BF16))
            srcs.append(src_s[w])
        src = jnp.concatenate(srcs, 1)
        total = contract_lanes(jnp.concatenate(highs, 1), src)
        total = total + contract_lanes(jnp.concatenate(lows, 1), src)
        total = total.T
        force_s[t] = total[0:8] + (total[8:16] + total[16:24])
        return carry

    lax.fori_loop(0, blocks, one_target, 0, unroll=math.gcd(blocks, 4))

    whole = jnp.concatenate([force_s[t] for t in range(blocks)], 1)
    centre = -0.5 * own[0:3]
    line = own[8:11]
    force = (0.5 * FORCE_SCALE) * (cross_rows(whole[0:3], centre) - whole[3:6])
    length = jnp.sqrt(jnp.sum(line * line, axis=0, keepdims=True)) * (0.5 / lanes)
    parts = split3(jnp.concatenate([force, length], 0))
    rows16 = lax.broadcasted_iota(jnp.int32, (2 * high_count, seg), 0)
    pack = own[...]
    out = None
    for end in range(2):
        mask = rows16 == end_address(pack, end, high_count)[0]
        lhs = jnp.concatenate(
            [
                jnp.where(mask, part[k : k + 1], 0.0)
                for part in parts
                for k in range(4)
            ],
            0,
        ).astype(BF16)
        term = contract_lanes(lhs, onehots[end])
        out = term if out is None else out + term
    n = 8 * high_count
    out = out[0:n] + (out[n : 2 * n] + out[2 * n : 3 * n])
    for k in range(4):
        first = 2 * high_count * k
        own_out[k] = out[first : first + high_count]
        next_out[k] = out[first + high_count : first + 2 * high_count]


def select_kernel(high_count, *refs):
    packs, (onehots, centre_out) = refs[:-2], refs[-2:]
    seg = packs[0].shape[1]
    blocks = seg // BLK
    rows = lax.broadcasted_iota(jnp.int32, (8, seg), 0)
    for d, ref in enumerate(packs):
        pack = ref[...]
        if d != REACH:
            slot = 2 * (d if d < REACH else d - 1)
            for end in range(2):
                onehots[slot + end] = low_onehot(end_address(pack, end, high_count)[1])
        near = six_right(jnp.where(rows < 5, pack[0:8], 0.0)).astype(BF16)
        for k in range(blocks):
            centre_out[d * blocks + k] = near[:, k * BLK : (k + 1) * BLK]


def near_kernel(high_count, targets, sources, own_onehots, onehots, centre_s, *refs):
    packs = refs[: 2 * REACH + 1]
    velocities = refs[2 * REACH + 1 : 4 * REACH + 3]
    near_out, vel_out, tgt_s, src_s, acc_s = refs[4 * REACH + 3 :]
    seg = packs[0].shape[1]
    blocks = seg // BLK
    rows8 = lax.broadcasted_iota(jnp.int32, (high_count, seg), 0)

    for k in range(high_count):
        for x in range(3):
            vel_out[x : x + 1, k * BLK : (k + 1) * BLK] = velocities[REACH][x, k : k + 1, :]

    one = jnp.ones((1, seg), F32)

    def zero(n):
        return jnp.zeros((n, seg), F32)

    for d, ref in enumerate(packs):
        pack = ref[...]
        table = jnp.concatenate(
            [velocities[d][x] for x in range(3)] + [velocities[d + 1][x] for x in range(3)], 0
        )
        top = table.astype(BF16).astype(F32)
        lhs = jnp.concatenate([top, table - top], 0).astype(BF16)
        n = 6 * high_count
        picked = [None] * 3
        for end in range(2):
            high = end_address(pack, end, high_count)[0]
            slot = 2 * (d if d < REACH else d - 1) + end
            onehot = own_onehots[end] if d == REACH else onehots[slot]
            got = jnp.dot(lhs, onehot, preferred_element_type=F32)
            got = got[0:n] + got[n : 2 * n]
            for owner in range(2):
                mask = rows8 + owner * high_count == high
                for x in range(3):
                    first = (3 * owner + x) * high_count
                    term = jnp.where(mask, got[first : first + high_count], 0.0)
                    picked[x] = term if picked[x] is None else picked[x] + term
        motion = jnp.concatenate(
            [jnp.sum(p, axis=0, keepdims=True) * (0.5 * TIME_STEP) for p in picked], 0
        )
        centre = -0.5 * pack[0:3]
        vv = jnp.sum(motion * motion, axis=0, keepdims=True)
        cv = jnp.sum(centre * motion, axis=0, keepdims=True)
        columns = [
            [[-motion, cv, zero(4)], [-centre, zero(1), one, zero(3)]],
            [[zero(3), vv, zero(4)], [-2.0 * motion, one, zero(4)]],
        ]
        for n, pair in enumerate(columns):
            six = jnp.concatenate(
                [six_right(jnp.concatenate(rows, 0)) for rows in pair], 0
            ).astype(BF16)
            for k in range(blocks):
                src_s[d * blocks + k, :, n * BLK : (n + 1) * BLK] = six[:, k * BLK : (k + 1) * BLK]
        if d == REACH:
            six = jnp.concatenate(
                [
                    six_left(jnp.concatenate([centre, one, pack[3:4], zero(3)], 0)),
                    six_left(jnp.concatenate([motion, vv, cv, zero(3)], 0)),
                ],
                0,
            )
            for k in range(blocks):
                tgt_s[k] = six[:, k * BLK : (k + 1) * BLK].T.astype(BF16)

    acc_s[...] = jnp.zeros_like(acc_s)
    count = targets.shape[1]
    group = max(g for g in (1, 2, 4, 8, 16) if count % g == 0)

    def some_pairs(step, carry):
        for u in range(group):
            k = step * group + u
            t = targets[0, k]
            w = sources[0, k]
            target = tgt_s[t]
            rr = jnp.dot(target[:, 0:48], centre_s[w], preferred_element_type=F32)
            both = jnp.dot(target, src_s[w], preferred_element_type=F32)
            rv = both[:, 0:BLK]
            vv = jnp.maximum(both[:, BLK : 2 * BLK], 0.0)
            s = jnp.clip(-rv / (vv + CORE_SQUARE), 0.0, 1.0)
            acc_s[t] += jnp.exp(-(rr + s * (2.0 * rv + s * vv)))
        return carry

    lax.fori_loop(0, count // group, some_pairs, 0)

    ones = jnp.ones((8, BLK), BF16)
    for t in range(blocks):
        total = acc_s[t]
        high = total.astype(BF16)
        low = (total - high.astype(F32)).astype(BF16)
        near_out[t : t + 1] = (contract_lanes(ones, high) + contract_lanes(ones, low))[0:1]


def velocity_kernel(mobility, *refs):
    out = refs[-1]
    total = refs[0][...]
    for ref in refs[1:-1]:
        total = total + ref[...]
    scale = mobility[...] / (1.0 + total[3])
    for x in range(3):
        out[x] = total[x] * scale


def rows_of(pieces, first, rows):
    total = None
    for piece in pieces:
        last = first + piece.shape[0]
        padded = jnp.pad(piece, ((first, rows - last), (0, 0)))
        total = padded if total is None else total + padded
        first = last
    return total


def local(
    centres, seg_lines, burgers, neighbour_blocks, seg_nodes, node_owner, mobility, cand_target, cand_source
):
    seg = centres.shape[1]
    blocks = seg // BLK
    high_count = mobility.shape[0] // BLK
    lanes = lax.axis_size("lanes")
    window = (2 * REACH + 1) * blocks
    fields = rows_of([centres, seg_lines, burgers], 0, 13)
    fields = fields + rows_of([seg_nodes, node_owner], 9, 13).astype(F32)
    own = pl.pallas_call(
        pack_kernel,
        out_shape=jax.ShapeDtypeStruct((24, seg), F32),
        in_specs=[VM],
        out_specs=VM,
        compiler_params=params(4),
        name="pack",
    )(fields)
    packs = [own if o == 0 else shifted(own, o, 0) for o in range(-REACH, REACH + 1)]
    small = [
        neighbour_blocks,
        mobility.reshape(high_count, BLK),
        cand_target.reshape(1, -1),
        cand_source.reshape(1, -1),
    ]
    lists, rate, targets, sources, lhs, own_onehots = pl.pallas_call(
        functools.partial(early_kernel, high_count),
        out_shape=[jax.ShapeDtypeStruct(x.shape, x.dtype) for x in small]
        + [
            jax.ShapeDtypeStruct((blocks, BLK, 48), BF16),
            jax.ShapeDtypeStruct((2, BLK, seg), BF16),
        ],
        in_specs=[VM] * (1 + len(small)),
        out_specs=[VM] * (2 + len(small)),
        compiler_params=params(8),
        cost_estimate=pl.CostEstimate(flops=1 << 28, bytes_accessed=1 << 23, transcendentals=0),
        name="early",
    )(own, *small)
    part = jax.ShapeDtypeStruct((4, high_count, BLK), F32)
    own_part, next_part = pl.pallas_call(
        functools.partial(force_kernel, lanes, high_count),
        out_shape=(part, part),
        in_specs=[SM] + [VM] * (2 + len(packs)),
        out_specs=(VM, VM),
        scratch_shapes=[
            pltpu.VMEM((window, 48, 2 * BLK), BF16),
            pltpu.VMEM((window, 32, BLK), BF16),
            pltpu.VMEM((blocks, 8, BLK), F32),
        ],
        compiler_params=params(16),
        name="forces",
    )(lists, lhs, own_onehots, *packs)
    terms = [own_part]
    terms += [shifted(own_part, 0, lane) for lane in range(1, lanes)]
    terms += [shifted(next_part, -1, lane) for lane in range(lanes)]
    velocity = pl.pallas_call(
        velocity_kernel,
        out_shape=jax.ShapeDtypeStruct((3, high_count, BLK), F32),
        in_specs=[VM] * (1 + len(terms)),
        out_specs=VM,
        compiler_params=params(4),
        name="velocity",
    )(rate, *terms)
    velocities = [
        velocity if o == 0 else shifted(velocity, o, 0) for o in range(-REACH, REACH + 2)
    ]
    onehots, near_sources = pl.pallas_call(
        functools.partial(select_kernel, high_count),
        out_shape=(
            jax.ShapeDtypeStruct((2 * len(packs) - 2, BLK, seg), BF16),
            jax.ShapeDtypeStruct((window, 48, BLK), BF16),
        ),
        in_specs=[VM] * len(packs),
        out_specs=(VM, VM),
        compiler_params=params(16),
        cost_estimate=pl.CostEstimate(flops=1 << 28, bytes_accessed=1 << 23, transcendentals=0),
        name="select",
    )(*packs)
    near, vel = pl.pallas_call(
        functools.partial(near_kernel, high_count),
        out_shape=(
            jax.ShapeDtypeStruct((blocks, BLK), F32),
            jax.ShapeDtypeStruct((3, high_count * BLK), F32),
        ),
        in_specs=[SM, SM] + [VM] * (3 + len(packs) + len(velocities)),
        out_specs=(VM, VM),
        scratch_shapes=[
            pltpu.VMEM((blocks, BLK, 96), BF16),
            pltpu.VMEM((window, 96, 2 * BLK), BF16),
            pltpu.VMEM((blocks, BLK, BLK), F32),
        ],
        compiler_params=params(16),
        name="nearness",
    )(targets, sources, own_onehots, onehots, near_sources, *packs, *velocities)
    return vel, near.reshape(seg)


def solution(mesh):
    in_specs = (
        P(None, "cells"),
        P(None, "cells"),
        P(None, "cells"),
        P("cells", "lanes"),
        P(None, "cells"),
        P(None, "cells"),
        P("cells"),
        P("cells"),
        P("cells"),
    )
    out_specs = (P(None, "cells"), P("cells"))
    return jax.shard_map(local, mesh=mesh, in_specs=in_specs, out_specs=out_specs, check_vma=False)
```

time: 45.4 us -> 40.6 us (0.89)
  Pallas kernels: 12.7 us -> 9.23 us
  waiting for transfers between devices: 18 us -> 15.3 us
  local copies, waits for them, and re-layouts: 0.03 us -> 2.68 us
  other arithmetic: 2.17 us -> 0.82 us
    ppermute x12, waiting for transfers between devices: 18 us -> 15.3 us  [shifted(): return lax.ppermute(block, ('cells', 'lanes'), route)]
    unnamed x12 -> x8, local copies, waits for them, and re-layouts: 0.03 us -> 2.68 us
    pallas_call x1, Pallas kernels: 6.8 us -> 4.19 us  [local(): pl.pallas_call(functools.partial(force_kernel, lanes, high_count), out_sh...]
    pallas_call x1, Pallas kernels: 5.84 us -> 4.16 us  [local(): pl.pallas_call(functools.partial(near_kernel, high_count), out_shape=(jax...]
    convert_element_type x2 -> x0, other arithmetic: 1.41 us -> none  [the longest x1 0.71 us: local(): seg_nodes.astype(F32)]
    pallas_call x0 -> x3, Pallas kernels: none -> 0.86 us  [the longest x1 0.46 us: local(): pl.pallas_call(functools.partial(select_kernel, high_count), out_shape=(j...]
  transfers between devices with their start and end apart: 12 -> 12, of which waited for: 10 -> 8; matrix products, arithmetic and copies ran while one was open for 0% -> 0% of each run, Pallas kernels for 0% -> 2%
where the time goes in v3:
time: 40.6 us; the launch traced here: 40.2 us
  waiting for transfers between devices  15.3 us (38%)
  starting transfers between devices  11.5 us (28%)
  Pallas kernels  9.23 us (23%)
  local copies, waits for them, and re-layouts  2.68 us (7%)
  other arithmetic  0.82 us (2%)
  between operations  0.71 us (2%)
    ppermute x12, waiting for transfers between devices, shifted(): return lax.ppermute(block, ('cells', 'lanes'), route)  15.3 us
    ppermute x12, starting transfers between devices, shifted(): return lax.ppermute(block, ('cells', 'lanes'), route)  11.5 us
    pallas_call x1, Pallas kernels, local(): pl.pallas_call(functools.partial(force_kernel, lanes, high_count), out_sh...  4.19 us
    pallas_call x1, Pallas kernels, local(): pl.pallas_call(functools.partial(near_kernel, high_count), out_shape=(jax...  4.16 us
    unnamed x8, local copies, waits for them, and re-layouts  2.68 us
    add x1, other arithmetic, local(): fields = fields + rows_of([seg_nodes, node_owner], 9, 13).astype(F32)  0.82 us
  transfers between devices with their start and end apart: 12, of which 8 were waited for; matrix products, arithmetic and copies ran while one was open for 0% of the time, Pallas kernels for 2%

profile of v3, /device:TPU:0, one launch (start us, length us, event | category | flops | bytes accessed | tf_op | source)
XLA Modules:
  0.0 40.2 jit_solution(15959478807161429222)
XLA Ops:
  0.6 0.8 %convert_add_fusion.fields = f32[13,1024]{1,0:T(8,128)S(1)} fusion(s32[2,1024]{1,0:T(2,128)} %param.14, s32[2,1024]{1,0:T(2,128)} %param.13, f32[3,1024]{1,0:T(4,128)} %param.11, f32[3,1024]{1,0:T(4,128)} %param.10, f32[3,1024]{1,0:T(4,128)} %param.9), kind=kLoop, calls=%fused_computation | loop fusion | flops 66560 | bytes 106496 | tf_op jit(solution)/shard_map/add | solution.py:325
  1.5 6.1 %collective-permute-start.3 = (f32[24,1024]{1,0:T(8,128)S(1)}, f32[24,1024]{1,0:T(8,128)S(1)}, u32[]{:S(2)}, u32[]{:S(2)}) collective-permute-start(f32[24,1024]{1,0:T(8,128)S(1)} %pack.1.own.refs_2_), channel_id=1, source_target_pairs={{4,0},{5,1},{6,2},{7,3},{8,4},{9,5},{10,6},{11,7},{12,8},{13,9},{1... | collective-permute-start | bytes 294920 | tf_op jit(solution)/shard_map/ppermute | solution.py:35
  7.6 0.0 collective-permute-start.2
  7.6 0.5 %collective-permute-start.1 = (f32[24,1024]{1,0:T(8,128)S(1)}, f32[24,1024]{1,0:T(8,128)S(1)}, u32[]{:S(2)}, u32[]{:S(2)}) collective-permute-start(f32[24,1024]{1,0:T(8,128)S(1)} %pack.1.own.refs_2_), channel_id=1, source_target_pairs={{30,0},{31,1},{0,2},{1,3},{2,4},{3,5},{4,6},{5,7},{6,8},{7,9},{8,1... | collective-permute-start | bytes 294920 | tf_op jit(solution)/shard_map/ppermute | solution.py:35
  8.1 0.7 %collective-permute-start = (f32[24,1024]{1,0:T(8,128)S(1)}, f32[24,1024]{1,0:T(8,128)S(1)}, u32[]{:S(2)}, u32[]{:S(2)}) collective-permute-start(f32[24,1024]{1,0:T(8,128)S(1)} %pack.1.own.refs_2_), channel_id=1, source_target_pairs={{28,0},{29,1},{30,2},{31,3},{0,4},{1,5},{2,6},{3,7},{4,8},{5,9},{6... | collective-permute-start | bytes 294920 | tf_op jit(solution)/shard_map/ppermute | solution.py:35
  8.8 0.0 copy-start
  8.8 0.7 %copy-done = s32[8,8]{1,0:T(8,128)S(1)} copy-done((s32[8,8]{1,0:T(8,128)S(1)}, s32[8,8]{1,0:T(8,128)}, u32[]{:S(2)}) %copy-start) | copy-done | bytes 280
  9.5 0.0 copy-start.1
  9.5 0.7 %copy-done.1 = f32[1024]{0:T(1024)S(1)} copy-done((f32[1024]{0:T(1024)S(1)}, f32[1024]{0:T(1024)}, u32[]{:S(2)}) %copy-start.1) | copy-done | bytes 4120
  10.2 0.0 copy-start.2
  10.2 0.7 %copy-done.2 = s32[32]{0:T(128)S(1)} copy-done((s32[32]{0:T(128)S(1)}, s32[32]{0:T(128)}, u32[]{:S(2)}) %copy-start.2) | copy-done | bytes 152
  10.8 0.0 copy-start.3
  10.8 0.7 %copy-done.3 = s32[32]{0:T(128)S(1)} copy-done((s32[32]{0:T(128)S(1)}, s32[32]{0:T(128)}, u32[]{:S(2)}) %copy-start.3) | copy-done | bytes 152
  11.5 0.4 early.1
  11.8 0.0 collective-permute-done.3.refs_4_
  11.8 0.0 collective-permute-done.2.refs_3_
  11.8 2.5 %collective-permute-done.1.refs_1_ = f32[24,1024]{1,0:T(8,128)S(1)} collective-permute-done((f32[24,1024]{1,0:T(8,128)S(1)}, f32[24,1024]{1,0:T(8,128)S(1)}, u32[]{:S(2)}, u32[]{:S(2)}) %collective-permute-start.1) | collective-permute-done | bytes 98336 | tf_op jit(solution)/shard_map/ppermute | solution.py:35
  14.3 2.1 %collective-permute-done.refs_0_ = f32[24,1024]{1,0:T(8,128)S(1)} collective-permute-done((f32[24,1024]{1,0:T(8,128)S(1)}, f32[24,1024]{1,0:T(8,128)S(1)}, u32[]{:S(2)}, u32[]{:S(2)}) %collective-permute-start) | collective-permute-done | bytes 98336 | tf_op jit(solution)/shard_map/ppermute | solution.py:35
  16.4 4.2 %forces.1 = (f32[4,8,128]{2,1,0:T(8,128)S(1)}, f32[4,8,128]{2,1,0:T(8,128)S(1)}) custom-call(s32[8,8]{1,0:T(8,128)S(1)} %get-tuple-element.20.lists, bf16[8,128,48]{2,1,0:T(8,128)(2,1)S(1)} %get-tuple-element.21.lhs_s, bf16[2,128,1024]{2,1,0:T(8,128)(2,1)S(1)} %get-tuple-element.16.onehots.own_onehots, f32[24,1024]{1,0:T(8,128)S(1)} %collective-permute-done.refs_0_, ...), custom_call_target="tpu_custom_call" | custom-call | tf_op jit(solution)/shard_map/forces/pallas_call | solution.py:355
  20.6 1.6 %collective-permute-start.4 = (f32[4,8,128]{2,1,0:T(8,128)S(1)}, f32[4,8,128]{2,1,0:T(8,128)S(1)}, u32[]{:S(2)}, u32[]{:S(2)}) collective-permute-start(f32[4,8,128]{2,1,0:T(8,128)S(1)} %get-tuple-element.22.refs_0_), channel_id=1, source_target_pairs={{1,0},{0,1},{3,2},{2,3},{5,4},{4,5},{7,6},{6,7},{9,8},{8,9},{11,10... | collective-permute-start | bytes 49160 | tf_op jit(solution)/shard_map/ppermute | solution.py:35
  22.2 0.0 collective-permute-start.6
  22.2 0.0 collective-permute-start.5
  22.2 2.2 %collective-permute-done.4.refs_1_ = f32[4,8,128]{2,1,0:T(8,128)S(1)} collective-permute-done((f32[4,8,128]{2,1,0:T(8,128)S(1)}, f32[4,8,128]{2,1,0:T(8,128)S(1)}, u32[]{:S(2)}, u32[]{:S(2)}) %collective-permute-start.4) | collective-permute-done | bytes 16416 | tf_op jit(solution)/shard_map/ppermute | solution.py:35
  24.4 4.5 %collective-permute-done.6.refs_3_ = f32[4,8,128]{2,1,0:T(8,128)S(1)} collective-permute-done((f32[4,8,128]{2,1,0:T(8,128)S(1)}, f32[4,8,128]{2,1,0:T(8,128)S(1)}, u32[]{:S(2)}, u32[]{:S(2)}) %collective-permute-start.6) | collective-permute-done | bytes 16416 | tf_op jit(solution)/shard_map/ppermute | solution.py:35
  29.0 0.0 collective-permute-done.5.refs_2_
  29.0 0.1 collective-permute-start.11
  29.0 0.1 collective-permute-start.10
  29.1 0.1 collective-permute-start.9
  29.2 0.5 %collective-permute-start.8 = (f32[3,8,128]{2,1,0:T(8,128)S(1)}, f32[3,8,128]{2,1,0:T(8,128)S(1)}, u32[]{:S(2)}, u32[]{:S(2)}) collective-permute-start(f32[3,8,128]{2,1,0:T(8,128)S(1)} %velocity.1.refs_7_), channel_id=1, source_target_pairs={{30,0},{31,1},{0,2},{1,3},{2,4},{3,5},{4,6},{5,7},{6,8},{7,9},{8,1... | collective-permute-start | bytes 36872 | tf_op jit(solution)/shard_map/ppermute | solution.py:35
  29.7 2.0 %collective-permute-start.7 = (f32[3,8,128]{2,1,0:T(8,128)S(1)}, f32[3,8,128]{2,1,0:T(8,128)S(1)}, u32[]{:S(2)}, u32[]{:S(2)}) collective-permute-start(f32[3,8,128]{2,1,0:T(8,128)S(1)} %velocity.1.refs_7_), channel_id=1, source_target_pairs={{28,0},{29,1},{30,2},{31,3},{0,4},{1,5},{2,6},{3,7},{4,8},{5,9},{6... | collective-permute-start | bytes 36872 | tf_op jit(solution)/shard_map/ppermute | solution.py:35
  31.6 0.5 %select.6 = (bf16[8,128,1024]{2,1,0:T(8,128)(2,1)S(1)}, bf16[40,48,128]{2,1,0:T(8,128)(2,1)S(1)}) custom-call(f32[24,1024]{1,0:T(8,128)S(1)} %collective-permute-done.refs_0_, f32[24,1024]{1,0:T(8,128)S(1)} %collective-permute-done.1.refs_1_, f32[24,1024]{1,0:T(8,128)S(1)} %pack.1.own.refs_2_, f32[24,1024]{1,0:T(8,128)S(1)} %collective-permute-done.2.refs_3_, ...), custom_call_target="tpu_custom_call" | custom-call | flops 268435456 | bytes 8388608 | tf_op jit(solution)/shard_map/select/pallas_call | solution.py:382
  32.1 0.1 collective-permute-done.11.refs_10_
  32.1 0.6 %collective-permute-done.10.refs_9_ = f32[3,8,128]{2,1,0:T(8,128)S(1)} collective-permute-done((f32[3,8,128]{2,1,0:T(8,128)S(1)}, f32[3,8,128]{2,1,0:T(8,128)S(1)}, u32[]{:S(2)}, u32[]{:S(2)}) %collective-permute-start.10) | collective-permute-done | bytes 12320 | tf_op jit(solution)/shard_map/ppermute | solution.py:35
  32.8 0.0 collective-permute-done.9.refs_8_
  32.8 2.2 %collective-permute-done.8.refs_6_ = f32[3,8,128]{2,1,0:T(8,128)S(1)} collective-permute-done((f32[3,8,128]{2,1,0:T(8,128)S(1)}, f32[3,8,128]{2,1,0:T(8,128)S(1)}, u32[]{:S(2)}, u32[]{:S(2)}) %collective-permute-start.8) | collective-permute-done | bytes 12320 | tf_op jit(solution)/shard_map/ppermute | solution.py:35
  35.0 1.0 %collective-permute-done.7.refs_5_ = f32[3,8,128]{2,1,0:T(8,128)S(1)} collective-permute-done((f32[3,8,128]{2,1,0:T(8,128)S(1)}, f32[3,8,128]{2,1,0:T(8,128)S(1)}, u32[]{:S(2)}, u32[]{:S(2)}) %collective-permute-start.7) | collective-permute-done | bytes 12320 | tf_op jit(solution)/shard_map/ppermute | solution.py:35
  36.1 4.2 %nearness.1 = (f32[8,128]{1,0:T(8,128)}, f32[3,1024]{1,0:T(4,128)}) custom-call(s32[1,32]{1,0:T(1,128)S(1)} %get-tuple-element.14.targets, s32[1,32]{1,0:T(1,128)S(1)} %get-tuple-element.15.sources, bf16[2,128,1024]{2,1,0:T(8,128)(2,1)S(1)} %get-tuple-element.16.onehots.own_onehots, bf16[8,128,1024]{2,1,0:T(8,128)(2,1)S(1)} %get-tuple-element.17.onehots, ...), custom_call_target="tpu_custom_call" | custom-call | tf_op jit(solution)/shard_map/nearness/pallas_call | solution.py:394
  (2 shorter events, 0.1 us)
Async XLA Ops:
  1.5 10.3 %collective-permute-start.3 = (f32[24,1024]{1,0:T(8,128)S(1)}, f32[24,1024]{1,0:T(8,128)S(1)}, u32[]{:S(2)}, u32[]{:S(2)}) collective-permute-start(f32[24,1024]{1,0:T(8,128)S(1)} %pack.1.own.refs_2_), channel_id=1, source_target_pairs={{4,0},{5,1},{6,2},{7,3},{8,4},{9,5},{10,6},{11,7},{12,8},{13,9},{1... | collective-permute-start | bytes 294920 | tf_op jit(solution)/shard_map/ppermute | solution.py:35
  7.6 4.3 %collective-permute-start.2 = (f32[24,1024]{1,0:T(8,128)S(1)}, f32[24,1024]{1,0:T(8,128)S(1)}, u32[]{:S(2)}, u32[]{:S(2)}) collective-permute-start(f32[24,1024]{1,0:T(8,128)S(1)} %pack.1.own.refs_2_), channel_id=1, source_target_pairs={{2,0},{3,1},{4,2},{5,3},{6,4},{7,5},{8,6},{9,7},{10,8},{11,9},{12,... | collective-permute-start | bytes 294920 | tf_op jit(solution)/shard_map/ppermute | solution.py:35
  7.6 6.7 %collective-permute-start.1 = (f32[24,1024]{1,0:T(8,128)S(1)}, f32[24,1024]{1,0:T(8,128)S(1)}, u32[]{:S(2)}, u32[]{:S(2)}) collective-permute-start(f32[24,1024]{1,0:T(8,128)S(1)} %pack.1.own.refs_2_), channel_id=1, source_target_pairs={{30,0},{31,1},{0,2},{1,3},{2,4},{3,5},{4,6},{5,7},{6,8},{7,9},{8,1... | collective-permute-start | bytes 294920 | tf_op jit(solution)/shard_map/ppermute | solution.py:35
  8.1 8.3 %collective-permute-start = (f32[24,1024]{1,0:T(8,128)S(1)}, f32[24,1024]{1,0:T(8,128)S(1)}, u32[]{:S(2)}, u32[]{:S(2)}) collective-permute-start(f32[24,1024]{1,0:T(8,128)S(1)} %pack.1.own.refs_2_), channel_id=1, source_target_pairs={{28,0},{29,1},{30,2},{31,3},{0,4},{1,5},{2,6},{3,7},{4,8},{5,9},{6... | collective-permute-start | bytes 294920 | tf_op jit(solution)/shard_map/ppermute | solution.py:35
  8.8 0.7 %copy-start = (s32[8,8]{1,0:T(8,128)S(1)}, s32[8,8]{1,0:T(8,128)}, u32[]{:S(2)}) copy-start(s32[8,8]{1,0:T(8,128)} %refs_0_.1) | copy-start | bytes 772
  9.5 0.7 %copy-start.1 = (f32[1024]{0:T(1024)S(1)}, f32[1024]{0:T(1024)}, u32[]{:S(2)}) copy-start(f32[1024]{0:T(1024)} %param.15) | copy-start | bytes 12292
  10.2 0.7 %copy-start.2 = (s32[32]{0:T(128)S(1)}, s32[32]{0:T(128)}, u32[]{:S(2)}) copy-start(s32[32]{0:T(128)} %param.16) | copy-start | bytes 388
  10.8 0.7 %copy-start.3 = (s32[32]{0:T(128)S(1)}, s32[32]{0:T(128)}, u32[]{:S(2)}) copy-start(s32[32]{0:T(128)} %param.17) | copy-start | bytes 388
  20.6 3.8 %collective-permute-start.4 = (f32[4,8,128]{2,1,0:T(8,128)S(1)}, f32[4,8,128]{2,1,0:T(8,128)S(1)}, u32[]{:S(2)}, u32[]{:S(2)}) collective-permute-start(f32[4,8,128]{2,1,0:T(8,128)S(1)} %get-tuple-element.22.refs_0_), channel_id=1, source_target_pairs={{1,0},{0,1},{3,2},{2,3},{5,4},{4,5},{7,6},{6,7},{9,8},{8,9},{11,10... | collective-permute-start | bytes 49160 | tf_op jit(solution)/shard_map/ppermute | solution.py:35
  22.2 6.8 %collective-permute-start.6 = (f32[4,8,128]{2,1,0:T(8,128)S(1)}, f32[4,8,128]{2,1,0:T(8,128)S(1)}, u32[]{:S(2)}, u32[]{:S(2)}) collective-permute-start(f32[4,8,128]{2,1,0:T(8,128)S(1)} %get-tuple-element.23), channel_id=1, source_target_pairs={{31,0},{30,1},{1,2},{0,3},{3,4},{2,5},{5,6},{4,7},{7,8},{6,9},{9,1... | collective-permute-start | bytes 49160 | tf_op jit(solution)/shard_map/ppermute | solution.py:35
  22.2 6.8 %collective-permute-start.5 = (f32[4,8,128]{2,1,0:T(8,128)S(1)}, f32[4,8,128]{2,1,0:T(8,128)S(1)}, u32[]{:S(2)}, u32[]{:S(2)}) collective-permute-start(f32[4,8,128]{2,1,0:T(8,128)S(1)} %get-tuple-element.23), channel_id=1, source_target_pairs={{30,0},{31,1},{0,2},{1,3},{2,4},{3,5},{4,6},{5,7},{6,8},{7,9},{8,1... | collective-permute-start | bytes 49160 | tf_op jit(solution)/shard_map/ppermute | solution.py:35
  29.0 3.2 %collective-permute-start.11 = (f32[3,8,128]{2,1,0:T(8,128)S(1)}, f32[3,8,128]{2,1,0:T(8,128)S(1)}, u32[]{:S(2)}, u32[]{:S(2)}) collective-permute-start(f32[3,8,128]{2,1,0:T(8,128)S(1)} %velocity.1.refs_7_), channel_id=1, source_target_pairs={{6,0},{7,1},{8,2},{9,3},{10,4},{11,5},{12,6},{13,7},{14,8},{15,9},... | collective-permute-start | bytes 36872 | tf_op jit(solution)/shard_map/ppermute | solution.py:35
  29.0 3.7 %collective-permute-start.10 = (f32[3,8,128]{2,1,0:T(8,128)S(1)}, f32[3,8,128]{2,1,0:T(8,128)S(1)}, u32[]{:S(2)}, u32[]{:S(2)}) collective-permute-start(f32[3,8,128]{2,1,0:T(8,128)S(1)} %velocity.1.refs_7_), channel_id=1, source_target_pairs={{4,0},{5,1},{6,2},{7,3},{8,4},{9,5},{10,6},{11,7},{12,8},{13,9},{1... | collective-permute-start | bytes 36872 | tf_op jit(solution)/shard_map/ppermute | solution.py:35
  29.1 3.7 %collective-permute-start.9 = (f32[3,8,128]{2,1,0:T(8,128)S(1)}, f32[3,8,128]{2,1,0:T(8,128)S(1)}, u32[]{:S(2)}, u32[]{:S(2)}) collective-permute-start(f32[3,8,128]{2,1,0:T(8,128)S(1)} %velocity.1.refs_7_), channel_id=1, source_target_pairs={{2,0},{3,1},{4,2},{5,3},{6,4},{7,5},{8,6},{9,7},{10,8},{11,9},{12,... | collective-permute-start | bytes 36872 | tf_op jit(solution)/shard_map/ppermute | solution.py:35
  29.2 5.9 %collective-permute-start.8 = (f32[3,8,128]{2,1,0:T(8,128)S(1)}, f32[3,8,128]{2,1,0:T(8,128)S(1)}, u32[]{:S(2)}, u32[]{:S(2)}) collective-permute-start(f32[3,8,128]{2,1,0:T(8,128)S(1)} %velocity.1.refs_7_), channel_id=1, source_target_pairs={{30,0},{31,1},{0,2},{1,3},{2,4},{3,5},{4,6},{5,7},{6,8},{7,9},{8,1... | collective-permute-start | bytes 36872 | tf_op jit(solution)/shard_map/ppermute | solution.py:35
  29.7 6.4 %collective-permute-start.7 = (f32[3,8,128]{2,1,0:T(8,128)S(1)}, f32[3,8,128]{2,1,0:T(8,128)S(1)}, u32[]{:S(2)}, u32[]{:S(2)}) collective-permute-start(f32[3,8,128]{2,1,0:T(8,128)S(1)} %velocity.1.refs_7_), channel_id=1, source_target_pairs={{28,0},{29,1},{30,2},{31,3},{0,4},{1,5},{2,6},{3,7},{4,8},{5,9},{6... | collective-permute-start | bytes 36872 | tf_op jit(solution)/shard_map/ppermute | solution.py:35

commit v4 on v3

v4 whole, which is shorter than its diff:
```python
import functools
import math

import jax
import jax.numpy as jnp
from jax import lax
from jax.experimental import pallas as pl
from jax.experimental.pallas import tpu as pltpu
from jax.sharding import PartitionSpec as P

BLK = 128
FIELDS = 13
REACH = 2
FORCE_SCALE = 0.02
CORE_SQUARE = 0.25
TIME_STEP = 4.0
MIDDLE = 2.0
LOG2E = math.log2(math.e)

F32 = jnp.float32
BF16 = jnp.bfloat16
VM = pl.BlockSpec(memory_space=pltpu.VMEM)
SM = pl.BlockSpec(memory_space=pltpu.SMEM)


def params(mib):
    return pltpu.CompilerParams(vmem_limit_bytes=mib << 20)


def shifted(block, cell_step, lane_step):
    cells, lanes = lax.axis_size("cells"), lax.axis_size("lanes")
    route = []
    for c in range(cells):
        for l in range(lanes):
            source = ((c + cell_step) % cells) * lanes + (l + lane_step) % lanes
            route.append((source, c * lanes + l))
    return lax.ppermute(block, ("cells", "lanes"), route)


def split3(x):
    high = x.astype(BF16).astype(F32)
    rest = x - high
    mid = rest.astype(BF16).astype(F32)
    return high, mid, rest - mid


def row(ref, field, k):
    blocks = ref.shape[0] // FIELDS
    return ref[pl.ds(field * blocks + k, 8, stride=0), :]


def rows_at(ref, field, k):
    blocks = ref.shape[0] // FIELDS
    return ref[pl.ds(field * blocks + k, 8, stride=blocks), :]


def cross(a, b):
    return [
        a[1] * b[2] - a[2] * b[1],
        a[2] * b[0] - a[0] * b[2],
        a[0] * b[1] - a[1] * b[0],
    ]


def dot3(a, b):
    return a[0] * b[0] + a[1] * b[1] + a[2] * b[2]


def choose(rows, values, other):
    for number, value in values.items():
        other = jnp.where(rows == number, value, other)
    return other


def contract_lanes(a, b):
    return lax.dot_general(a, b, (((1,), (1,)), ((), ())), preferred_element_type=F32)


def end_address(ref, end, k, high_count):
    node = row(ref, 9 + end, k).astype(jnp.int32)
    owner = row(ref, 11 + end, k).astype(jnp.int32)
    return owner * high_count + lax.shift_right_logical(node, BLK.bit_length() - 1), node & (BLK - 1)


def six_left(x):
    h, m, l = split3(x)
    return jnp.concatenate([h, h, m, h, l, m], 0)


def right_order(parts):
    h, m, l = parts
    return jnp.concatenate([h, m, h, l, h, m], 0).astype(BF16)


def pack_kernel(fields, out):
    blocks = fields.shape[1] // BLK
    for k in range(blocks):
        piece = fields[:, k * BLK : (k + 1) * BLK]
        rows = lax.broadcasted_iota(jnp.int32, piece.shape, 0)
        out[pl.ds(k, FIELDS, stride=blocks), :] = jnp.where(rows < 3, piece - MIDDLE, piece)


def early_kernel(high_count, own, *refs):
    count = (len(refs) - 2) // 2
    for source, out in zip(refs[:count], refs[count : 2 * count]):
        out[...] = source[...]
    lhs_out, onehots = refs[2 * count :]
    rows = lax.broadcasted_iota(jnp.int32, (8, BLK), 0)
    nodes = lax.broadcasted_iota(jnp.int32, (BLK, BLK), 0)
    for k in range(own.shape[0] // FIELDS):
        c = [row(own, x, k) for x in range(3)]
        l = {3 + x: row(own, 6 + x, k) for x in range(3)}
        target = choose(rows, {**l, 6: 1.0, 7: dot3(c, c) + CORE_SQUARE}, rows_at(own, 0, k))
        lhs_out[k] = six_left(target).T.astype(BF16)
        for end in range(2):
            low = end_address(own, end, k, high_count)[1]
            onehots[end, :, k * BLK : (k + 1) * BLK] = (nodes == low[0:1]).astype(F32).astype(BF16)


def force_kernel(lanes, high_count, lists, lhs_s, onehots, *refs):
    packs = refs[: 2 * REACH + 1]
    own_out, next_out, rhs_s, src_s, force_s = refs[2 * REACH + 1 :]
    own = packs[REACH]
    blocks = own.shape[0] // FIELDS
    rows = lax.broadcasted_iota(jnp.int32, (8, BLK), 0)

    for d, ref in enumerate(packs):
        for k in range(blocks):
            c = [row(ref, x, k) for x in range(3)]
            l = [row(ref, 6 + x, k) for x in range(3)]
            upper, lower = rows_at(ref, 0, k), rows_at(ref, 5, k)
            near = jnp.where(rows < 3, -2.0 * upper, choose(rows, {6: dot3(c, c), 7: 1.0}, 0.0))
            along = jnp.where((rows >= 3) & (rows < 6), upper, 0.0)
            moment = cross(l, c)
            sums = choose(rows, {5 + x: moment[x] for x in range(3)}, lower)
            w = d * blocks + k
            rhs_s[w, :, 0:BLK] = right_order(split3(near))
            rhs_s[w, :, BLK : 2 * BLK] = right_order(split3(along))
            src_s[w] = jnp.concatenate([*split3(sums), jnp.zeros((8, BLK), F32)], 0).astype(BF16)

    def one_target(t, carry):
        lhs = lhs_s[t]
        highs, lows, srcs = [], [], []
        for e in range(lists.shape[1]):
            w = lists[t, e]
            both = jnp.dot(lhs, rhs_s[w], preferred_element_type=F32)
            inverse = lax.rsqrt(both[:, :BLK])
            weight = both[:, BLK:] * inverse * (inverse * inverse)
            high = weight.astype(BF16)
            highs.append(high)
            lows.append((weight - high.astype(F32)).astype(BF16))
            srcs.append(src_s[w])
        src = jnp.concatenate(srcs, 1)
        total = contract_lanes(jnp.concatenate(highs, 1), src)
        total = total + contract_lanes(jnp.concatenate(lows, 1), src)
        total = total.T
        force_s[t] = total[0:8] + (total[8:16] + total[16:24])
        return carry

    lax.fori_loop(0, blocks, one_target, 0, unroll=math.gcd(blocks, 4))

    out = None
    for k in range(blocks):
        whole = force_s.at[k]
        line = [whole[pl.ds(1 + x, 8, stride=0), :] for x in range(3)]
        moment = [whole[pl.ds(5 + x, 8, stride=0), :] for x in range(3)]
        c = [row(own, x, k) for x in range(3)]
        l = [row(own, 6 + x, k) for x in range(3)]
        turned = cross(line, c)
        values = [(0.5 * FORCE_SCALE) * (turned[x] - moment[x]) for x in range(3)]
        values.append(jnp.sqrt(dot3(l, l)) * (0.5 / lanes))
        tops = [value.astype(BF16).astype(F32) for value in values]
        parts = tops + [value - top for value, top in zip(values, tops)]
        pieces = []
        for end in range(2):
            high = end_address(own, end, k, high_count)[0]
            groups = range(0, 2 * high_count, 8)
            masks = [rows + first == high for first in groups]
            pieces.append([jnp.where(mask, part, 0.0) for part in parts for mask in masks])
        lhs = jnp.concatenate([jnp.concatenate(p, 0) for p in pieces], 1).astype(BF16)
        cut = slice(k * BLK, (k + 1) * BLK)
        term = contract_lanes(lhs, jnp.concatenate([onehots[end, :, cut] for end in range(2)], 1))
        out = term if out is None else out + term
    n = 8 * high_count
    out = out[0:n] + out[n : 2 * n]
    for k in range(4):
        first = 2 * high_count * k
        own_out[k] = out[first : first + high_count]
        next_out[k] = out[first + high_count : first + 2 * high_count]


def select_kernel(*refs):
    packs, (near_out, centre_out) = refs[:-2], refs[-2:]
    blocks = packs[0].shape[0] // FIELDS
    rows = lax.broadcasted_iota(jnp.int32, (8, BLK), 0)
    for d, ref in enumerate(packs):
        for k in range(blocks):
            w = d * blocks + k
            c = [row(ref, x, k) for x in range(3)]
            centre = LOG2E * rows_at(ref, 0, k)
            extra = choose(rows, {6: LOG2E * dot3(c, c), 7: LOG2E}, 0.0)
            near_out[w] = right_order(split3(jnp.where(rows < 3, -2.0 * centre, extra)))
            parts = split3(jnp.where(rows < 3, centre, choose(rows, {6: -LOG2E}, 0.0)))
            centre_out[w] = jnp.concatenate(parts, 0)


def near_kernel(high_count, targets, sources, near_s, centre_s, *refs):
    packs = refs[: 2 * REACH + 1]
    velocities = refs[2 * REACH + 1 : 4 * REACH + 3]
    near_out, vel_out, tgt_s, src_s, acc_s = refs[4 * REACH + 3 :]
    blocks = packs[0].shape[0] // FIELDS
    rows = lax.broadcasted_iota(jnp.int32, (8, BLK), 0)

    for k in range(high_count):
        for x in range(3):
            vel_out[x : x + 1, k * BLK : (k + 1) * BLK] = velocities[REACH][x, k : k + 1, :]

    zero = jnp.zeros((8, BLK), F32)
    nothing = jnp.zeros((48, BLK), BF16)
    signs = choose(rows, {4: -LOG2E}, zero + LOG2E)
    turn = jnp.where(rows < 3, -2.0, choose(rows, {3: 1.0}, zero))
    constant = split3(choose(rows, {5: LOG2E}, zero))
    for d, ref in enumerate(packs):
        for k in range(blocks):
            w = d * blocks + k
            v = [zero] * 3
            for end in range(2):
                high, low = end_address(ref, end, k, high_count)
                for owner in range(2):
                    for first in range(0, high_count, 8):
                        mask = rows + (owner * high_count + first) == high
                        for x in range(3):
                            table = velocities[d + owner][x, first : first + 8, :]
                            got = jnp.take_along_axis(table, low, axis=1, mode="promise_in_bounds")
                            v[x] = v[x] + jnp.where(mask, got, 0.0)
            for x in range(3):
                for shift in (4, 2, 1):
                    v[x] = v[x] + pltpu.roll(v[x], shift, 0)
                v[x] = v[x] * (0.5 * TIME_STEP)
            c = [row(ref, x, k) for x in range(3)]
            vv, cv = dot3(v, v), dot3(c, v)
            moved = choose(rows, {0: v[0], 1: v[1], 2: v[2], 3: vv}, cv)
            parts = split3(moved * signs)
            centre = centre_s[w]
            still = [centre[8 * n : 8 * n + 8] for n in range(3)]
            src_s[w, 0:48, 0:BLK] = right_order([jnp.where(rows < 3, p, 0.0) for p in parts])
            src_s[w, 48:96, 0:BLK] = right_order(
                [jnp.where(rows == 4, p, q) for p, q in zip(parts, still)]
            )
            src_s[w, 0:48, BLK : 2 * BLK] = nothing
            src_s[w, 48:96, BLK : 2 * BLK] = right_order(
                [p * turn + q for p, q in zip(parts, constant)]
            )
            if d == REACH:
                first = choose(rows, {6: 1.0, 7: dot3(c, c)}, rows_at(ref, 0, k))
                second = choose(rows, {3: 1.0, 4: 1.0, 5: vv, 6: cv, 7: 0.0}, moved)
                six = jnp.concatenate([six_left(first), six_left(second)], 0)
                tgt_s[k] = six.T.astype(BF16)

    acc_s[...] = jnp.zeros_like(acc_s)
    count = targets.shape[1]
    group = math.gcd(count, 16)

    def some_pairs(step, carry):
        for u in range(group):
            t = targets[0, step * group + u]
            w = sources[0, step * group + u]
            target = tgt_s[t]
            rr = jnp.dot(target[:, 0:48], near_s[w], preferred_element_type=F32)
            both = jnp.dot(target, src_s[w], preferred_element_type=F32)
            toward = both[:, 0:BLK]
            square = jnp.maximum(both[:, BLK : 2 * BLK], 0.0)
            s = jnp.clip(toward / (square + LOG2E * CORE_SQUARE), 0.0, 1.0)
            acc_s[t] += jnp.exp2(s * (toward + (toward - s * square)) - rr)
        return carry

    lax.fori_loop(0, count // group, some_pairs, 0)
    for t in range(blocks):
        near_out[t : t + 1] = jnp.sum(acc_s[t].T, axis=0, keepdims=True)


def velocity_kernel(mobility, *refs):
    out = refs[-1]
    total = refs[0][...]
    for ref in refs[1:-1]:
        total = total + ref[...]
    scale = mobility[...] / (1.0 + total[3])
    for x in range(3):
        out[x] = total[x] * scale


def rows_of(pieces, first, rows):
    total = None
    for piece in pieces:
        last = first + piece.shape[0]
        padded = jnp.pad(piece, ((first, rows - last), (0, 0)))
        total = padded if total is None else total + padded
        first = last
    return total


def local(
    centres, seg_lines, burgers, neighbour_blocks, seg_nodes, node_owner, mobility, cand_target, cand_source
):
    seg = centres.shape[1]
    blocks = seg // BLK
    high_count = mobility.shape[0] // BLK
    lanes = lax.axis_size("lanes")
    window = (2 * REACH + 1) * blocks
    fields = rows_of([centres, burgers, seg_lines], 0, FIELDS)
    fields = fields + rows_of([seg_nodes, node_owner], 9, FIELDS).astype(F32)
    own = pl.pallas_call(
        pack_kernel,
        out_shape=jax.ShapeDtypeStruct((FIELDS * blocks, BLK), F32),
        in_specs=[VM],
        out_specs=VM,
        compiler_params=params(4),
        name="pack",
    )(fields)
    packs = [own if o == 0 else shifted(own, o, 0) for o in range(-REACH, REACH + 1)]
    small = [
        neighbour_blocks,
        mobility.reshape(high_count, BLK),
        cand_target.reshape(1, -1),
        cand_source.reshape(1, -1),
    ]
    lists, rate, targets, sources, lhs, own_onehots = pl.pallas_call(
        functools.partial(early_kernel, high_count),
        out_shape=[jax.ShapeDtypeStruct(x.shape, x.dtype) for x in small]
        + [
            jax.ShapeDtypeStruct((blocks, BLK, 48), BF16),
            jax.ShapeDtypeStruct((2, BLK, seg), BF16),
        ],
        in_specs=[VM] * (1 + len(small)),
        out_specs=[VM] * (2 + len(small)),
        compiler_params=params(8),
        cost_estimate=pl.CostEstimate(flops=1 << 28, bytes_accessed=1 << 23, transcendentals=0),
        name="early",
    )(own, *small)
    part = jax.ShapeDtypeStruct((4, high_count, BLK), F32)
    own_part, next_part = pl.pallas_call(
        functools.partial(force_kernel, lanes, high_count),
        out_shape=(part, part),
        in_specs=[SM] + [VM] * (2 + len(packs)),
        out_specs=(VM, VM),
        scratch_shapes=[
            pltpu.VMEM((window, 48, 2 * BLK), BF16),
            pltpu.VMEM((window, 32, BLK), BF16),
            pltpu.VMEM((blocks, 8, BLK), F32),
        ],
        compiler_params=params(16),
        name="forces",
    )(lists, lhs, own_onehots, *packs)
    terms = [own_part]
    terms += [shifted(own_part, 0, lane) for lane in range(1, lanes)]
    terms += [shifted(next_part, -1, lane) for lane in range(lanes)]
    velocity = pl.pallas_call(
        velocity_kernel,
        out_shape=jax.ShapeDtypeStruct((3, high_count, BLK), F32),
        in_specs=[VM] * (1 + len(terms)),
        out_specs=VM,
        compiler_params=params(4),
        name="velocity",
    )(rate, *terms)
    velocities = [
        velocity if o == 0 else shifted(velocity, o, 0) for o in range(-REACH, REACH + 2)
    ]
    near_sources, centre_sources = pl.pallas_call(
        select_kernel,
        out_shape=(
            jax.ShapeDtypeStruct((window, 48, BLK), BF16),
            jax.ShapeDtypeStruct((window, 24, BLK), F32),
        ),
        in_specs=[VM] * len(packs),
        out_specs=(VM, VM),
        compiler_params=params(16),
        cost_estimate=pl.CostEstimate(flops=1 << 28, bytes_accessed=1 << 23, transcendentals=0),
        name="select",
    )(*packs)
    near, vel = pl.pallas_call(
        functools.partial(near_kernel, high_count),
        out_shape=(
            jax.ShapeDtypeStruct((blocks, BLK), F32),
            jax.ShapeDtypeStruct((3, high_count * BLK), F32),
        ),
        in_specs=[SM, SM] + [VM] * (2 + len(packs) + len(velocities)),
        out_specs=(VM, VM),
        scratch_shapes=[
            pltpu.VMEM((blocks, BLK, 96), BF16),
            pltpu.VMEM((window, 96, 2 * BLK), BF16),
            pltpu.VMEM((blocks, BLK, BLK), F32),
        ],
        compiler_params=params(16),
        name="nearness",
    )(targets, sources, near_sources, centre_sources, *packs, *velocities)
    return vel, near.reshape(seg)


def solution(mesh):
    in_specs = (
        P(None, "cells"),
        P(None, "cells"),
        P(None, "cells"),
        P("cells", "lanes"),
        P(None, "cells"),
        P(None, "cells"),
        P("cells"),
        P("cells"),
        P("cells"),
    )
    out_specs = (P(None, "cells"), P("cells"))
    return jax.shard_map(local, mesh=mesh, in_specs=in_specs, out_specs=out_specs, check_vma=False)
```

time: 40.6 us -> 39 us (0.961)
  local copies, waits for them, and re-layouts: 2.68 us -> 0.67 us
  waiting for transfers between devices: 15.3 us -> 16.6 us
  Pallas kernels: 9.23 us -> 8.44 us
    unnamed x8, local copies, waits for them, and re-layouts: 2.68 us -> 0.67 us
    ppermute x12, waiting for transfers between devices: 15.3 us -> 16.6 us  [shifted(): return lax.ppermute(block, ('cells', 'lanes'), route)]
    pallas_call x1, Pallas kernels: 4.16 us -> 3.75 us  [local(): pl.pallas_call(functools.partial(near_kernel, high_count), out_shape=(jax...]
  transfers between devices with their start and end apart: 12 -> 12, of which waited for: 8 -> 9; matrix products, arithmetic and copies ran while one was open for 0% -> 0% of each run, Pallas kernels for 2% -> 1%
where the time goes in v4:
time: 39 us; the launch traced here: 38.7 us
  waiting for transfers between devices  16.6 us (43%)
  starting transfers between devices  11.5 us (29%)
  Pallas kernels  8.44 us (22%)
  other arithmetic  0.82 us (2%)
  between operations  0.72 us (2%)
  local copies, waits for them, and re-layouts  0.67 us (2%)
    ppermute x12, waiting for transfers between devices, shifted(): return lax.ppermute(block, ('cells', 'lanes'), route)  16.6 us
    ppermute x12, starting transfers between devices, shifted(): return lax.ppermute(block, ('cells', 'lanes'), route)  11.5 us
    pallas_call x1, Pallas kernels, local(): pl.pallas_call(functools.partial(force_kernel, lanes, high_count), out_sh...  4.21 us
    pallas_call x1, Pallas kernels, local(): pl.pallas_call(functools.partial(near_kernel, high_count), out_shape=(jax...  3.75 us
    add x1, other arithmetic, local(): fields = fields + rows_of([seg_nodes, node_owner], 9, FIELDS).astype(F32)  0.82 us
  transfers between devices with their start and end apart: 12, of which 9 were waited for; matrix products, arithmetic and copies ran while one was open for 0% of the time, Pallas kernels for 1%

profile of v4, /device:TPU:0, one launch (start us, length us, event | category | flops | bytes accessed | tf_op | source)
XLA Modules:
  0.0 38.7 jit_solution(13762741724117758873)
XLA Ops:
  0.6 0.8 %convert_add_fusion.fields = f32[13,1024]{1,0:T(8,128)S(1)} fusion(s32[2,1024]{1,0:T(2,128)} %param.14, s32[2,1024]{1,0:T(2,128)} %param.13, f32[3,1024]{1,0:T(4,128)} %param.10, f32[3,1024]{1,0:T(4,128)} %param.11, f32[3,1024]{1,0:T(4,128)} %param.9), kind=kLoop, calls=%fused_computation | loop fusion | flops 66560 | bytes 106496 | tf_op jit(solution)/shard_map/add | solution.py:311
  1.4 0.0 copy-start.1
  1.5 0.0 copy-start
  1.5 6.1 %collective-permute-start.3 = (f32[104,128]{1,0:T(8,128)S(1)}, f32[104,128]{1,0:T(8,128)S(1)}, u32[]{:S(2)}, u32[]{:S(2)}) collective-permute-start(f32[104,128]{1,0:T(8,128)S(1)} %pack.1.own.refs_2_), channel_id=1, source_target_pairs={{4,0},{5,1},{6,2},{7,3},{8,4},{9,5},{10,6},{11,7},{12,8},{13,9},{1... | collective-permute-start | bytes 159752 | tf_op jit(solution)/shard_map/ppermute | solution.py:37
  7.6 0.0 collective-permute-start.2
  7.6 0.5 %collective-permute-start.1 = (f32[104,128]{1,0:T(8,128)S(1)}, f32[104,128]{1,0:T(8,128)S(1)}, u32[]{:S(2)}, u32[]{:S(2)}) collective-permute-start(f32[104,128]{1,0:T(8,128)S(1)} %pack.1.own.refs_2_), channel_id=1, source_target_pairs={{30,0},{31,1},{0,2},{1,3},{2,4},{3,5},{4,6},{5,7},{6,8},{7,9},{8,1... | collective-permute-start | bytes 159752 | tf_op jit(solution)/shard_map/ppermute | solution.py:37
  8.1 0.7 %collective-permute-start = (f32[104,128]{1,0:T(8,128)S(1)}, f32[104,128]{1,0:T(8,128)S(1)}, u32[]{:S(2)}, u32[]{:S(2)}) collective-permute-start(f32[104,128]{1,0:T(8,128)S(1)} %pack.1.own.refs_2_), channel_id=1, source_target_pairs={{28,0},{29,1},{30,2},{31,3},{0,4},{1,5},{2,6},{3,7},{4,8},{5,9},{6... | collective-permute-start | bytes 159752 | tf_op jit(solution)/shard_map/ppermute | solution.py:37
  8.8 0.0 copy-start.2
  8.8 0.0 copy-start.3
  8.8 0.0 copy-done.1
  8.8 0.0 copy-done
  8.8 0.6 %copy-done.2 = s32[32]{0:T(128)S(1)} copy-done((s32[32]{0:T(128)S(1)}, s32[32]{0:T(128)}, u32[]{:S(2)}) %copy-start.2) | copy-done | bytes 152
  9.4 0.0 copy-done.3
  9.4 0.3 early.1
  9.8 0.0 collective-permute-done.3.refs_4_
  9.8 0.1 collective-permute-done.2.refs_3_
  9.9 4.0 %collective-permute-done.1.refs_1_ = f32[104,128]{1,0:T(8,128)S(1)} collective-permute-done((f32[104,128]{1,0:T(8,128)S(1)}, f32[104,128]{1,0:T(8,128)S(1)}, u32[]{:S(2)}, u32[]{:S(2)}) %collective-permute-start.1) | collective-permute-done | bytes 53280 | tf_op jit(solution)/shard_map/ppermute | solution.py:37
  13.8 1.5 %collective-permute-done.refs_0_ = f32[104,128]{1,0:T(8,128)S(1)} collective-permute-done((f32[104,128]{1,0:T(8,128)S(1)}, f32[104,128]{1,0:T(8,128)S(1)}, u32[]{:S(2)}, u32[]{:S(2)}) %collective-permute-start) | collective-permute-done | bytes 53280 | tf_op jit(solution)/shard_map/ppermute | solution.py:37
  15.3 4.2 %forces.1 = (f32[4,8,128]{2,1,0:T(8,128)S(1)}, f32[4,8,128]{2,1,0:T(8,128)S(1)}) custom-call(s32[8,8]{1,0:T(8,128)S(1)} %get-tuple-element.19.lists, bf16[8,128,48]{2,1,0:T(8,128)(2,1)S(1)} %get-tuple-element.20.lhs_s, bf16[2,128,1024]{2,1,0:T(8,128)(2,1)S(1)} %get-tuple-element.21.onehots, f32[104,128]{1,0:T(8,128)S(1)} %collective-permute-done.refs_0_, ...), custom_call_target="tpu_custom_call" | custom-call | tf_op jit(solution)/shard_map/forces/pallas_call | solution.py:341
  19.5 1.6 %collective-permute-start.4 = (f32[4,8,128]{2,1,0:T(8,128)S(1)}, f32[4,8,128]{2,1,0:T(8,128)S(1)}, u32[]{:S(2)}, u32[]{:S(2)}) collective-permute-start(f32[4,8,128]{2,1,0:T(8,128)S(1)} %get-tuple-element.22.refs_0_), channel_id=1, source_target_pairs={{1,0},{0,1},{3,2},{2,3},{5,4},{4,5},{7,6},{6,7},{9,8},{8,9},{11,10... | collective-permute-start | bytes 49160 | tf_op jit(solution)/shard_map/ppermute | solution.py:37
  21.1 0.0 collective-permute-start.6
  21.1 0.0 collective-permute-start.5
  21.1 2.2 %collective-permute-done.4.refs_1_ = f32[4,8,128]{2,1,0:T(8,128)S(1)} collective-permute-done((f32[4,8,128]{2,1,0:T(8,128)S(1)}, f32[4,8,128]{2,1,0:T(8,128)S(1)}, u32[]{:S(2)}, u32[]{:S(2)}) %collective-permute-start.4) | collective-permute-done | bytes 16416 | tf_op jit(solution)/shard_map/ppermute | solution.py:37
  23.3 4.5 %collective-permute-done.6.refs_3_ = f32[4,8,128]{2,1,0:T(8,128)S(1)} collective-permute-done((f32[4,8,128]{2,1,0:T(8,128)S(1)}, f32[4,8,128]{2,1,0:T(8,128)S(1)}, u32[]{:S(2)}, u32[]{:S(2)}) %collective-permute-start.6) | collective-permute-done | bytes 16416 | tf_op jit(solution)/shard_map/ppermute | solution.py:37
  27.8 0.0 collective-permute-done.5.refs_2_
  27.9 0.1 collective-permute-start.11
  27.9 0.1 collective-permute-start.10
  28.0 0.1 collective-permute-start.9
  28.1 0.5 %collective-permute-start.8 = (f32[3,8,128]{2,1,0:T(8,128)S(1)}, f32[3,8,128]{2,1,0:T(8,128)S(1)}, u32[]{:S(2)}, u32[]{:S(2)}) collective-permute-start(f32[3,8,128]{2,1,0:T(8,128)S(1)} %velocity.1.refs_7_), channel_id=1, source_target_pairs={{30,0},{31,1},{0,2},{1,3},{2,4},{3,5},{4,6},{5,7},{6,8},{7,9},{8,1... | collective-permute-start | bytes 36872 | tf_op jit(solution)/shard_map/ppermute | solution.py:37
  28.6 2.0 %collective-permute-start.7 = (f32[3,8,128]{2,1,0:T(8,128)S(1)}, f32[3,8,128]{2,1,0:T(8,128)S(1)}, u32[]{:S(2)}, u32[]{:S(2)}) collective-permute-start(f32[3,8,128]{2,1,0:T(8,128)S(1)} %velocity.1.refs_7_), channel_id=1, source_target_pairs={{28,0},{29,1},{30,2},{31,3},{0,4},{1,5},{2,6},{3,7},{4,8},{5,9},{6... | collective-permute-start | bytes 36872 | tf_op jit(solution)/shard_map/ppermute | solution.py:37
  30.5 0.2 select.6
  30.7 0.4 collective-permute-done.11.refs_10_
  31.0 0.6 %collective-permute-done.10.refs_9_ = f32[3,8,128]{2,1,0:T(8,128)S(1)} collective-permute-done((f32[3,8,128]{2,1,0:T(8,128)S(1)}, f32[3,8,128]{2,1,0:T(8,128)S(1)}, u32[]{:S(2)}, u32[]{:S(2)}) %collective-permute-start.10) | collective-permute-done | bytes 12320 | tf_op jit(solution)/shard_map/ppermute | solution.py:37
  31.7 0.0 collective-permute-done.9.refs_8_
  31.7 2.2 %collective-permute-done.8.refs_6_ = f32[3,8,128]{2,1,0:T(8,128)S(1)} collective-permute-done((f32[3,8,128]{2,1,0:T(8,128)S(1)}, f32[3,8,128]{2,1,0:T(8,128)S(1)}, u32[]{:S(2)}, u32[]{:S(2)}) %collective-permute-start.8) | collective-permute-done | bytes 12320 | tf_op jit(solution)/shard_map/ppermute | solution.py:37
  33.9 1.0 %collective-permute-done.7.refs_5_ = f32[3,8,128]{2,1,0:T(8,128)S(1)} collective-permute-done((f32[3,8,128]{2,1,0:T(8,128)S(1)}, f32[3,8,128]{2,1,0:T(8,128)S(1)}, u32[]{:S(2)}, u32[]{:S(2)}) %collective-permute-start.7) | collective-permute-done | bytes 12320 | tf_op jit(solution)/shard_map/ppermute | solution.py:37
  34.9 3.8 %nearness.1 = (f32[8,128]{1,0:T(8,128)}, f32[3,1024]{1,0:T(4,128)}) custom-call(s32[1,32]{1,0:T(1,128)S(1)} %get-tuple-element.14.targets, s32[1,32]{1,0:T(1,128)S(1)} %get-tuple-element.15.sources, bf16[40,48,128]{2,1,0:T(8,128)(2,1)S(1)} %get-tuple-element.16.near_s, f32[40,24,128]{2,1,0:T(8,128)S(1)} %get-tuple-element.17.centre_s, ...), custom_call_target="tpu_custom_call" | custom-call | tf_op jit(solution)/shard_map/nearness/pallas_call | solution.py:380
  (2 shorter events, 0.0 us)
Async XLA Ops:
  1.4 7.3 %copy-start.1 = (f32[1024]{0:T(1024)S(1)}, f32[1024]{0:T(1024)}, u32[]{:S(2)}) copy-start(f32[1024]{0:T(1024)} %param.15) | copy-start | bytes 12292
  1.5 7.3 %copy-start = (s32[8,8]{1,0:T(8,128)S(1)}, s32[8,8]{1,0:T(8,128)}, u32[]{:S(2)}) copy-start(s32[8,8]{1,0:T(8,128)} %refs_0_.1) | copy-start | bytes 772
  1.5 8.3 %collective-permute-start.3 = (f32[104,128]{1,0:T(8,128)S(1)}, f32[104,128]{1,0:T(8,128)S(1)}, u32[]{:S(2)}, u32[]{:S(2)}) collective-permute-start(f32[104,128]{1,0:T(8,128)S(1)} %pack.1.own.refs_2_), channel_id=1, source_target_pairs={{4,0},{5,1},{6,2},{7,3},{8,4},{9,5},{10,6},{11,7},{12,8},{13,9},{1... | collective-permute-start | bytes 159752 | tf_op jit(solution)/shard_map/ppermute | solution.py:37
  7.6 2.3 %collective-permute-start.2 = (f32[104,128]{1,0:T(8,128)S(1)}, f32[104,128]{1,0:T(8,128)S(1)}, u32[]{:S(2)}, u32[]{:S(2)}) collective-permute-start(f32[104,128]{1,0:T(8,128)S(1)} %pack.1.own.refs_2_), channel_id=1, source_target_pairs={{2,0},{3,1},{4,2},{5,3},{6,4},{7,5},{8,6},{9,7},{10,8},{11,9},{12,... | collective-permute-start | bytes 159752 | tf_op jit(solution)/shard_map/ppermute | solution.py:37
  7.6 6.3 %collective-permute-start.1 = (f32[104,128]{1,0:T(8,128)S(1)}, f32[104,128]{1,0:T(8,128)S(1)}, u32[]{:S(2)}, u32[]{:S(2)}) collective-permute-start(f32[104,128]{1,0:T(8,128)S(1)} %pack.1.own.refs_2_), channel_id=1, source_target_pairs={{30,0},{31,1},{0,2},{1,3},{2,4},{3,5},{4,6},{5,7},{6,8},{7,9},{8,1... | collective-permute-start | bytes 159752 | tf_op jit(solution)/shard_map/ppermute | solution.py:37
  8.1 7.2 %collective-permute-start = (f32[104,128]{1,0:T(8,128)S(1)}, f32[104,128]{1,0:T(8,128)S(1)}, u32[]{:S(2)}, u32[]{:S(2)}) collective-permute-start(f32[104,128]{1,0:T(8,128)S(1)} %pack.1.own.refs_2_), channel_id=1, source_target_pairs={{28,0},{29,1},{30,2},{31,3},{0,4},{1,5},{2,6},{3,7},{4,8},{5,9},{6... | collective-permute-start | bytes 159752 | tf_op jit(solution)/shard_map/ppermute | solution.py:37
  8.8 0.7 %copy-start.2 = (s32[32]{0:T(128)S(1)}, s32[32]{0:T(128)}, u32[]{:S(2)}) copy-start(s32[32]{0:T(128)} %param.16) | copy-start | bytes 388
  8.8 0.7 %copy-start.3 = (s32[32]{0:T(128)S(1)}, s32[32]{0:T(128)}, u32[]{:S(2)}) copy-start(s32[32]{0:T(128)} %param.17) | copy-start | bytes 388
  19.5 3.8 %collective-permute-start.4 = (f32[4,8,128]{2,1,0:T(8,128)S(1)}, f32[4,8,128]{2,1,0:T(8,128)S(1)}, u32[]{:S(2)}, u32[]{:S(2)}) collective-permute-start(f32[4,8,128]{2,1,0:T(8,128)S(1)} %get-tuple-element.22.refs_0_), channel_id=1, source_target_pairs={{1,0},{0,1},{3,2},{2,3},{5,4},{4,5},{7,6},{6,7},{9,8},{8,9},{11,10... | collective-permute-start | bytes 49160 | tf_op jit(solution)/shard_map/ppermute | solution.py:37
  21.1 6.8 %collective-permute-start.6 = (f32[4,8,128]{2,1,0:T(8,128)S(1)}, f32[4,8,128]{2,1,0:T(8,128)S(1)}, u32[]{:S(2)}, u32[]{:S(2)}) collective-permute-start(f32[4,8,128]{2,1,0:T(8,128)S(1)} %get-tuple-element.23), channel_id=1, source_target_pairs={{31,0},{30,1},{1,2},{0,3},{3,4},{2,5},{5,6},{4,7},{7,8},{6,9},{9,1... | collective-permute-start | bytes 49160 | tf_op jit(solution)/shard_map/ppermute | solution.py:37
  21.1 6.8 %collective-permute-start.5 = (f32[4,8,128]{2,1,0:T(8,128)S(1)}, f32[4,8,128]{2,1,0:T(8,128)S(1)}, u32[]{:S(2)}, u32[]{:S(2)}) collective-permute-start(f32[4,8,128]{2,1,0:T(8,128)S(1)} %get-tuple-element.23), channel_id=1, source_target_pairs={{30,0},{31,1},{0,2},{1,3},{2,4},{3,5},{4,6},{5,7},{6,8},{7,9},{8,1... | collective-permute-start | bytes 49160 | tf_op jit(solution)/shard_map/ppermute | solution.py:37
  27.9 3.2 %collective-permute-start.11 = (f32[3,8,128]{2,1,0:T(8,128)S(1)}, f32[3,8,128]{2,1,0:T(8,128)S(1)}, u32[]{:S(2)}, u32[]{:S(2)}) collective-permute-start(f32[3,8,128]{2,1,0:T(8,128)S(1)} %velocity.1.refs_7_), channel_id=1, source_target_pairs={{6,0},{7,1},{8,2},{9,3},{10,4},{11,5},{12,6},{13,7},{14,8},{15,9},... | collective-permute-start | bytes 36872 | tf_op jit(solution)/shard_map/ppermute | solution.py:37
  27.9 3.7 %collective-permute-start.10 = (f32[3,8,128]{2,1,0:T(8,128)S(1)}, f32[3,8,128]{2,1,0:T(8,128)S(1)}, u32[]{:S(2)}, u32[]{:S(2)}) collective-permute-start(f32[3,8,128]{2,1,0:T(8,128)S(1)} %velocity.1.refs_7_), channel_id=1, source_target_pairs={{4,0},{5,1},{6,2},{7,3},{8,4},{9,5},{10,6},{11,7},{12,8},{13,9},{1... | collective-permute-start | bytes 36872 | tf_op jit(solution)/shard_map/ppermute | solution.py:37
  28.0 3.7 %collective-permute-start.9 = (f32[3,8,128]{2,1,0:T(8,128)S(1)}, f32[3,8,128]{2,1,0:T(8,128)S(1)}, u32[]{:S(2)}, u32[]{:S(2)}) collective-permute-start(f32[3,8,128]{2,1,0:T(8,128)S(1)} %velocity.1.refs_7_), channel_id=1, source_target_pairs={{2,0},{3,1},{4,2},{5,3},{6,4},{7,5},{8,6},{9,7},{10,8},{11,9},{12,... | collective-permute-start | bytes 36872 | tf_op jit(solution)/shard_map/ppermute | solution.py:37
  28.1 5.9 %collective-permute-start.8 = (f32[3,8,128]{2,1,0:T(8,128)S(1)}, f32[3,8,128]{2,1,0:T(8,128)S(1)}, u32[]{:S(2)}, u32[]{:S(2)}) collective-permute-start(f32[3,8,128]{2,1,0:T(8,128)S(1)} %velocity.1.refs_7_), channel_id=1, source_target_pairs={{30,0},{31,1},{0,2},{1,3},{2,4},{3,5},{4,6},{5,7},{6,8},{7,9},{8,1... | collective-permute-start | bytes 36872 | tf_op jit(solution)/shard_map/ppermute | solution.py:37
  28.6 6.4 %collective-permute-start.7 = (f32[3,8,128]{2,1,0:T(8,128)S(1)}, f32[3,8,128]{2,1,0:T(8,128)S(1)}, u32[]{:S(2)}, u32[]{:S(2)}) collective-permute-start(f32[3,8,128]{2,1,0:T(8,128)S(1)} %velocity.1.refs_7_), channel_id=1, source_target_pairs={{28,0},{29,1},{30,2},{31,3},{0,4},{1,5},{2,6},{3,7},{4,8},{5,9},{6... | collective-permute-start | bytes 36872 | tf_op jit(solution)/shard_map/ppermute | solution.py:37

commit v5 on v4

v5 whole, which is shorter than its diff:
```python
import functools
import math

import jax
import jax.numpy as jnp
from jax import lax
from jax.experimental import pallas as pl
from jax.experimental.pallas import tpu as pltpu
from jax.sharding import PartitionSpec as P

BLK = 128
FIELDS = 9
GROUP = 8
REACH = 2
FORCE_SCALE = 0.02
CORE_SQUARE = 0.25
TIME_STEP = 4.0
MIDDLE = 2.0
LOG2E = math.log2(math.e)

F32 = jnp.float32
BF16 = jnp.bfloat16
VM = pl.BlockSpec(memory_space=pltpu.VMEM)
SM = pl.BlockSpec(memory_space=pltpu.SMEM)


def long_call():
    return pl.CostEstimate(flops=1 << 28, bytes_accessed=1 << 23, transcendentals=0)


def params(mib):
    return pltpu.CompilerParams(vmem_limit_bytes=mib << 20)


def shifted(block, cell_step, lane_step):
    cells, lanes = lax.axis_size("cells"), lax.axis_size("lanes")
    route = []
    for c in range(cells):
        for l in range(lanes):
            source = ((c + cell_step) % cells) * lanes + (l + lane_step) % lanes
            route.append((source, c * lanes + l))
    return lax.ppermute(block, ("cells", "lanes"), route)


def split3(x):
    high = x.astype(BF16).astype(F32)
    rest = x - high
    mid = rest.astype(BF16).astype(F32)
    return high, mid, rest - mid


def row(ref, field, k):
    blocks = ref.shape[0] // FIELDS
    return ref[pl.ds(field * blocks + k, 8, stride=0), :]


def rows_at(ref, field, k):
    blocks = ref.shape[0] // FIELDS
    return ref[pl.ds(field * blocks + k, 8, stride=blocks), :]


def cross(a, b):
    return [
        a[1] * b[2] - a[2] * b[1],
        a[2] * b[0] - a[0] * b[2],
        a[0] * b[1] - a[1] * b[0],
    ]


def dot3(a, b):
    return a[0] * b[0] + a[1] * b[1] + a[2] * b[2]


def choose(rows, values, other):
    for number, value in values.items():
        other = jnp.where(rows == number, value, other)
    return other


def contract_lanes(a, b):
    return lax.dot_general(a, b, (((1,), (1,)), ((), ())), preferred_element_type=F32)


def end_address(ref, first, end, k, high_count):
    node = ref[first + end, pl.ds(k, 8, stride=0), :].astype(jnp.int32)
    owner = ref[first + 2 + end, pl.ds(k, 8, stride=0), :].astype(jnp.int32)
    return owner * high_count + lax.shift_right_logical(node, BLK.bit_length() - 1), node & (BLK - 1)


def compact(entries, keep, base, discard, t_list, w_list):
    place = jnp.int32(0)
    for t, w in entries:
        t_list[place] = t
        w_list[place] = w - base
        place = place + keep(w).astype(jnp.int32)
    for u in range(GROUP):
        t_list[place + u] = jnp.int32(discard)
        w_list[place + u] = jnp.int32(0)
    return lax.div(place + (GROUP - 1), jnp.int32(GROUP))


def six_left(x):
    h, m, l = split3(x)
    return jnp.concatenate([h, h, m, h, l, m], 0)


def right_order(parts):
    h, m, l = parts
    return jnp.concatenate([h, m, h, l, h, m], 0).astype(BF16)


def pack_kernel(fields, out, numbers):
    blocks = fields.shape[1] // BLK
    for k in range(blocks):
        piece = fields[:, k * BLK : (k + 1) * BLK]
        rows = lax.broadcasted_iota(jnp.int32, piece.shape, 0)
        moved = jnp.where(rows < 3, piece - MIDDLE, piece)
        out[pl.ds(k, FIELDS, stride=blocks), :] = moved[0:FIELDS]
        for n in range(4):
            numbers[n, k : k + 1, :] = piece[FIELDS + n : FIELDS + n + 1]


def early_kernel(high_count, own, numbers, *refs):
    count = (len(refs) - 2) // 2
    for source, out in zip(refs[:count], refs[count : 2 * count]):
        out[...] = source[...]
    lhs_out, onehots = refs[2 * count :]
    rows = lax.broadcasted_iota(jnp.int32, (8, BLK), 0)
    nodes = lax.broadcasted_iota(jnp.int32, (BLK, BLK), 0)
    for k in range(own.shape[0] // FIELDS):
        c = [row(own, x, k) for x in range(3)]
        l = {3 + x: row(own, 6 + x, k) for x in range(3)}
        target = choose(rows, {**l, 6: 1.0, 7: dot3(c, c) + CORE_SQUARE}, rows_at(own, 0, k))
        lhs_out[k] = six_left(target).T
        for end in range(2):
            low = end_address(numbers, 0, end, k, high_count)[1]
            onehots[end, :, k * BLK : (k + 1) * BLK] = (nodes == low[0:1]).astype(F32).astype(BF16)


def force_tiles(lists, lhs, packs, keep, base, lhs_s, rhs_s, src_s, acc_s, t_list, w_list):
    blocks = lhs.shape[0]
    rows = lax.broadcasted_iota(jnp.int32, (8, BLK), 0)
    acc_s[...] = jnp.zeros_like(acc_s)
    entries = ((jnp.int32(t), lists[t, e]) for t in range(blocks) for e in range(lists.shape[1]))
    groups = compact(entries, keep, base, blocks, t_list, w_list)
    for t in range(blocks):
        lhs_s[t] = lhs[t].astype(BF16)
    for d, ref in enumerate(packs):
        for k in range(blocks):
            c = [row(ref, x, k) for x in range(3)]
            l = [row(ref, 6 + x, k) for x in range(3)]
            upper, lower = rows_at(ref, 0, k), rows_at(ref, 1, k)
            near = jnp.where(rows < 3, -2.0 * upper, choose(rows, {6: dot3(c, c), 7: 1.0}, 0.0))
            along = jnp.where((rows >= 3) & (rows < 6), upper, 0.0)
            moment = cross(l, c)
            sums = choose(rows, {1 + x: moment[x] for x in range(3)}, lower)
            w = d * blocks + k
            rhs_s[w, :, 0:BLK] = right_order(split3(near))
            rhs_s[w, :, BLK : 2 * BLK] = right_order(split3(along))
            src_s[w] = jnp.concatenate([*split3(sums), jnp.zeros((8, BLK), F32)], 0).astype(BF16)

    def some_tiles(step, carry):
        for u in range(GROUP):
            t = t_list[step * GROUP + u]
            w = w_list[step * GROUP + u]
            both = jnp.dot(
                lhs_s[jnp.minimum(t, blocks - 1)], rhs_s[w], preferred_element_type=F32
            )
            inverse = lax.rsqrt(both[:, :BLK])
            weight = both[:, BLK:] * inverse * (inverse * inverse)
            high = weight.astype(BF16)
            low = (weight - high.astype(F32)).astype(BF16)
            src = src_s[w]
            acc_s[t] += contract_lanes(
                jnp.concatenate([high, low], 1), jnp.concatenate([src, src], 1)
            )
        return carry

    lax.fori_loop(0, groups, some_tiles, 0)


def first_forces(lists, lhs, *refs):
    packs, acc_out, scratch = refs[: REACH + 1], refs[REACH + 1], refs[REACH + 2 :]
    lhs_s, rhs_s, src_s, t_list, w_list = scratch
    base = REACH * lhs.shape[0]
    force_tiles(
        lists, lhs, packs, lambda w: w >= base, base, lhs_s, rhs_s, src_s, acc_out, t_list, w_list
    )


def last_forces(lanes, high_count, lists, lhs, onehots, numbers, own, first_acc, *refs):
    packs, (own_out, next_out), scratch = refs[:REACH], refs[REACH : REACH + 2], refs[REACH + 2 :]
    lhs_s, rhs_s, src_s, acc_s, force_s, t_list, w_list = scratch
    blocks = lhs.shape[0]
    base = REACH * blocks
    rows = lax.broadcasted_iota(jnp.int32, (8, BLK), 0)
    force_tiles(
        lists, lhs, packs, lambda w: w < base, 0, lhs_s, rhs_s, src_s, acc_s, t_list, w_list
    )
    for t in range(blocks):
        total = (first_acc[t] + acc_s[t]).T
        force_s[t] = total[0:8] + (total[8:16] + total[16:24])

    out = None
    for k in range(blocks):
        whole = force_s.at[k]
        line = [whole[pl.ds(5 + x, 8, stride=0), :] for x in range(3)]
        moment = [whole[pl.ds(1 + x, 8, stride=0), :] for x in range(3)]
        c = [row(own, x, k) for x in range(3)]
        l = [row(own, 6 + x, k) for x in range(3)]
        turned = cross(line, c)
        values = [(0.5 * FORCE_SCALE) * (turned[x] - moment[x]) for x in range(3)]
        values.append(jnp.sqrt(dot3(l, l)) * (0.5 / lanes))
        tops = [value.astype(BF16).astype(F32) for value in values]
        parts = tops + [value - top for value, top in zip(values, tops)]
        pieces = []
        for end in range(2):
            high = end_address(numbers, 0, end, k, high_count)[0]
            masks = [rows + first == high for first in range(0, 2 * high_count, 8)]
            pieces.append([jnp.where(mask, part, 0.0) for part in parts for mask in masks])
        left = jnp.concatenate([jnp.concatenate(p, 0) for p in pieces], 1).astype(BF16)
        cut = slice(k * BLK, (k + 1) * BLK)
        term = contract_lanes(left, jnp.concatenate([onehots[end, :, cut] for end in range(2)], 1))
        out = term if out is None else out + term
    n = 8 * high_count
    out = out[0:n] + out[n : 2 * n]
    for k in range(4):
        first = 2 * high_count * k
        own_out[k] = out[first : first + high_count]
        next_out[k] = out[first + high_count : first + 2 * high_count]


def select_kernel(*refs):
    packs, (near_out, centre_out) = refs[:-2], refs[-2:]
    blocks = packs[0].shape[0] // FIELDS
    rows = lax.broadcasted_iota(jnp.int32, (8, BLK), 0)
    for d, ref in enumerate(packs):
        for k in range(blocks):
            w = d * blocks + k
            c = [row(ref, x, k) for x in range(3)]
            centre = LOG2E * rows_at(ref, 0, k)
            extra = choose(rows, {6: LOG2E * dot3(c, c), 7: LOG2E}, 0.0)
            near_out[w] = right_order(split3(jnp.where(rows < 3, -2.0 * centre, extra)))
            parts = split3(jnp.where(rows < 3, centre, choose(rows, {6: -LOG2E}, 0.0)))
            centre_out[w] = jnp.concatenate(parts, 0)


def near_tiles(
    high_count, targets, sources, keep, first_domain, near_s, centre_s, packs, nodes, make_target,
    tgt_s, src_s, acc_s, t_list, w_list,
):
    blocks = packs[0].shape[0] // FIELDS
    base = first_domain * blocks
    rows = lax.broadcasted_iota(jnp.int32, (8, BLK), 0)
    acc_s[...] = jnp.zeros_like(acc_s)
    entries = ((targets[0, k], sources[0, k]) for k in range(targets.shape[1]))
    groups = compact(entries, keep, base, blocks, t_list, w_list)
    zero = jnp.zeros((8, BLK), F32)
    nothing = jnp.zeros((48, BLK), BF16)
    signs = choose(rows, {4: -LOG2E}, zero + LOG2E)
    turn = jnp.where(rows < 3, -2.0, choose(rows, {3: 1.0}, zero))
    constant = split3(choose(rows, {5: LOG2E}, zero))
    for d, ref in enumerate(packs):
        for k in range(blocks):
            w = d * blocks + k
            v = [zero] * 3
            for end in range(2):
                high, low = end_address(nodes[d], 3, end, k, high_count)
                for owner in range(2):
                    for first in range(0, high_count, 8):
                        mask = rows + (owner * high_count + first) == high
                        for x in range(3):
                            table = nodes[d + owner][x, first : first + 8, :]
                            got = jnp.take_along_axis(table, low, axis=1, mode="promise_in_bounds")
                            v[x] = v[x] + jnp.where(mask, got, 0.0)
            for x in range(3):
                for shift in (4, 2, 1):
                    v[x] = v[x] + pltpu.roll(v[x], shift, 0)
                v[x] = v[x] * (0.5 * TIME_STEP)
            c = [row(ref, x, k) for x in range(3)]
            vv, cv = dot3(v, v), dot3(c, v)
            moved = choose(rows, {0: v[0], 1: v[1], 2: v[2], 3: vv}, cv)
            parts = split3(moved * signs)
            centre = centre_s[base + w]
            still = [centre[8 * n : 8 * n + 8] for n in range(3)]
            src_s[w, 0:48, 0:BLK] = right_order([jnp.where(rows < 3, p, 0.0) for p in parts])
            src_s[w, 48:96, 0:BLK] = right_order(
                [jnp.where(rows == 4, p, q) for p, q in zip(parts, still)]
            )
            src_s[w, 0:48, BLK : 2 * BLK] = nothing
            src_s[w, 48:96, BLK : 2 * BLK] = right_order(
                [p * turn + q for p, q in zip(parts, constant)]
            )
            if make_target is not None and d == 0:
                first = choose(rows, {6: 1.0, 7: dot3(c, c)}, rows_at(ref, 0, k))
                second = choose(rows, {3: 1.0, 4: 1.0, 5: vv, 6: cv, 7: 0.0}, moved)
                make_target(k, jnp.concatenate([six_left(first), six_left(second)], 0).T)

    def some_pairs(step, carry):
        for u in range(GROUP):
            t = t_list[step * GROUP + u]
            w = w_list[step * GROUP + u]
            target = tgt_s[jnp.minimum(t, blocks - 1)]
            rr = jnp.dot(target[:, 0:48], near_s[base + w], preferred_element_type=F32)
            both = jnp.dot(target, src_s[w], preferred_element_type=F32)
            toward = both[:, 0:BLK]
            square = jnp.maximum(both[:, BLK : 2 * BLK], 0.0)
            s = jnp.clip(toward / (square + LOG2E * CORE_SQUARE), 0.0, 1.0)
            acc_s[t] += jnp.exp2(s * (toward + (toward - s * square)) - rr)
        return carry

    lax.fori_loop(0, groups, some_pairs, 0)


def first_near(high_count, targets, sources, near_s, centre_s, *refs):
    packs, nodes = refs[: REACH + 1], refs[REACH + 1 : 2 * REACH + 3]
    acc_out, tgt_out, vel_out, tgt_s, src_s, t_list, w_list = refs[2 * REACH + 3 :]
    base = REACH * (packs[0].shape[0] // FIELDS)
    for k in range(high_count):
        for x in range(3):
            vel_out[x : x + 1, k * BLK : (k + 1) * BLK] = nodes[0][x, k : k + 1, :]

    def make_target(k, value):
        tgt_out[k] = value
        tgt_s[k] = value.astype(BF16)

    near_tiles(
        high_count, targets, sources, lambda w: w >= base, REACH, near_s, centre_s, packs, nodes,
        make_target, tgt_s, src_s, acc_out, t_list, w_list,
    )


def last_near(high_count, targets, sources, near_s, centre_s, first_acc, tgt, *refs):
    packs, nodes = refs[:REACH], refs[REACH : 2 * REACH + 1]
    near_out, tgt_s, src_s, acc_s, t_list, w_list = refs[2 * REACH + 1 :]
    blocks = tgt.shape[0]
    for t in range(blocks):
        tgt_s[t] = tgt[t].astype(BF16)
    near_tiles(
        high_count, targets, sources, lambda w: w < REACH * blocks, 0, near_s, centre_s, packs, nodes,
        None, tgt_s, src_s, acc_s, t_list, w_list,
    )
    for t in range(blocks):
        near_out[t : t + 1] = jnp.sum((first_acc[t] + acc_s[t]).T, axis=0, keepdims=True)


def velocity_kernel(mobility, numbers, *refs):
    out = refs[-1]
    total = refs[0][...]
    for ref in refs[1:-1]:
        total = total + ref[...]
    scale = mobility[...] / (1.0 + total[3])
    for x in range(3):
        out[x] = total[x] * scale
    out[3:7] = numbers[...]


def rows_of(pieces, first, rows):
    total = None
    for piece in pieces:
        last = first + piece.shape[0]
        padded = jnp.pad(piece, ((first, rows - last), (0, 0)))
        total = padded if total is None else total + padded
        first = last
    return total


def local(
    centres, seg_lines, burgers, neighbour_blocks, seg_nodes, node_owner, mobility, cand_target, cand_source
):
    seg = centres.shape[1]
    blocks = seg // BLK
    high_count = mobility.shape[0] // BLK
    lanes = lax.axis_size("lanes")
    window = (2 * REACH + 1) * blocks
    fields = rows_of([centres, burgers, seg_lines], 0, FIELDS + 4)
    fields = fields + rows_of([seg_nodes, node_owner], FIELDS, FIELDS + 4).astype(F32)
    own, numbers = pl.pallas_call(
        pack_kernel,
        out_shape=(
            jax.ShapeDtypeStruct((FIELDS * blocks, BLK), F32),
            jax.ShapeDtypeStruct((4, blocks, BLK), F32),
        ),
        in_specs=[VM],
        out_specs=(VM, VM),
        compiler_params=params(4),
        name="pack",
    )(fields)
    packs = [own if o == 0 else shifted(own, o, 0) for o in range(-REACH, REACH + 1)]
    small = [
        neighbour_blocks,
        mobility.reshape(high_count, BLK),
        cand_target.reshape(1, -1),
        cand_source.reshape(1, -1),
    ]
    lists, rate, targets, sources, lhs, own_onehots = pl.pallas_call(
        functools.partial(early_kernel, high_count),
        out_shape=[jax.ShapeDtypeStruct(x.shape, x.dtype) for x in small]
        + [
            jax.ShapeDtypeStruct((blocks, BLK, 48), F32),
            jax.ShapeDtypeStruct((2, BLK, seg), BF16),
        ],
        in_specs=[VM] * (2 + len(small)),
        out_specs=[VM] * (2 + len(small)),
        compiler_params=params(8),
        cost_estimate=long_call(),
        name="early",
    )(own, numbers, *small)

    entry_room = pltpu.SMEM((lists.shape[0] * lists.shape[1] + GROUP,), jnp.int32)
    accumulator = (blocks + 1, BLK, 32)

    def force_scratch(domains):
        return [
            pltpu.VMEM((blocks, BLK, 48), BF16),
            pltpu.VMEM((domains * blocks, 48, 2 * BLK), BF16),
            pltpu.VMEM((domains * blocks, 32, BLK), BF16),
        ]

    first_acc = pl.pallas_call(
        first_forces,
        out_shape=jax.ShapeDtypeStruct(accumulator, F32),
        in_specs=[SM] + [VM] * (2 + REACH),
        out_specs=VM,
        scratch_shapes=force_scratch(REACH + 1) + [entry_room] * 2,
        compiler_params=params(16),
        cost_estimate=long_call(),
        name="first_forces",
    )(lists, lhs, *packs[REACH:])
    part = jax.ShapeDtypeStruct((4, high_count, BLK), F32)
    own_part, next_part = pl.pallas_call(
        functools.partial(last_forces, lanes, high_count),
        out_shape=(part, part),
        in_specs=[SM] + [VM] * (5 + REACH),
        out_specs=(VM, VM),
        scratch_shapes=force_scratch(REACH)
        + [pltpu.VMEM(accumulator, F32), pltpu.VMEM((blocks, 8, BLK), F32)]
        + [entry_room] * 2,
        compiler_params=params(16),
        name="last_forces",
    )(lists, lhs, own_onehots, numbers, own, first_acc, *packs[:REACH])
    terms = [own_part]
    terms += [shifted(own_part, 0, lane) for lane in range(1, lanes)]
    terms += [shifted(next_part, -1, lane) for lane in range(lanes)]
    velocity = pl.pallas_call(
        velocity_kernel,
        out_shape=jax.ShapeDtypeStruct((7, high_count, BLK), F32),
        in_specs=[VM] * (2 + len(terms)),
        out_specs=VM,
        compiler_params=params(4),
        name="velocity",
    )(rate, numbers, *terms)
    nodes = [
        velocity if o == 0 else shifted(velocity, o, 0) for o in range(-REACH, REACH + 2)
    ]
    near_sources, centre_sources = pl.pallas_call(
        select_kernel,
        out_shape=(
            jax.ShapeDtypeStruct((window, 48, BLK), BF16),
            jax.ShapeDtypeStruct((window, 24, BLK), F32),
        ),
        in_specs=[VM] * len(packs),
        out_specs=(VM, VM),
        compiler_params=params(16),
        cost_estimate=long_call(),
        name="select",
    )(*packs)

    pair_room = pltpu.SMEM((targets.shape[1] + GROUP,), jnp.int32)
    accumulator = (blocks + 1, BLK, BLK)

    def near_scratch(domains):
        return [
            pltpu.VMEM((blocks, BLK, 96), BF16),
            pltpu.VMEM((domains * blocks, 96, 2 * BLK), BF16),
        ]

    first_sum, target_rows, vel = pl.pallas_call(
        functools.partial(first_near, high_count),
        out_shape=(
            jax.ShapeDtypeStruct(accumulator, F32),
            jax.ShapeDtypeStruct((blocks, BLK, 96), F32),
            jax.ShapeDtypeStruct((3, high_count * BLK), F32),
        ),
        in_specs=[SM, SM] + [VM] * (5 + 2 * REACH),
        out_specs=(VM, VM, VM),
        scratch_shapes=near_scratch(REACH + 1) + [pair_room] * 2,
        compiler_params=params(16),
        cost_estimate=long_call(),
        name="first_near",
    )(targets, sources, near_sources, centre_sources, *packs[REACH:], *nodes[REACH:])
    near = pl.pallas_call(
        functools.partial(last_near, high_count),
        out_shape=jax.ShapeDtypeStruct((blocks, BLK), F32),
        in_specs=[SM, SM] + [VM] * (5 + 2 * REACH),
        out_specs=VM,
        scratch_shapes=near_scratch(REACH) + [pltpu.VMEM(accumulator, F32)] + [pair_room] * 2,
        compiler_params=params(16),
        name="last_near",
    )(
        targets, sources, near_sources, centre_sources, first_sum, target_rows,
        *packs[:REACH], *nodes[: REACH + 1],
    )
    return vel, near.reshape(seg)


def solution(mesh):
    in_specs = (
        P(None, "cells"),
        P(None, "cells"),
        P(None, "cells"),
        P("cells", "lanes"),
        P(None, "cells"),
        P(None, "cells"),
        P("cells"),
        P("cells"),
        P("cells"),
    )
    out_specs = (P(None, "cells"), P("cells"))
    return jax.shard_map(local, mesh=mesh, in_specs=in_specs, out_specs=out_specs, check_vma=False)
```

time: 39 us -> 38.1 us (0.977)
  waiting for transfers between devices: 16.6 us -> 10.9 us
  Pallas kernels: 8.44 us -> 12.6 us
  starting transfers between devices: 11.5 us -> 12.1 us
    ppermute x12, waiting for transfers between devices: 16.6 us -> 10.9 us  [shifted(): return lax.ppermute(block, ('cells', 'lanes'), route)]
    pallas_call x4 -> x6, Pallas kernels: 7.98 us -> 12.1 us  [the longest x1 3.46 us: local(): pl.pallas_call(first_forces, out_shape=jax.ShapeDtypeStruct(accumulator,...]
    ppermute x12, starting transfers between devices: 11.5 us -> 12.1 us  [shifted(): return lax.ppermute(block, ('cells', 'lanes'), route)]
  transfers between devices with their start and end apart: 12 -> 12, of which waited for: 9 -> 7; matrix products, arithmetic and copies ran while one was open for 0% -> 0% of each run, Pallas kernels for 1% -> 19%
where the time goes in v5:
time: 38.1 us; the launch traced here: 37.9 us
  Pallas kernels  12.6 us (33%)
  starting transfers between devices  12.1 us (32%)
  waiting for transfers between devices  10.9 us (29%)
  other arithmetic  0.82 us (2%)
  between operations  0.73 us (2%)
  local copies, waits for them, and re-layouts  0.67 us (2%)
    ppermute x12, starting transfers between devices, shifted(): return lax.ppermute(block, ('cells', 'lanes'), route)  12.1 us
    ppermute x12, waiting for transfers between devices, shifted(): return lax.ppermute(block, ('cells', 'lanes'), route)  10.9 us
    pallas_call x1, Pallas kernels, local(): pl.pallas_call(first_forces, out_shape=jax.ShapeDtypeStruct(accumulator,...  3.46 us
    pallas_call x1, Pallas kernels, local(): pl.pallas_call(functools.partial(last_forces, lanes, high_count), out_sha...  3.27 us
    pallas_call x1, Pallas kernels, local(): pl.pallas_call(functools.partial(first_near, high_count), out_shape=(jax....  3.15 us
    pallas_call x1, Pallas kernels, local(): pl.pallas_call(functools.partial(last_near, high_count), out_shape=jax.Sh...  2.21 us
    add x1, other arithmetic, local(): fields + rows_of([seg_nodes, node_owner], FIELDS, FIELDS + 4).astype(F32)  0.82 us
  transfers between devices with their start and end apart: 12, of which 7 were waited for; matrix products, arithmetic and copies ran while one was open for 0% of the time, Pallas kernels for 19%

profile of v5, /device:TPU:0, one launch (start us, length us, event | category | flops | bytes accessed | tf_op | source)
XLA Modules:
  0.0 37.9 jit_solution(14240767151684389944)
XLA Ops:
  0.6 0.8 %convert_add_fusion.fields = f32[13,1024]{1,0:T(8,128)S(1)} fusion(s32[2,1024]{1,0:T(2,128)} %param.14, s32[2,1024]{1,0:T(2,128)} %param.13, f32[3,1024]{1,0:T(4,128)} %param.10, f32[3,1024]{1,0:T(4,128)} %param.11, f32[3,1024]{1,0:T(4,128)} %param.9), kind=kLoop, calls=%fused_computation | loop fusion | flops 66560 | bytes 106496 | tf_op jit(solution)/shard_map/add | solution.py:377
  1.5 0.0 copy-start.1
  1.5 0.0 copy-start
  1.5 5.5 %collective-permute-start.2 = (f32[72,128]{1,0:T(8,128)S(1)}, f32[72,128]{1,0:T(8,128)S(1)}, u32[]{:S(2)}, u32[]{:S(2)}) collective-permute-start(f32[72,128]{1,0:T(8,128)S(1)} %get-tuple-element.17.own.refs_2_.refs_0_), channel_id=1, source_target_pairs={{2,0},{3,1},{4,2},{5,3},{6,4},{7,5},{8,6},{9,7},{10,8},{11,9},{12,... | collective-permute-start | bytes 110600 | tf_op jit(solution)/shard_map/ppermute | solution.py:42
  7.0 0.6 %collective-permute-start.3 = (f32[72,128]{1,0:T(8,128)S(1)}, f32[72,128]{1,0:T(8,128)S(1)}, u32[]{:S(2)}, u32[]{:S(2)}) collective-permute-start(f32[72,128]{1,0:T(8,128)S(1)} %get-tuple-element.17.own.refs_2_.refs_0_), channel_id=1, source_target_pairs={{4,0},{5,1},{6,2},{7,3},{8,4},{9,5},{10,6},{11,7},{12,8},{13,9},{1... | collective-permute-start | bytes 110600 | tf_op jit(solution)/shard_map/ppermute | solution.py:42
  7.7 1.4 %collective-permute-start = (f32[72,128]{1,0:T(8,128)S(1)}, f32[72,128]{1,0:T(8,128)S(1)}, u32[]{:S(2)}, u32[]{:S(2)}) collective-permute-start(f32[72,128]{1,0:T(8,128)S(1)} %get-tuple-element.17.own.refs_2_.refs_0_), channel_id=1, source_target_pairs={{28,0},{29,1},{30,2},{31,3},{0,4},{1,5},{2,6},{3,7},{4,8},{5,9},{6... | collective-permute-start | bytes 110600 | tf_op jit(solution)/shard_map/ppermute | solution.py:42
  9.1 0.0 collective-permute-start.1
  9.1 0.0 copy-start.2
  9.1 0.0 copy-start.3
  9.1 0.0 copy-done.1
  9.1 0.0 copy-done
  9.1 0.6 %copy-done.2 = s32[32]{0:T(128)S(1)} copy-done((s32[32]{0:T(128)S(1)}, s32[32]{0:T(128)}, u32[]{:S(2)}) %copy-start.2) | copy-done | bytes 152
  9.7 0.0 copy-done.3
  9.7 0.4 early.1
  10.1 0.0 collective-permute-done.2.refs_3_.refs_1_
  10.1 0.9 %collective-permute-done.3.refs_4_.refs_2_ = f32[72,128]{1,0:T(8,128)S(1)} collective-permute-done((f32[72,128]{1,0:T(8,128)S(1)}, f32[72,128]{1,0:T(8,128)S(1)}, u32[]{:S(2)}, u32[]{:S(2)}) %collective-permute-start.3) | collective-permute-done | bytes 36896 | tf_op jit(solution)/shard_map/ppermute | solution.py:42
  11.0 3.5 %first_forces.1.first_acc = f32[9,128,32]{2,1,0:T(8,128)S(1)} custom-call(s32[8,8]{1,0:T(8,128)S(1)} %get-tuple-element.24.lists, f32[8,128,48]{2,1,0:T(8,128)S(1)} %get-tuple-element.25.lhs, f32[72,128]{1,0:T(8,128)S(1)} %get-tuple-element.17.own.refs_2_.refs_0_, f32[72,128]{1,0:T(8,128)S(1)} %collective-permute-done.2.refs_3_.refs_1_, ...), custom_call_target="tpu_custom_call" | custom-call | flops 268435456 | bytes 8388608 | tf_op jit(solution)/shard_map/first_forces/pallas_call | solution.py:420
  14.5 0.0 collective-permute-done.refs_0_
  14.5 0.7 %collective-permute-done.1.refs_1_ = f32[72,128]{1,0:T(8,128)S(1)} collective-permute-done((f32[72,128]{1,0:T(8,128)S(1)}, f32[72,128]{1,0:T(8,128)S(1)}, u32[]{:S(2)}, u32[]{:S(2)}) %collective-permute-start.1) | collective-permute-done | bytes 36896 | tf_op jit(solution)/shard_map/ppermute | solution.py:42
  15.1 3.3 %last_forces.1 = (f32[4,8,128]{2,1,0:T(8,128)S(1)}, f32[4,8,128]{2,1,0:T(8,128)S(1)}) custom-call(s32[8,8]{1,0:T(8,128)S(1)} %get-tuple-element.24.lists, f32[8,128,48]{2,1,0:T(8,128)S(1)} %get-tuple-element.25.lhs, bf16[2,128,1024]{2,1,0:T(8,128)(2,1)S(1)} %get-tuple-element.26.onehots, f32[4,8,128]{2,1,0:T(8,128)S(1)} %get-tuple-element.18.numbers, ...), custom_call_target="tpu_custom_call" | custom-call | tf_op jit(solution)/shard_map/last_forces/pallas_call | solution.py:431
  18.4 1.6 %collective-permute-start.4 = (f32[4,8,128]{2,1,0:T(8,128)S(1)}, f32[4,8,128]{2,1,0:T(8,128)S(1)}, u32[]{:S(2)}, u32[]{:S(2)}) collective-permute-start(f32[4,8,128]{2,1,0:T(8,128)S(1)} %get-tuple-element.27.refs_0_), channel_id=1, source_target_pairs={{1,0},{0,1},{3,2},{2,3},{5,4},{4,5},{7,6},{6,7},{9,8},{8,9},{11,10... | collective-permute-start | bytes 49160 | tf_op jit(solution)/shard_map/ppermute | solution.py:42
  20.0 0.0 collective-permute-start.5
  20.0 0.0 collective-permute-start.6
  20.0 2.2 %collective-permute-done.4.refs_1_ = f32[4,8,128]{2,1,0:T(8,128)S(1)} collective-permute-done((f32[4,8,128]{2,1,0:T(8,128)S(1)}, f32[4,8,128]{2,1,0:T(8,128)S(1)}, u32[]{:S(2)}, u32[]{:S(2)}) %collective-permute-start.4) | collective-permute-done | bytes 16416 | tf_op jit(solution)/shard_map/ppermute | solution.py:42
  22.2 3.7 %collective-permute-done.5.refs_2_ = f32[4,8,128]{2,1,0:T(8,128)S(1)} collective-permute-done((f32[4,8,128]{2,1,0:T(8,128)S(1)}, f32[4,8,128]{2,1,0:T(8,128)S(1)}, u32[]{:S(2)}, u32[]{:S(2)}) %collective-permute-start.5) | collective-permute-done | bytes 16416 | tf_op jit(solution)/shard_map/ppermute | solution.py:42
  25.9 0.8 %collective-permute-done.6.refs_3_ = f32[4,8,128]{2,1,0:T(8,128)S(1)} collective-permute-done((f32[4,8,128]{2,1,0:T(8,128)S(1)}, f32[4,8,128]{2,1,0:T(8,128)S(1)}, u32[]{:S(2)}, u32[]{:S(2)}) %collective-permute-start.6) | collective-permute-done | bytes 16416 | tf_op jit(solution)/shard_map/ppermute | solution.py:42
  26.7 0.9 %collective-permute-start.7 = (f32[7,8,128]{2,1,0:T(8,128)S(1)}, f32[7,8,128]{2,1,0:T(8,128)S(1)}, u32[]{:S(2)}, u32[]{:S(2)}) collective-permute-start(f32[7,8,128]{2,1,0:T(8,128)S(1)} %velocity.1.refs_3_.refs_4_), channel_id=1, source_target_pairs={{2,0},{3,1},{4,2},{5,3},{6,4},{7,5},{8,6},{9,7},{10,8},{11,9},{12,... | collective-permute-start | bytes 86024 | tf_op jit(solution)/shard_map/ppermute | solution.py:42
  27.6 0.2 collective-permute-start.8
  27.9 0.0 collective-permute-start.9
  27.9 1.8 %collective-permute-start.10 = (f32[7,8,128]{2,1,0:T(8,128)S(1)}, f32[7,8,128]{2,1,0:T(8,128)S(1)}, u32[]{:S(2)}, u32[]{:S(2)}) collective-permute-start(f32[7,8,128]{2,1,0:T(8,128)S(1)} %velocity.1.refs_3_.refs_4_), channel_id=1, source_target_pairs={{28,0},{29,1},{30,2},{31,3},{0,4},{1,5},{2,6},{3,7},{4,8},{5,9},{6... | collective-permute-start | bytes 86024 | tf_op jit(solution)/shard_map/ppermute | solution.py:42
  29.7 0.1 collective-permute-start.11
  29.7 0.2 select.6
  29.9 0.0 collective-permute-done.7.refs_4_
  29.9 1.6 %collective-permute-done.8.refs_5_ = f32[7,8,128]{2,1,0:T(8,128)S(1)} collective-permute-done((f32[7,8,128]{2,1,0:T(8,128)S(1)}, f32[7,8,128]{2,1,0:T(8,128)S(1)}, u32[]{:S(2)}, u32[]{:S(2)}) %collective-permute-start.8) | collective-permute-done | bytes 28704 | tf_op jit(solution)/shard_map/ppermute | solution.py:42
  31.5 0.0 collective-permute-done.9.refs_6_
  31.5 3.2 %first_near.1 = (f32[9,128,128]{2,1,0:T(8,128)S(1)}, f32[8,128,96]{2,1,0:T(8,128)S(1)}, f32[3,1024]{1,0:T(4,128)}) custom-call(s32[1,32]{1,0:T(1,128)S(1)} %get-tuple-element.19.targets, s32[1,32]{1,0:T(1,128)S(1)} %get-tuple-element.20.sources, bf16[40,48,128]{2,1,0:T(8,128)(2,1)S(1)} %get-tuple-element.21.near_s, ...), custom_call_target="tpu_custom_call" | custom-call | flops 268435456 | bytes 8388608 | tf_op jit(solution)/shard_map/first_near/pallas_call | solution.py:478
  34.7 0.0 collective-permute-done.10.refs_2_
  34.7 1.0 %collective-permute-done.11.refs_3_ = f32[7,8,128]{2,1,0:T(8,128)S(1)} collective-permute-done((f32[7,8,128]{2,1,0:T(8,128)S(1)}, f32[7,8,128]{2,1,0:T(8,128)S(1)}, u32[]{:S(2)}, u32[]{:S(2)}) %collective-permute-start.11) | collective-permute-done | bytes 28704 | tf_op jit(solution)/shard_map/ppermute | solution.py:42
  35.7 2.2 %last_near.1 = f32[8,128]{1,0:T(8,128)} custom-call(s32[1,32]{1,0:T(1,128)S(1)} %get-tuple-element.19.targets, s32[1,32]{1,0:T(1,128)S(1)} %get-tuple-element.20.sources, bf16[40,48,128]{2,1,0:T(8,128)(2,1)S(1)} %get-tuple-element.21.near_s, f32[40,24,128]{2,1,0:T(8,128)S(1)} %get-tuple-element.22.centre_s, f32[9,128,128]{2,1,0:T(8,128)S(1)} %get-tuple-element.30.first_acc, ...), custom_call_target="tpu_custom_call" | custom-call | tf_op jit(solution)/shard_map/last_near/pallas_call | solution.py:492
  (2 shorter events, 0.0 us)
Async XLA Ops:
  1.5 7.6 %copy-start.1 = (f32[1024]{0:T(1024)S(1)}, f32[1024]{0:T(1024)}, u32[]{:S(2)}) copy-start(f32[1024]{0:T(1024)} %param.15) | copy-start | bytes 12292
  1.5 7.6 %copy-start = (s32[8,8]{1,0:T(8,128)S(1)}, s32[8,8]{1,0:T(8,128)}, u32[]{:S(2)}) copy-start(s32[8,8]{1,0:T(8,128)} %refs_0_.1) | copy-start | bytes 772
  1.5 8.6 %collective-permute-start.2 = (f32[72,128]{1,0:T(8,128)S(1)}, f32[72,128]{1,0:T(8,128)S(1)}, u32[]{:S(2)}, u32[]{:S(2)}) collective-permute-start(f32[72,128]{1,0:T(8,128)S(1)} %get-tuple-element.17.own.refs_2_.refs_0_), channel_id=1, source_target_pairs={{2,0},{3,1},{4,2},{5,3},{6,4},{7,5},{8,6},{9,7},{10,8},{11,9},{12,... | collective-permute-start | bytes 110600 | tf_op jit(solution)/shard_map/ppermute | solution.py:42
  7.0 4.0 %collective-permute-start.3 = (f32[72,128]{1,0:T(8,128)S(1)}, f32[72,128]{1,0:T(8,128)S(1)}, u32[]{:S(2)}, u32[]{:S(2)}) collective-permute-start(f32[72,128]{1,0:T(8,128)S(1)} %get-tuple-element.17.own.refs_2_.refs_0_), channel_id=1, source_target_pairs={{4,0},{5,1},{6,2},{7,3},{8,4},{9,5},{10,6},{11,7},{12,8},{13,9},{1... | collective-permute-start | bytes 110600 | tf_op jit(solution)/shard_map/ppermute | solution.py:42
  7.7 6.8 %collective-permute-start = (f32[72,128]{1,0:T(8,128)S(1)}, f32[72,128]{1,0:T(8,128)S(1)}, u32[]{:S(2)}, u32[]{:S(2)}) collective-permute-start(f32[72,128]{1,0:T(8,128)S(1)} %get-tuple-element.17.own.refs_2_.refs_0_), channel_id=1, source_target_pairs={{28,0},{29,1},{30,2},{31,3},{0,4},{1,5},{2,6},{3,7},{4,8},{5,9},{6... | collective-permute-start | bytes 110600 | tf_op jit(solution)/shard_map/ppermute | solution.py:42
  9.1 6.1 %collective-permute-start.1 = (f32[72,128]{1,0:T(8,128)S(1)}, f32[72,128]{1,0:T(8,128)S(1)}, u32[]{:S(2)}, u32[]{:S(2)}) collective-permute-start(f32[72,128]{1,0:T(8,128)S(1)} %get-tuple-element.17.own.refs_2_.refs_0_), channel_id=1, source_target_pairs={{30,0},{31,1},{0,2},{1,3},{2,4},{3,5},{4,6},{5,7},{6,8},{7,9},{8,1... | collective-permute-start | bytes 110600 | tf_op jit(solution)/shard_map/ppermute | solution.py:42
  9.1 0.7 %copy-start.2 = (s32[32]{0:T(128)S(1)}, s32[32]{0:T(128)}, u32[]{:S(2)}) copy-start(s32[32]{0:T(128)} %param.16) | copy-start | bytes 388
  9.1 0.7 %copy-start.3 = (s32[32]{0:T(128)S(1)}, s32[32]{0:T(128)}, u32[]{:S(2)}) copy-start(s32[32]{0:T(128)} %param.17) | copy-start | bytes 388
  18.4 3.8 %collective-permute-start.4 = (f32[4,8,128]{2,1,0:T(8,128)S(1)}, f32[4,8,128]{2,1,0:T(8,128)S(1)}, u32[]{:S(2)}, u32[]{:S(2)}) collective-permute-start(f32[4,8,128]{2,1,0:T(8,128)S(1)} %get-tuple-element.27.refs_0_), channel_id=1, source_target_pairs={{1,0},{0,1},{3,2},{2,3},{5,4},{4,5},{7,6},{6,7},{9,8},{8,9},{11,10... | collective-permute-start | bytes 49160 | tf_op jit(solution)/shard_map/ppermute | solution.py:42
  20.0 6.0 %collective-permute-start.5 = (f32[4,8,128]{2,1,0:T(8,128)S(1)}, f32[4,8,128]{2,1,0:T(8,128)S(1)}, u32[]{:S(2)}, u32[]{:S(2)}) collective-permute-start(f32[4,8,128]{2,1,0:T(8,128)S(1)} %get-tuple-element.28), channel_id=1, source_target_pairs={{30,0},{31,1},{0,2},{1,3},{2,4},{3,5},{4,6},{5,7},{6,8},{7,9},{8,1... | collective-permute-start | bytes 49160 | tf_op jit(solution)/shard_map/ppermute | solution.py:42
  20.0 6.8 %collective-permute-start.6 = (f32[4,8,128]{2,1,0:T(8,128)S(1)}, f32[4,8,128]{2,1,0:T(8,128)S(1)}, u32[]{:S(2)}, u32[]{:S(2)}) collective-permute-start(f32[4,8,128]{2,1,0:T(8,128)S(1)} %get-tuple-element.28), channel_id=1, source_target_pairs={{31,0},{30,1},{1,2},{0,3},{3,4},{2,5},{5,6},{4,7},{7,8},{6,9},{9,1... | collective-permute-start | bytes 49160 | tf_op jit(solution)/shard_map/ppermute | solution.py:42
  26.7 3.1 %collective-permute-start.7 = (f32[7,8,128]{2,1,0:T(8,128)S(1)}, f32[7,8,128]{2,1,0:T(8,128)S(1)}, u32[]{:S(2)}, u32[]{:S(2)}) collective-permute-start(f32[7,8,128]{2,1,0:T(8,128)S(1)} %velocity.1.refs_3_.refs_4_), channel_id=1, source_target_pairs={{2,0},{3,1},{4,2},{5,3},{6,4},{7,5},{8,6},{9,7},{10,8},{11,9},{12,... | collective-permute-start | bytes 86024 | tf_op jit(solution)/shard_map/ppermute | solution.py:42
  27.6 3.9 %collective-permute-start.8 = (f32[7,8,128]{2,1,0:T(8,128)S(1)}, f32[7,8,128]{2,1,0:T(8,128)S(1)}, u32[]{:S(2)}, u32[]{:S(2)}) collective-permute-start(f32[7,8,128]{2,1,0:T(8,128)S(1)} %velocity.1.refs_3_.refs_4_), channel_id=1, source_target_pairs={{4,0},{5,1},{6,2},{7,3},{8,4},{9,5},{10,6},{11,7},{12,8},{13,9},{1... | collective-permute-start | bytes 86024 | tf_op jit(solution)/shard_map/ppermute | solution.py:42
  27.9 3.7 %collective-permute-start.9 = (f32[7,8,128]{2,1,0:T(8,128)S(1)}, f32[7,8,128]{2,1,0:T(8,128)S(1)}, u32[]{:S(2)}, u32[]{:S(2)}) collective-permute-start(f32[7,8,128]{2,1,0:T(8,128)S(1)} %velocity.1.refs_3_.refs_4_), channel_id=1, source_target_pairs={{6,0},{7,1},{8,2},{9,3},{10,4},{11,5},{12,6},{13,7},{14,8},{15,9},... | collective-permute-start | bytes 86024 | tf_op jit(solution)/shard_map/ppermute | solution.py:42
  27.9 6.8 %collective-permute-start.10 = (f32[7,8,128]{2,1,0:T(8,128)S(1)}, f32[7,8,128]{2,1,0:T(8,128)S(1)}, u32[]{:S(2)}, u32[]{:S(2)}) collective-permute-start(f32[7,8,128]{2,1,0:T(8,128)S(1)} %velocity.1.refs_3_.refs_4_), channel_id=1, source_target_pairs={{28,0},{29,1},{30,2},{31,3},{0,4},{1,5},{2,6},{3,7},{4,8},{5,9},{6... | collective-permute-start | bytes 86024 | tf_op jit(solution)/shard_map/ppermute | solution.py:42
  29.7 6.0 %collective-permute-start.11 = (f32[7,8,128]{2,1,0:T(8,128)S(1)}, f32[7,8,128]{2,1,0:T(8,128)S(1)}, u32[]{:S(2)}, u32[]{:S(2)}) collective-permute-start(f32[7,8,128]{2,1,0:T(8,128)S(1)} %velocity.1.refs_3_.refs_4_), channel_id=1, source_target_pairs={{30,0},{31,1},{0,2},{1,3},{2,4},{3,5},{4,6},{5,7},{6,8},{7,9},{8,1... | collective-permute-start | bytes 86024 | tf_op jit(solution)/shard_map/ppermute | solution.py:42

commit v6 on v5

--- a/solution.py
+++ b/solution.py
@@ -8,9 +8,10 @@
 from jax.experimental.pallas import tpu as pltpu
 from jax.sharding import PartitionSpec as P
 
+
 BLK = 128
 FIELDS = 9
-GROUP = 8
+GROUP = 16
 REACH = 2
 FORCE_SCALE = 0.02
 CORE_SQUARE = 0.25
@@ -32,7 +33,8 @@
     return pltpu.CompilerParams(vmem_limit_bytes=mib << 20)
 
 
-def shifted(block, cell_step, lane_step):
+def shifted(block, *steps):
+    cell_step, lane_step = (*steps, 0)[:2]
     cells, lanes = lax.axis_size("cells"), lax.axis_size("lanes")
     route = []
     for c in range(cells):
@@ -386,7 +388,7 @@
         compiler_params=params(4),
         name="pack",
     )(fields)
-    packs = [own if o == 0 else shifted(own, o, 0) for o in range(-REACH, REACH + 1)]
+    packs = [own if o == 0 else shifted(own, o) for o in range(-REACH, REACH + 1)]
     small = [
         neighbour_blocks,
         mobility.reshape(high_count, BLK),
@@ -450,9 +452,7 @@
         compiler_params=params(4),
         name="velocity",
     )(rate, numbers, *terms)
-    nodes = [
-        velocity if o == 0 else shifted(velocity, o, 0) for o in range(-REACH, REACH + 2)
-    ]
+    nodes = [velocity if o == 0 else shifted(velocity, o) for o in range(-REACH, REACH + 2)]
     near_sources, centre_sources = pl.pallas_call(
         select_kernel,
         out_shape=(
@@ -517,4 +517,5 @@
         P("cells"),
     )
     out_specs = (P(None, "cells"), P("cells"))
+
     return jax.shard_map(local, mesh=mesh, in_specs=in_specs, out_specs=out_specs, check_vma=False)

time: 38.1 us -> 37.9 us (level)
    pallas_call x1, Pallas kernels: 3.27 us -> 2.77 us  [local(): pl.pallas_call(functools.partial(last_forces, lanes, high_count), out_sha...]
  transfers between devices with their start and end apart: 12 -> 12, of which waited for: 7 -> 8; matrix products, arithmetic and copies ran while one was open for 0% -> 0% of each run, Pallas kernels for 19% -> 19%
where the time goes in v6:
time: 37.9 us; the launch traced here: 37.6 us
  Pallas kernels  12.3 us (32%)
  starting transfers between devices  12.1 us (32%)
  waiting for transfers between devices  11 us (29%)
  other arithmetic  0.82 us (2%)
  between operations  0.72 us (2%)
  local copies, waits for them, and re-layouts  0.67 us (2%)
    ppermute x12, starting transfers between devices, shifted(): return lax.ppermute(block, ('cells', 'lanes'), route)  12.1 us
    ppermute x12, waiting for transfers between devices, shifted(): return lax.ppermute(block, ('cells', 'lanes'), route)  11 us
    pallas_call x1, Pallas kernels, local(): pl.pallas_call(functools.partial(first_near, high_count), out_shape=(jax....  3.3 us
    pallas_call x1, Pallas kernels, local(): pl.pallas_call(first_forces, out_shape=jax.ShapeDtypeStruct(accumulator,...  3.23 us
    pallas_call x1, Pallas kernels, local(): pl.pallas_call(functools.partial(last_forces, lanes, high_count), out_sha...  2.77 us
    pallas_call x1, Pallas kernels, local(): pl.pallas_call(functools.partial(last_near, high_count), out_shape=jax.Sh...  2.47 us
    add x1, other arithmetic, local(): fields + rows_of([seg_nodes, node_owner], FIELDS, FIELDS + 4).astype(F32)  0.82 us
  transfers between devices with their start and end apart: 12, of which 8 were waited for; matrix products, arithmetic and copies ran while one was open for 0% of the time, Pallas kernels for 19%

profile of v6, /device:TPU:0, one launch (start us, length us, event | category | flops | bytes accessed | tf_op | source)
XLA Modules:
  0.0 37.6 jit_solution(9762698736428095089)
XLA Ops:
  0.6 0.8 %convert_add_fusion.fields = f32[13,1024]{1,0:T(8,128)S(1)} fusion(s32[2,1024]{1,0:T(2,128)} %param.14, s32[2,1024]{1,0:T(2,128)} %param.13, f32[3,1024]{1,0:T(4,128)} %param.10, f32[3,1024]{1,0:T(4,128)} %param.11, f32[3,1024]{1,0:T(4,128)} %param.9), kind=kLoop, calls=%fused_computation | loop fusion | flops 66560 | bytes 106496 | tf_op jit(solution)/shard_map/add | solution.py:379
  1.5 0.0 copy-start.1
  1.5 0.0 copy-start
  1.5 5.5 %collective-permute-start.2 = (f32[72,128]{1,0:T(8,128)S(1)}, f32[72,128]{1,0:T(8,128)S(1)}, u32[]{:S(2)}, u32[]{:S(2)}) collective-permute-start(f32[72,128]{1,0:T(8,128)S(1)} %get-tuple-element.17.own.refs_2_.refs_0_), channel_id=1, source_target_pairs={{2,0},{3,1},{4,2},{5,3},{6,4},{7,5},{8,6},{9,7},{10,8},{11,9},{12,... | collective-permute-start | bytes 110600 | tf_op jit(solution)/shard_map/ppermute | solution.py:44
  7.0 0.6 %collective-permute-start.3 = (f32[72,128]{1,0:T(8,128)S(1)}, f32[72,128]{1,0:T(8,128)S(1)}, u32[]{:S(2)}, u32[]{:S(2)}) collective-permute-start(f32[72,128]{1,0:T(8,128)S(1)} %get-tuple-element.17.own.refs_2_.refs_0_), channel_id=1, source_target_pairs={{4,0},{5,1},{6,2},{7,3},{8,4},{9,5},{10,6},{11,7},{12,8},{13,9},{1... | collective-permute-start | bytes 110600 | tf_op jit(solution)/shard_map/ppermute | solution.py:44
  7.7 1.4 %collective-permute-start = (f32[72,128]{1,0:T(8,128)S(1)}, f32[72,128]{1,0:T(8,128)S(1)}, u32[]{:S(2)}, u32[]{:S(2)}) collective-permute-start(f32[72,128]{1,0:T(8,128)S(1)} %get-tuple-element.17.own.refs_2_.refs_0_), channel_id=1, source_target_pairs={{28,0},{29,1},{30,2},{31,3},{0,4},{1,5},{2,6},{3,7},{4,8},{5,9},{6... | collective-permute-start | bytes 110600 | tf_op jit(solution)/shard_map/ppermute | solution.py:44
  9.1 0.0 collective-permute-start.1
  9.1 0.0 copy-start.2
  9.1 0.0 copy-start.3
  9.1 0.0 copy-done.1
  9.1 0.0 copy-done
  9.1 0.6 %copy-done.2 = s32[32]{0:T(128)S(1)} copy-done((s32[32]{0:T(128)S(1)}, s32[32]{0:T(128)}, u32[]{:S(2)}) %copy-start.2) | copy-done | bytes 152
  9.7 0.0 copy-done.3
  9.7 0.4 early.1
  10.1 0.0 collective-permute-done.2.refs_3_.refs_1_
  10.1 0.9 %collective-permute-done.3.refs_4_.refs_2_ = f32[72,128]{1,0:T(8,128)S(1)} collective-permute-done((f32[72,128]{1,0:T(8,128)S(1)}, f32[72,128]{1,0:T(8,128)S(1)}, u32[]{:S(2)}, u32[]{:S(2)}) %collective-permute-start.3) | collective-permute-done | bytes 36896 | tf_op jit(solution)/shard_map/ppermute | solution.py:44
  11.0 3.2 %first_forces.1.first_acc = f32[9,128,32]{2,1,0:T(8,128)S(1)} custom-call(s32[8,8]{1,0:T(8,128)S(1)} %get-tuple-element.24.lists, f32[8,128,48]{2,1,0:T(8,128)S(1)} %get-tuple-element.25.lhs, f32[72,128]{1,0:T(8,128)S(1)} %get-tuple-element.17.own.refs_2_.refs_0_, f32[72,128]{1,0:T(8,128)S(1)} %collective-permute-done.2.refs_3_.refs_1_, ...), custom_call_target="tpu_custom_call" | custom-call | flops 268435456 | bytes 8388608 | tf_op jit(solution)/shard_map/first_forces/pallas_call | solution.py:422
  14.2 0.1 collective-permute-done.refs_0_
  14.3 0.8 %collective-permute-done.1.refs_1_ = f32[72,128]{1,0:T(8,128)S(1)} collective-permute-done((f32[72,128]{1,0:T(8,128)S(1)}, f32[72,128]{1,0:T(8,128)S(1)}, u32[]{:S(2)}, u32[]{:S(2)}) %collective-permute-start.1) | collective-permute-done | bytes 36896 | tf_op jit(solution)/shard_map/ppermute | solution.py:44
  15.1 2.8 %last_forces.1 = (f32[4,8,128]{2,1,0:T(8,128)S(1)}, f32[4,8,128]{2,1,0:T(8,128)S(1)}) custom-call(s32[8,8]{1,0:T(8,128)S(1)} %get-tuple-element.24.lists, f32[8,128,48]{2,1,0:T(8,128)S(1)} %get-tuple-element.25.lhs, bf16[2,128,1024]{2,1,0:T(8,128)(2,1)S(1)} %get-tuple-element.26.onehots, f32[4,8,128]{2,1,0:T(8,128)S(1)} %get-tuple-element.18.numbers, ...), custom_call_target="tpu_custom_call" | custom-call | tf_op jit(solution)/shard_map/last_forces/pallas_call | solution.py:433
  17.9 1.6 %collective-permute-start.4 = (f32[4,8,128]{2,1,0:T(8,128)S(1)}, f32[4,8,128]{2,1,0:T(8,128)S(1)}, u32[]{:S(2)}, u32[]{:S(2)}) collective-permute-start(f32[4,8,128]{2,1,0:T(8,128)S(1)} %get-tuple-element.27.refs_0_), channel_id=1, source_target_pairs={{1,0},{0,1},{3,2},{2,3},{5,4},{4,5},{7,6},{6,7},{9,8},{8,9},{11,10... | collective-permute-start | bytes 49160 | tf_op jit(solution)/shard_map/ppermute | solution.py:44
  19.5 0.0 collective-permute-start.5
  19.5 0.0 collective-permute-start.6
  19.5 2.2 %collective-permute-done.4.refs_1_ = f32[4,8,128]{2,1,0:T(8,128)S(1)} collective-permute-done((f32[4,8,128]{2,1,0:T(8,128)S(1)}, f32[4,8,128]{2,1,0:T(8,128)S(1)}, u32[]{:S(2)}, u32[]{:S(2)}) %collective-permute-start.4) | collective-permute-done | bytes 16416 | tf_op jit(solution)/shard_map/ppermute | solution.py:44
  21.7 3.7 %collective-permute-done.5.refs_2_ = f32[4,8,128]{2,1,0:T(8,128)S(1)} collective-permute-done((f32[4,8,128]{2,1,0:T(8,128)S(1)}, f32[4,8,128]{2,1,0:T(8,128)S(1)}, u32[]{:S(2)}, u32[]{:S(2)}) %collective-permute-start.5) | collective-permute-done | bytes 16416 | tf_op jit(solution)/shard_map/ppermute | solution.py:44
  25.4 0.8 %collective-permute-done.6.refs_3_ = f32[4,8,128]{2,1,0:T(8,128)S(1)} collective-permute-done((f32[4,8,128]{2,1,0:T(8,128)S(1)}, f32[4,8,128]{2,1,0:T(8,128)S(1)}, u32[]{:S(2)}, u32[]{:S(2)}) %collective-permute-start.6) | collective-permute-done | bytes 16416 | tf_op jit(solution)/shard_map/ppermute | solution.py:44
  26.2 0.9 %collective-permute-start.7 = (f32[7,8,128]{2,1,0:T(8,128)S(1)}, f32[7,8,128]{2,1,0:T(8,128)S(1)}, u32[]{:S(2)}, u32[]{:S(2)}) collective-permute-start(f32[7,8,128]{2,1,0:T(8,128)S(1)} %velocity.1.refs_3_.refs_4_), channel_id=1, source_target_pairs={{2,0},{3,1},{4,2},{5,3},{6,4},{7,5},{8,6},{9,7},{10,8},{11,9},{12,... | collective-permute-start | bytes 86024 | tf_op jit(solution)/shard_map/ppermute | solution.py:44
  27.1 0.2 collective-permute-start.8
  27.3 0.0 collective-permute-start.9
  27.3 1.8 %collective-permute-start.10 = (f32[7,8,128]{2,1,0:T(8,128)S(1)}, f32[7,8,128]{2,1,0:T(8,128)S(1)}, u32[]{:S(2)}, u32[]{:S(2)}) collective-permute-start(f32[7,8,128]{2,1,0:T(8,128)S(1)} %velocity.1.refs_3_.refs_4_), channel_id=1, source_target_pairs={{28,0},{29,1},{30,2},{31,3},{0,4},{1,5},{2,6},{3,7},{4,8},{5,9},{6... | collective-permute-start | bytes 86024 | tf_op jit(solution)/shard_map/ppermute | solution.py:44
  29.2 0.0 collective-permute-start.11
  29.2 0.2 select.6
  29.4 0.0 collective-permute-done.7.refs_4_
  29.4 1.6 %collective-permute-done.8.refs_5_ = f32[7,8,128]{2,1,0:T(8,128)S(1)} collective-permute-done((f32[7,8,128]{2,1,0:T(8,128)S(1)}, f32[7,8,128]{2,1,0:T(8,128)S(1)}, u32[]{:S(2)}, u32[]{:S(2)}) %collective-permute-start.8) | collective-permute-done | bytes 28704 | tf_op jit(solution)/shard_map/ppermute | solution.py:44
  31.0 0.0 collective-permute-done.9.refs_6_
  31.0 3.3 %first_near.1 = (f32[9,128,128]{2,1,0:T(8,128)S(1)}, f32[8,128,96]{2,1,0:T(8,128)S(1)}, f32[3,1024]{1,0:T(4,128)}) custom-call(s32[1,32]{1,0:T(1,128)S(1)} %get-tuple-element.19.targets, s32[1,32]{1,0:T(1,128)S(1)} %get-tuple-element.20.sources, bf16[40,48,128]{2,1,0:T(8,128)(2,1)S(1)} %get-tuple-element.21.near_s, ...), custom_call_target="tpu_custom_call" | custom-call | flops 268435456 | bytes 8388608 | tf_op jit(solution)/shard_map/first_near/pallas_call | solution.py:478
  34.3 0.0 collective-permute-done.10.refs_2_
  34.3 0.8 %collective-permute-done.11.refs_3_ = f32[7,8,128]{2,1,0:T(8,128)S(1)} collective-permute-done((f32[7,8,128]{2,1,0:T(8,128)S(1)}, f32[7,8,128]{2,1,0:T(8,128)S(1)}, u32[]{:S(2)}, u32[]{:S(2)}) %collective-permute-start.11) | collective-permute-done | bytes 28704 | tf_op jit(solution)/shard_map/ppermute | solution.py:44
  35.2 2.5 %last_near.1 = f32[8,128]{1,0:T(8,128)} custom-call(s32[1,32]{1,0:T(1,128)S(1)} %get-tuple-element.19.targets, s32[1,32]{1,0:T(1,128)S(1)} %get-tuple-element.20.sources, bf16[40,48,128]{2,1,0:T(8,128)(2,1)S(1)} %get-tuple-element.21.near_s, f32[40,24,128]{2,1,0:T(8,128)S(1)} %get-tuple-element.22.centre_s, f32[9,128,128]{2,1,0:T(8,128)S(1)} %get-tuple-element.30.first_acc, ...), custom_call_target="tpu_custom_call" | custom-call | tf_op jit(solution)/shard_map/last_near/pallas_call | solution.py:492
  (2 shorter events, 0.0 us)
Async XLA Ops:
  1.5 7.6 %copy-start.1 = (f32[1024]{0:T(1024)S(1)}, f32[1024]{0:T(1024)}, u32[]{:S(2)}) copy-start(f32[1024]{0:T(1024)} %param.15) | copy-start | bytes 12292
  1.5 7.6 %copy-start = (s32[8,8]{1,0:T(8,128)S(1)}, s32[8,8]{1,0:T(8,128)}, u32[]{:S(2)}) copy-start(s32[8,8]{1,0:T(8,128)} %refs_0_.1) | copy-start | bytes 772
  1.5 8.6 %collective-permute-start.2 = (f32[72,128]{1,0:T(8,128)S(1)}, f32[72,128]{1,0:T(8,128)S(1)}, u32[]{:S(2)}, u32[]{:S(2)}) collective-permute-start(f32[72,128]{1,0:T(8,128)S(1)} %get-tuple-element.17.own.refs_2_.refs_0_), channel_id=1, source_target_pairs={{2,0},{3,1},{4,2},{5,3},{6,4},{7,5},{8,6},{9,7},{10,8},{11,9},{12,... | collective-permute-start | bytes 110600 | tf_op jit(solution)/shard_map/ppermute | solution.py:44
  7.0 4.0 %collective-permute-start.3 = (f32[72,128]{1,0:T(8,128)S(1)}, f32[72,128]{1,0:T(8,128)S(1)}, u32[]{:S(2)}, u32[]{:S(2)}) collective-permute-start(f32[72,128]{1,0:T(8,128)S(1)} %get-tuple-element.17.own.refs_2_.refs_0_), channel_id=1, source_target_pairs={{4,0},{5,1},{6,2},{7,3},{8,4},{9,5},{10,6},{11,7},{12,8},{13,9},{1... | collective-permute-start | bytes 110600 | tf_op jit(solution)/shard_map/ppermute | solution.py:44
  7.7 6.7 %collective-permute-start = (f32[72,128]{1,0:T(8,128)S(1)}, f32[72,128]{1,0:T(8,128)S(1)}, u32[]{:S(2)}, u32[]{:S(2)}) collective-permute-start(f32[72,128]{1,0:T(8,128)S(1)} %get-tuple-element.17.own.refs_2_.refs_0_), channel_id=1, source_target_pairs={{28,0},{29,1},{30,2},{31,3},{0,4},{1,5},{2,6},{3,7},{4,8},{5,9},{6... | collective-permute-start | bytes 110600 | tf_op jit(solution)/shard_map/ppermute | solution.py:44
  9.1 6.1 %collective-permute-start.1 = (f32[72,128]{1,0:T(8,128)S(1)}, f32[72,128]{1,0:T(8,128)S(1)}, u32[]{:S(2)}, u32[]{:S(2)}) collective-permute-start(f32[72,128]{1,0:T(8,128)S(1)} %get-tuple-element.17.own.refs_2_.refs_0_), channel_id=1, source_target_pairs={{30,0},{31,1},{0,2},{1,3},{2,4},{3,5},{4,6},{5,7},{6,8},{7,9},{8,1... | collective-permute-start | bytes 110600 | tf_op jit(solution)/shard_map/ppermute | solution.py:44
  9.1 0.7 %copy-start.2 = (s32[32]{0:T(128)S(1)}, s32[32]{0:T(128)}, u32[]{:S(2)}) copy-start(s32[32]{0:T(128)} %param.16) | copy-start | bytes 388
  9.1 0.7 %copy-start.3 = (s32[32]{0:T(128)S(1)}, s32[32]{0:T(128)}, u32[]{:S(2)}) copy-start(s32[32]{0:T(128)} %param.17) | copy-start | bytes 388
  17.9 3.8 %collective-permute-start.4 = (f32[4,8,128]{2,1,0:T(8,128)S(1)}, f32[4,8,128]{2,1,0:T(8,128)S(1)}, u32[]{:S(2)}, u32[]{:S(2)}) collective-permute-start(f32[4,8,128]{2,1,0:T(8,128)S(1)} %get-tuple-element.27.refs_0_), channel_id=1, source_target_pairs={{1,0},{0,1},{3,2},{2,3},{5,4},{4,5},{7,6},{6,7},{9,8},{8,9},{11,10... | collective-permute-start | bytes 49160 | tf_op jit(solution)/shard_map/ppermute | solution.py:44
  19.5 6.0 %collective-permute-start.5 = (f32[4,8,128]{2,1,0:T(8,128)S(1)}, f32[4,8,128]{2,1,0:T(8,128)S(1)}, u32[]{:S(2)}, u32[]{:S(2)}) collective-permute-start(f32[4,8,128]{2,1,0:T(8,128)S(1)} %get-tuple-element.28), channel_id=1, source_target_pairs={{30,0},{31,1},{0,2},{1,3},{2,4},{3,5},{4,6},{5,7},{6,8},{7,9},{8,1... | collective-permute-start | bytes 49160 | tf_op jit(solution)/shard_map/ppermute | solution.py:44
  19.5 6.8 %collective-permute-start.6 = (f32[4,8,128]{2,1,0:T(8,128)S(1)}, f32[4,8,128]{2,1,0:T(8,128)S(1)}, u32[]{:S(2)}, u32[]{:S(2)}) collective-permute-start(f32[4,8,128]{2,1,0:T(8,128)S(1)} %get-tuple-element.28), channel_id=1, source_target_pairs={{31,0},{30,1},{1,2},{0,3},{3,4},{2,5},{5,6},{4,7},{7,8},{6,9},{9,1... | collective-permute-start | bytes 49160 | tf_op jit(solution)/shard_map/ppermute | solution.py:44
  26.2 3.1 %collective-permute-start.7 = (f32[7,8,128]{2,1,0:T(8,128)S(1)}, f32[7,8,128]{2,1,0:T(8,128)S(1)}, u32[]{:S(2)}, u32[]{:S(2)}) collective-permute-start(f32[7,8,128]{2,1,0:T(8,128)S(1)} %velocity.1.refs_3_.refs_4_), channel_id=1, source_target_pairs={{2,0},{3,1},{4,2},{5,3},{6,4},{7,5},{8,6},{9,7},{10,8},{11,9},{12,... | collective-permute-start | bytes 86024 | tf_op jit(solution)/shard_map/ppermute | solution.py:44
  27.1 3.9 %collective-permute-start.8 = (f32[7,8,128]{2,1,0:T(8,128)S(1)}, f32[7,8,128]{2,1,0:T(8,128)S(1)}, u32[]{:S(2)}, u32[]{:S(2)}) collective-permute-start(f32[7,8,128]{2,1,0:T(8,128)S(1)} %velocity.1.refs_3_.refs_4_), channel_id=1, source_target_pairs={{4,0},{5,1},{6,2},{7,3},{8,4},{9,5},{10,6},{11,7},{12,8},{13,9},{1... | collective-permute-start | bytes 86024 | tf_op jit(solution)/shard_map/ppermute | solution.py:44
  27.3 3.7 %collective-permute-start.9 = (f32[7,8,128]{2,1,0:T(8,128)S(1)}, f32[7,8,128]{2,1,0:T(8,128)S(1)}, u32[]{:S(2)}, u32[]{:S(2)}) collective-permute-start(f32[7,8,128]{2,1,0:T(8,128)S(1)} %velocity.1.refs_3_.refs_4_), channel_id=1, source_target_pairs={{6,0},{7,1},{8,2},{9,3},{10,4},{11,5},{12,6},{13,7},{14,8},{15,9},... | collective-permute-start | bytes 86024 | tf_op jit(solution)/shard_map/ppermute | solution.py:44
  27.3 7.0 %collective-permute-start.10 = (f32[7,8,128]{2,1,0:T(8,128)S(1)}, f32[7,8,128]{2,1,0:T(8,128)S(1)}, u32[]{:S(2)}, u32[]{:S(2)}) collective-permute-start(f32[7,8,128]{2,1,0:T(8,128)S(1)} %velocity.1.refs_3_.refs_4_), channel_id=1, source_target_pairs={{28,0},{29,1},{30,2},{31,3},{0,4},{1,5},{2,6},{3,7},{4,8},{5,9},{6... | collective-permute-start | bytes 86024 | tf_op jit(solution)/shard_map/ppermute | solution.py:44
  29.2 6.0 %collective-permute-start.11 = (f32[7,8,128]{2,1,0:T(8,128)S(1)}, f32[7,8,128]{2,1,0:T(8,128)S(1)}, u32[]{:S(2)}, u32[]{:S(2)}) collective-permute-start(f32[7,8,128]{2,1,0:T(8,128)S(1)} %velocity.1.refs_3_.refs_4_), channel_id=1, source_target_pairs={{30,0},{31,1},{0,2},{1,3},{2,4},{3,5},{4,6},{5,7},{6,8},{7,9},{8,1... | collective-permute-start | bytes 86024 | tf_op jit(solution)/shard_map/ppermute | solution.py:44

commit v7 on v6

--- a/solution.py
+++ b/solution.py
@@ -11,7 +11,8 @@
 
 BLK = 128
 FIELDS = 9
-GROUP = 16
+FORCE_GROUP = 16
+NEAR_GROUP = 8
 REACH = 2
 FORCE_SCALE = 0.02
 CORE_SQUARE = 0.25
@@ -89,16 +90,16 @@
     return owner * high_count + lax.shift_right_logical(node, BLK.bit_length() - 1), node & (BLK - 1)
 
 
-def compact(entries, keep, base, discard, t_list, w_list):
+def compact(entries, keep, base, discard, group, t_list, w_list):
     place = jnp.int32(0)
     for t, w in entries:
         t_list[place] = t
         w_list[place] = w - base
         place = place + keep(w).astype(jnp.int32)
-    for u in range(GROUP):
+    for u in range(group):
         t_list[place + u] = jnp.int32(discard)
         w_list[place + u] = jnp.int32(0)
-    return lax.div(place + (GROUP - 1), jnp.int32(GROUP))
+    return lax.div(place + (group - 1), jnp.int32(group))
 
 
 def six_left(x):
@@ -144,7 +145,7 @@
     rows = lax.broadcasted_iota(jnp.int32, (8, BLK), 0)
     acc_s[...] = jnp.zeros_like(acc_s)
     entries = ((jnp.int32(t), lists[t, e]) for t in range(blocks) for e in range(lists.shape[1]))
-    groups = compact(entries, keep, base, blocks, t_list, w_list)
+    groups = compact(entries, keep, base, blocks, FORCE_GROUP, t_list, w_list)
     for t in range(blocks):
         lhs_s[t] = lhs[t].astype(BF16)
     for d, ref in enumerate(packs):
@@ -162,9 +163,9 @@
             src_s[w] = jnp.concatenate([*split3(sums), jnp.zeros((8, BLK), F32)], 0).astype(BF16)
 
     def some_tiles(step, carry):
-        for u in range(GROUP):
-            t = t_list[step * GROUP + u]
-            w = w_list[step * GROUP + u]
+        for u in range(FORCE_GROUP):
+            t = t_list[step * FORCE_GROUP + u]
+            w = w_list[step * FORCE_GROUP + u]
             both = jnp.dot(
                 lhs_s[jnp.minimum(t, blocks - 1)], rhs_s[w], preferred_element_type=F32
             )
@@ -256,7 +257,7 @@
     rows = lax.broadcasted_iota(jnp.int32, (8, BLK), 0)
     acc_s[...] = jnp.zeros_like(acc_s)
     entries = ((targets[0, k], sources[0, k]) for k in range(targets.shape[1]))
-    groups = compact(entries, keep, base, blocks, t_list, w_list)
+    groups = compact(entries, keep, base, blocks, NEAR_GROUP, t_list, w_list)
     zero = jnp.zeros((8, BLK), F32)
     nothing = jnp.zeros((48, BLK), BF16)
     signs = choose(rows, {4: -LOG2E}, zero + LOG2E)
@@ -299,9 +300,9 @@
                 make_target(k, jnp.concatenate([six_left(first), six_left(second)], 0).T)
 
     def some_pairs(step, carry):
-        for u in range(GROUP):
-            t = t_list[step * GROUP + u]
-            w = w_list[step * GROUP + u]
+        for u in range(NEAR_GROUP):
+            t = t_list[step * NEAR_GROUP + u]
+            w = w_list[step * NEAR_GROUP + u]
             target = tgt_s[jnp.minimum(t, blocks - 1)]
             rr = jnp.dot(target[:, 0:48], near_s[base + w], preferred_element_type=F32)
             both = jnp.dot(target, src_s[w], preferred_element_type=F32)
@@ -409,7 +410,7 @@
         name="early",
     )(own, numbers, *small)
 
-    entry_room = pltpu.SMEM((lists.shape[0] * lists.shape[1] + GROUP,), jnp.int32)
+    entry_room = pltpu.SMEM((lists.shape[0] * lists.shape[1] + FORCE_GROUP,), jnp.int32)
     accumulator = (blocks + 1, BLK, 32)
 
     def force_scratch(domains):
@@ -466,7 +467,7 @@
         name="select",
     )(*packs)
 
-    pair_room = pltpu.SMEM((targets.shape[1] + GROUP,), jnp.int32)
+    pair_room = pltpu.SMEM((targets.shape[1] + NEAR_GROUP,), jnp.int32)
     accumulator = (blocks + 1, BLK, BLK)
 
     def near_scratch(domains):

time: 37.9 us -> 38 us (level)
  transfers between devices with their start and end apart: 12 -> 12, of which waited for: 8 -> 8; matrix products, arithmetic and copies ran while one was open for 0% -> 0% of each run, Pallas kernels for 19% -> 18%
where the time goes in v7:
time: 38 us; the launch traced here: 37.8 us
  Pallas kernels  12.3 us (32%)
  starting transfers between devices  12.1 us (32%)
  waiting for transfers between devices  11.2 us (29%)
  other arithmetic  0.82 us (2%)
  between operations  0.72 us (2%)
  local copies, waits for them, and re-layouts  0.67 us (2%)
    ppermute x12, starting transfers between devices, shifted(): return lax.ppermute(block, ('cells', 'lanes'), route)  12.1 us
    ppermute x12, waiting for transfers between devices, shifted(): return lax.ppermute(block, ('cells', 'lanes'), route)  11.2 us
    pallas_call x1, Pallas kernels, local(): pl.pallas_call(first_forces, out_shape=jax.ShapeDtypeStruct(accumulator,...  3.23 us
    pallas_call x1, Pallas kernels, local(): pl.pallas_call(functools.partial(first_near, high_count), out_shape=(jax....  3.16 us
    pallas_call x1, Pallas kernels, local(): pl.pallas_call(functools.partial(last_forces, lanes, high_count), out_sha...  2.77 us
    pallas_call x1, Pallas kernels, local(): pl.pallas_call(functools.partial(last_near, high_count), out_shape=jax.Sh...  2.62 us
    add x1, other arithmetic, local(): fields + rows_of([seg_nodes, node_owner], FIELDS, FIELDS + 4).astype(F32)  0.82 us
  transfers between devices with their start and end apart: 12, of which 8 were waited for; matrix products, arithmetic and copies ran while one was open for 0% of the time, Pallas kernels for 18%

profile of v7, /device:TPU:0, one launch (start us, length us, event | category | flops | bytes accessed | tf_op | source)
XLA Modules:
  0.0 37.8 jit_solution(5167996333770644598)
XLA Ops:
  0.6 0.8 %convert_add_fusion.fields = f32[13,1024]{1,0:T(8,128)S(1)} fusion(s32[2,1024]{1,0:T(2,128)} %param.14, s32[2,1024]{1,0:T(2,128)} %param.13, f32[3,1024]{1,0:T(4,128)} %param.10, f32[3,1024]{1,0:T(4,128)} %param.11, f32[3,1024]{1,0:T(4,128)} %param.9), kind=kLoop, calls=%fused_computation | loop fusion | flops 66560 | bytes 106496 | tf_op jit(solution)/shard_map/add | solution.py:380
  1.5 0.0 copy-start.1
  1.5 0.0 copy-start
  1.5 5.5 %collective-permute-start.2 = (f32[72,128]{1,0:T(8,128)S(1)}, f32[72,128]{1,0:T(8,128)S(1)}, u32[]{:S(2)}, u32[]{:S(2)}) collective-permute-start(f32[72,128]{1,0:T(8,128)S(1)} %get-tuple-element.17.own.refs_2_.refs_0_), channel_id=1, source_target_pairs={{2,0},{3,1},{4,2},{5,3},{6,4},{7,5},{8,6},{9,7},{10,8},{11,9},{12,... | collective-permute-start | bytes 110600 | tf_op jit(solution)/shard_map/ppermute | solution.py:45
  7.0 0.6 %collective-permute-start.3 = (f32[72,128]{1,0:T(8,128)S(1)}, f32[72,128]{1,0:T(8,128)S(1)}, u32[]{:S(2)}, u32[]{:S(2)}) collective-permute-start(f32[72,128]{1,0:T(8,128)S(1)} %get-tuple-element.17.own.refs_2_.refs_0_), channel_id=1, source_target_pairs={{4,0},{5,1},{6,2},{7,3},{8,4},{9,5},{10,6},{11,7},{12,8},{13,9},{1... | collective-permute-start | bytes 110600 | tf_op jit(solution)/shard_map/ppermute | solution.py:45
  7.7 1.4 %collective-permute-start = (f32[72,128]{1,0:T(8,128)S(1)}, f32[72,128]{1,0:T(8,128)S(1)}, u32[]{:S(2)}, u32[]{:S(2)}) collective-permute-start(f32[72,128]{1,0:T(8,128)S(1)} %get-tuple-element.17.own.refs_2_.refs_0_), channel_id=1, source_target_pairs={{28,0},{29,1},{30,2},{31,3},{0,4},{1,5},{2,6},{3,7},{4,8},{5,9},{6... | collective-permute-start | bytes 110600 | tf_op jit(solution)/shard_map/ppermute | solution.py:45
  9.1 0.0 collective-permute-start.1
  9.1 0.0 copy-start.2
  9.1 0.0 copy-start.3
  9.1 0.0 copy-done.1
  9.1 0.0 copy-done
  9.1 0.6 %copy-done.2 = s32[32]{0:T(128)S(1)} copy-done((s32[32]{0:T(128)S(1)}, s32[32]{0:T(128)}, u32[]{:S(2)}) %copy-start.2) | copy-done | bytes 152
  9.7 0.0 copy-done.3
  9.7 0.4 early.1
  10.1 0.0 collective-permute-done.2.refs_3_.refs_1_
  10.1 0.9 %collective-permute-done.3.refs_4_.refs_2_ = f32[72,128]{1,0:T(8,128)S(1)} collective-permute-done((f32[72,128]{1,0:T(8,128)S(1)}, f32[72,128]{1,0:T(8,128)S(1)}, u32[]{:S(2)}, u32[]{:S(2)}) %collective-permute-start.3) | collective-permute-done | bytes 36896 | tf_op jit(solution)/shard_map/ppermute | solution.py:45
  11.0 3.2 %first_forces.1.first_acc = f32[9,128,32]{2,1,0:T(8,128)S(1)} custom-call(s32[8,8]{1,0:T(8,128)S(1)} %get-tuple-element.24.lists, f32[8,128,48]{2,1,0:T(8,128)S(1)} %get-tuple-element.25.lhs, f32[72,128]{1,0:T(8,128)S(1)} %get-tuple-element.17.own.refs_2_.refs_0_, f32[72,128]{1,0:T(8,128)S(1)} %collective-permute-done.2.refs_3_.refs_1_, ...), custom_call_target="tpu_custom_call" | custom-call | flops 268435456 | bytes 8388608 | tf_op jit(solution)/shard_map/first_forces/pallas_call | solution.py:423
  14.2 0.1 collective-permute-done.refs_0_
  14.3 0.8 %collective-permute-done.1.refs_1_ = f32[72,128]{1,0:T(8,128)S(1)} collective-permute-done((f32[72,128]{1,0:T(8,128)S(1)}, f32[72,128]{1,0:T(8,128)S(1)}, u32[]{:S(2)}, u32[]{:S(2)}) %collective-permute-start.1) | collective-permute-done | bytes 36896 | tf_op jit(solution)/shard_map/ppermute | solution.py:45
  15.1 2.8 %last_forces.1 = (f32[4,8,128]{2,1,0:T(8,128)S(1)}, f32[4,8,128]{2,1,0:T(8,128)S(1)}) custom-call(s32[8,8]{1,0:T(8,128)S(1)} %get-tuple-element.24.lists, f32[8,128,48]{2,1,0:T(8,128)S(1)} %get-tuple-element.25.lhs, bf16[2,128,1024]{2,1,0:T(8,128)(2,1)S(1)} %get-tuple-element.26.onehots, f32[4,8,128]{2,1,0:T(8,128)S(1)} %get-tuple-element.18.numbers, ...), custom_call_target="tpu_custom_call" | custom-call | tf_op jit(solution)/shard_map/last_forces/pallas_call | solution.py:434
  17.9 1.6 %collective-permute-start.4 = (f32[4,8,128]{2,1,0:T(8,128)S(1)}, f32[4,8,128]{2,1,0:T(8,128)S(1)}, u32[]{:S(2)}, u32[]{:S(2)}) collective-permute-start(f32[4,8,128]{2,1,0:T(8,128)S(1)} %get-tuple-element.27.refs_0_), channel_id=1, source_target_pairs={{1,0},{0,1},{3,2},{2,3},{5,4},{4,5},{7,6},{6,7},{9,8},{8,9},{11,10... | collective-permute-start | bytes 49160 | tf_op jit(solution)/shard_map/ppermute | solution.py:45
  19.5 0.0 collective-permute-start.5
  19.5 0.0 collective-permute-start.6
  19.5 2.2 %collective-permute-done.4.refs_1_ = f32[4,8,128]{2,1,0:T(8,128)S(1)} collective-permute-done((f32[4,8,128]{2,1,0:T(8,128)S(1)}, f32[4,8,128]{2,1,0:T(8,128)S(1)}, u32[]{:S(2)}, u32[]{:S(2)}) %collective-permute-start.4) | collective-permute-done | bytes 16416 | tf_op jit(solution)/shard_map/ppermute | solution.py:45
  21.7 3.7 %collective-permute-done.5.refs_2_ = f32[4,8,128]{2,1,0:T(8,128)S(1)} collective-permute-done((f32[4,8,128]{2,1,0:T(8,128)S(1)}, f32[4,8,128]{2,1,0:T(8,128)S(1)}, u32[]{:S(2)}, u32[]{:S(2)}) %collective-permute-start.5) | collective-permute-done | bytes 16416 | tf_op jit(solution)/shard_map/ppermute | solution.py:45
  25.4 0.8 %collective-permute-done.6.refs_3_ = f32[4,8,128]{2,1,0:T(8,128)S(1)} collective-permute-done((f32[4,8,128]{2,1,0:T(8,128)S(1)}, f32[4,8,128]{2,1,0:T(8,128)S(1)}, u32[]{:S(2)}, u32[]{:S(2)}) %collective-permute-start.6) | collective-permute-done | bytes 16416 | tf_op jit(solution)/shard_map/ppermute | solution.py:45
  26.2 0.9 %collective-permute-start.7 = (f32[7,8,128]{2,1,0:T(8,128)S(1)}, f32[7,8,128]{2,1,0:T(8,128)S(1)}, u32[]{:S(2)}, u32[]{:S(2)}) collective-permute-start(f32[7,8,128]{2,1,0:T(8,128)S(1)} %velocity.1.refs_3_.refs_4_), channel_id=1, source_target_pairs={{2,0},{3,1},{4,2},{5,3},{6,4},{7,5},{8,6},{9,7},{10,8},{11,9},{12,... | collective-permute-start | bytes 86024 | tf_op jit(solution)/shard_map/ppermute | solution.py:45
  27.1 0.2 collective-permute-start.8
  27.3 0.0 collective-permute-start.9
  27.3 1.8 %collective-permute-start.10 = (f32[7,8,128]{2,1,0:T(8,128)S(1)}, f32[7,8,128]{2,1,0:T(8,128)S(1)}, u32[]{:S(2)}, u32[]{:S(2)}) collective-permute-start(f32[7,8,128]{2,1,0:T(8,128)S(1)} %velocity.1.refs_3_.refs_4_), channel_id=1, source_target_pairs={{28,0},{29,1},{30,2},{31,3},{0,4},{1,5},{2,6},{3,7},{4,8},{5,9},{6... | collective-permute-start | bytes 86024 | tf_op jit(solution)/shard_map/ppermute | solution.py:45
  29.2 0.0 collective-permute-start.11
  29.2 0.2 select.6
  29.4 0.0 collective-permute-done.7.refs_4_
  29.4 1.6 %collective-permute-done.8.refs_5_ = f32[7,8,128]{2,1,0:T(8,128)S(1)} collective-permute-done((f32[7,8,128]{2,1,0:T(8,128)S(1)}, f32[7,8,128]{2,1,0:T(8,128)S(1)}, u32[]{:S(2)}, u32[]{:S(2)}) %collective-permute-start.8) | collective-permute-done | bytes 28704 | tf_op jit(solution)/shard_map/ppermute | solution.py:45
  31.0 0.0 collective-permute-done.9.refs_6_
  31.0 3.2 %first_near.1 = (f32[9,128,128]{2,1,0:T(8,128)S(1)}, f32[8,128,96]{2,1,0:T(8,128)S(1)}, f32[3,1024]{1,0:T(4,128)}) custom-call(s32[1,32]{1,0:T(1,128)S(1)} %get-tuple-element.19.targets, s32[1,32]{1,0:T(1,128)S(1)} %get-tuple-element.20.sources, bf16[40,48,128]{2,1,0:T(8,128)(2,1)S(1)} %get-tuple-element.21.near_s, ...), custom_call_target="tpu_custom_call" | custom-call | flops 268435456 | bytes 8388608 | tf_op jit(solution)/shard_map/first_near/pallas_call | solution.py:479
  34.2 0.0 collective-permute-done.10.refs_2_
  34.2 1.0 %collective-permute-done.11.refs_3_ = f32[7,8,128]{2,1,0:T(8,128)S(1)} collective-permute-done((f32[7,8,128]{2,1,0:T(8,128)S(1)}, f32[7,8,128]{2,1,0:T(8,128)S(1)}, u32[]{:S(2)}, u32[]{:S(2)}) %collective-permute-start.11) | collective-permute-done | bytes 28704 | tf_op jit(solution)/shard_map/ppermute | solution.py:45
  35.2 2.6 %last_near.1 = f32[8,128]{1,0:T(8,128)} custom-call(s32[1,32]{1,0:T(1,128)S(1)} %get-tuple-element.19.targets, s32[1,32]{1,0:T(1,128)S(1)} %get-tuple-element.20.sources, bf16[40,48,128]{2,1,0:T(8,128)(2,1)S(1)} %get-tuple-element.21.near_s, f32[40,24,128]{2,1,0:T(8,128)S(1)} %get-tuple-element.22.centre_s, f32[9,128,128]{2,1,0:T(8,128)S(1)} %get-tuple-element.30.first_acc, ...), custom_call_target="tpu_custom_call" | custom-call | tf_op jit(solution)/shard_map/last_near/pallas_call | solution.py:493
  (2 shorter events, 0.0 us)
Async XLA Ops:
  1.5 7.6 %copy-start.1 = (f32[1024]{0:T(1024)S(1)}, f32[1024]{0:T(1024)}, u32[]{:S(2)}) copy-start(f32[1024]{0:T(1024)} %param.15) | copy-start | bytes 12292
  1.5 7.6 %copy-start = (s32[8,8]{1,0:T(8,128)S(1)}, s32[8,8]{1,0:T(8,128)}, u32[]{:S(2)}) copy-start(s32[8,8]{1,0:T(8,128)} %refs_0_.1) | copy-start | bytes 772
  1.5 8.6 %collective-permute-start.2 = (f32[72,128]{1,0:T(8,128)S(1)}, f32[72,128]{1,0:T(8,128)S(1)}, u32[]{:S(2)}, u32[]{:S(2)}) collective-permute-start(f32[72,128]{1,0:T(8,128)S(1)} %get-tuple-element.17.own.refs_2_.refs_0_), channel_id=1, source_target_pairs={{2,0},{3,1},{4,2},{5,3},{6,4},{7,5},{8,6},{9,7},{10,8},{11,9},{12,... | collective-permute-start | bytes 110600 | tf_op jit(solution)/shard_map/ppermute | solution.py:45
  7.0 4.0 %collective-permute-start.3 = (f32[72,128]{1,0:T(8,128)S(1)}, f32[72,128]{1,0:T(8,128)S(1)}, u32[]{:S(2)}, u32[]{:S(2)}) collective-permute-start(f32[72,128]{1,0:T(8,128)S(1)} %get-tuple-element.17.own.refs_2_.refs_0_), channel_id=1, source_target_pairs={{4,0},{5,1},{6,2},{7,3},{8,4},{9,5},{10,6},{11,7},{12,8},{13,9},{1... | collective-permute-start | bytes 110600 | tf_op jit(solution)/shard_map/ppermute | solution.py:45
  7.7 6.7 %collective-permute-start = (f32[72,128]{1,0:T(8,128)S(1)}, f32[72,128]{1,0:T(8,128)S(1)}, u32[]{:S(2)}, u32[]{:S(2)}) collective-permute-start(f32[72,128]{1,0:T(8,128)S(1)} %get-tuple-element.17.own.refs_2_.refs_0_), channel_id=1, source_target_pairs={{28,0},{29,1},{30,2},{31,3},{0,4},{1,5},{2,6},{3,7},{4,8},{5,9},{6... | collective-permute-start | bytes 110600 | tf_op jit(solution)/shard_map/ppermute | solution.py:45
  9.1 6.1 %collective-permute-start.1 = (f32[72,128]{1,0:T(8,128)S(1)}, f32[72,128]{1,0:T(8,128)S(1)}, u32[]{:S(2)}, u32[]{:S(2)}) collective-permute-start(f32[72,128]{1,0:T(8,128)S(1)} %get-tuple-element.17.own.refs_2_.refs_0_), channel_id=1, source_target_pairs={{30,0},{31,1},{0,2},{1,3},{2,4},{3,5},{4,6},{5,7},{6,8},{7,9},{8,1... | collective-permute-start | bytes 110600 | tf_op jit(solution)/shard_map/ppermute | solution.py:45
  9.1 0.7 %copy-start.2 = (s32[32]{0:T(128)S(1)}, s32[32]{0:T(128)}, u32[]{:S(2)}) copy-start(s32[32]{0:T(128)} %param.16) | copy-start | bytes 388
  9.1 0.7 %copy-start.3 = (s32[32]{0:T(128)S(1)}, s32[32]{0:T(128)}, u32[]{:S(2)}) copy-start(s32[32]{0:T(128)} %param.17) | copy-start | bytes 388
  17.9 3.8 %collective-permute-start.4 = (f32[4,8,128]{2,1,0:T(8,128)S(1)}, f32[4,8,128]{2,1,0:T(8,128)S(1)}, u32[]{:S(2)}, u32[]{:S(2)}) collective-permute-start(f32[4,8,128]{2,1,0:T(8,128)S(1)} %get-tuple-element.27.refs_0_), channel_id=1, source_target_pairs={{1,0},{0,1},{3,2},{2,3},{5,4},{4,5},{7,6},{6,7},{9,8},{8,9},{11,10... | collective-permute-start | bytes 49160 | tf_op jit(solution)/shard_map/ppermute | solution.py:45
  19.5 6.0 %collective-permute-start.5 = (f32[4,8,128]{2,1,0:T(8,128)S(1)}, f32[4,8,128]{2,1,0:T(8,128)S(1)}, u32[]{:S(2)}, u32[]{:S(2)}) collective-permute-start(f32[4,8,128]{2,1,0:T(8,128)S(1)} %get-tuple-element.28), channel_id=1, source_target_pairs={{30,0},{31,1},{0,2},{1,3},{2,4},{3,5},{4,6},{5,7},{6,8},{7,9},{8,1... | collective-permute-start | bytes 49160 | tf_op jit(solution)/shard_map/ppermute | solution.py:45
  19.5 6.8 %collective-permute-start.6 = (f32[4,8,128]{2,1,0:T(8,128)S(1)}, f32[4,8,128]{2,1,0:T(8,128)S(1)}, u32[]{:S(2)}, u32[]{:S(2)}) collective-permute-start(f32[4,8,128]{2,1,0:T(8,128)S(1)} %get-tuple-element.28), channel_id=1, source_target_pairs={{31,0},{30,1},{1,2},{0,3},{3,4},{2,5},{5,6},{4,7},{7,8},{6,9},{9,1... | collective-permute-start | bytes 49160 | tf_op jit(solution)/shard_map/ppermute | solution.py:45
  26.2 3.1 %collective-permute-start.7 = (f32[7,8,128]{2,1,0:T(8,128)S(1)}, f32[7,8,128]{2,1,0:T(8,128)S(1)}, u32[]{:S(2)}, u32[]{:S(2)}) collective-permute-start(f32[7,8,128]{2,1,0:T(8,128)S(1)} %velocity.1.refs_3_.refs_4_), channel_id=1, source_target_pairs={{2,0},{3,1},{4,2},{5,3},{6,4},{7,5},{8,6},{9,7},{10,8},{11,9},{12,... | collective-permute-start | bytes 86024 | tf_op jit(solution)/shard_map/ppermute | solution.py:45
  27.1 3.9 %collective-permute-start.8 = (f32[7,8,128]{2,1,0:T(8,128)S(1)}, f32[7,8,128]{2,1,0:T(8,128)S(1)}, u32[]{:S(2)}, u32[]{:S(2)}) collective-permute-start(f32[7,8,128]{2,1,0:T(8,128)S(1)} %velocity.1.refs_3_.refs_4_), channel_id=1, source_target_pairs={{4,0},{5,1},{6,2},{7,3},{8,4},{9,5},{10,6},{11,7},{12,8},{13,9},{1... | collective-permute-start | bytes 86024 | tf_op jit(solution)/shard_map/ppermute | solution.py:45
  27.3 3.7 %collective-permute-start.9 = (f32[7,8,128]{2,1,0:T(8,128)S(1)}, f32[7,8,128]{2,1,0:T(8,128)S(1)}, u32[]{:S(2)}, u32[]{:S(2)}) collective-permute-start(f32[7,8,128]{2,1,0:T(8,128)S(1)} %velocity.1.refs_3_.refs_4_), channel_id=1, source_target_pairs={{6,0},{7,1},{8,2},{9,3},{10,4},{11,5},{12,6},{13,7},{14,8},{15,9},... | collective-permute-start | bytes 86024 | tf_op jit(solution)/shard_map/ppermute | solution.py:45
  27.3 6.8 %collective-permute-start.10 = (f32[7,8,128]{2,1,0:T(8,128)S(1)}, f32[7,8,128]{2,1,0:T(8,128)S(1)}, u32[]{:S(2)}, u32[]{:S(2)}) collective-permute-start(f32[7,8,128]{2,1,0:T(8,128)S(1)} %velocity.1.refs_3_.refs_4_), channel_id=1, source_target_pairs={{28,0},{29,1},{30,2},{31,3},{0,4},{1,5},{2,6},{3,7},{4,8},{5,9},{6... | collective-permute-start | bytes 86024 | tf_op jit(solution)/shard_map/ppermute | solution.py:45
  29.2 6.0 %collective-permute-start.11 = (f32[7,8,128]{2,1,0:T(8,128)S(1)}, f32[7,8,128]{2,1,0:T(8,128)S(1)}, u32[]{:S(2)}, u32[]{:S(2)}) collective-permute-start(f32[7,8,128]{2,1,0:T(8,128)S(1)} %velocity.1.refs_3_.refs_4_), channel_id=1, source_target_pairs={{30,0},{31,1},{0,2},{1,3},{2,4},{3,5},{4,6},{5,7},{6,8},{7,9},{8,1... | collective-permute-start | bytes 86024 | tf_op jit(solution)/shard_map/ppermute | solution.py:45
